TPU v7x, 128 devices: a whole 4x4x4 slice. The times are simulated.
128 devices in a mesh: row: 16 (over x, z_hi, core), col: 8 (over z_lo, y).
Axes of the slice: x: 4, y: 4, z: 4 (z_hi: 2, z_lo: 2; z = z_hi * 2 + z_lo), core: 2. Of those that a mesh axis runs over, the one named last changes fastest.
Arguments:
- vectors: bfloat16 [16, 262144], P(None, ('row', 'col'))
- stiffness: bfloat16 [16, 8, 192, 128, 128], P('row', 'col'), may hold values from -0.109375 to 0.109375
- block_row: int32 [16, 8, 192], P('row', 'col'), may hold values from 0 to 127
- block_col: int32 [16, 8, 192], P('row', 'col'), may hold values from 0 to 255
- block_count: int32 [16, 8], P('row', 'col'), may hold values from 1 to 192, as said below
- diag_blocks: bfloat16 [2048, 128, 128], P(('row', 'col'))
- precond: bfloat16 [2048, 128, 128], P(('row', 'col')), may hold values from -0.5 to 0.5
Outputs:
- image: float32 [16, 262144], P(None, ('row', 'col'))
- search: bfloat16 [16, 262144], P(None, ('row', 'col'))
Inputs may be any that keep to these rules, and one draw needn't show every extreme that they name: block_count is at most 192 and equals 192 on at least one grid cell in every draw.
All inputs are finite; a program needn't handle non-finite values.
Results may differ from a plain program's by a relative error of at most 0.0051.
Values may be sent and summed in bfloat16 or wider, within the bound.
No kernel may reach another device: no remote copies, remote signals or barrier semaphores. Data moves between devices by JAX's collectives and lax.ppermute only.
A program may use at most 128 MiB of HBM per device.

v0:
```python
import jax
import jax.numpy as jnp
from jax import lax
from jax.sharding import PartitionSpec as P


def per_device(vectors, stiffness, block_row, block_col, block_count, diag_blocks, precond):
    blocks = stiffness[0, 0]
    rows_index = block_row[0, 0]
    cols_index = block_col[0, 0]
    live_count = block_count[0, 0]
    vec_count = vectors.shape[0]
    owned = diag_blocks.shape[0]
    block_len = diag_blocks.shape[1]
    slots = blocks.shape[0]
    row_devs = lax.axis_size("row")
    col_devs = lax.axis_size("col")
    vectors_f = vectors.astype(jnp.float32)
    lengths_local = jnp.sum(vectors_f * vectors_f, axis=1)
    everything = lax.all_gather(vectors, ("row", "col"), axis=1, tiled=True)
    spread = everything.reshape(vec_count, row_devs, col_devs, owned, block_len)
    row_part = lax.dynamic_index_in_dim(spread, lax.axis_index("row"), 1, False)
    col_part = lax.dynamic_index_in_dim(spread, lax.axis_index("col"), 2, False)
    row_part = row_part.reshape(vec_count, col_devs * owned, block_len)
    col_part = col_part.reshape(vec_count, row_devs * owned, block_len)
    picked_col = jnp.take(col_part, cols_index, axis=1)
    picked_row = jnp.take(row_part, rows_index, axis=1)
    toward_row = jnp.einsum("knb,nab->kna", picked_col, blocks, preferred_element_type=jnp.float32)
    toward_col = jnp.einsum("kna,nab->knb", picked_row, blocks, preferred_element_type=jnp.float32)
    live = jnp.arange(slots, dtype=jnp.int32) < live_count
    row_onehot = (
        (rows_index[None, :] == jnp.arange(col_devs * owned, dtype=jnp.int32)[:, None])
        & live[None, :]
    ).astype(jnp.float32)
    col_onehot = (
        (cols_index[None, :] == jnp.arange(row_devs * owned, dtype=jnp.int32)[:, None])
        & live[None, :]
    ).astype(jnp.float32)
    row_partial = jnp.einsum(
        "kna,gn->kga",
        toward_row,
        row_onehot,
        precision=lax.Precision.HIGHEST,
        preferred_element_type=jnp.float32,
    )
    col_partial = jnp.einsum(
        "kna,gn->kga",
        toward_col,
        col_onehot,
        precision=lax.Precision.HIGHEST,
        preferred_element_type=jnp.float32,
    )
    zero_term = jnp.zeros((vec_count, row_devs, col_devs, owned * block_len), jnp.float32)
    term = lax.dynamic_update_index_in_dim(
        zero_term,
        row_partial.reshape(vec_count, col_devs, owned * block_len),
        lax.axis_index("row"),
        1,
    )
    term = term + lax.dynamic_update_index_in_dim(
        zero_term,
        col_partial.reshape(vec_count, row_devs, owned * block_len),
        lax.axis_index("col"),
        2,
    )
    mine = lax.psum_scatter(
        term.reshape(vec_count, row_devs * col_devs * owned * block_len),
        ("row", "col"),
        scatter_dimension=1,
        tiled=True,
    )
    own_vec = vectors.reshape(vec_count, owned, block_len)
    diag_term = jnp.einsum("nab,knb->kna", diag_blocks, own_vec, preferred_element_type=jnp.float32)
    diag_term = diag_term + jnp.einsum(
        "nba,knb->kna", diag_blocks, own_vec, preferred_element_type=jnp.float32
    )
    image = mine + diag_term.reshape(vec_count, owned * block_len)
    inner_local = jnp.sum(vectors_f * image, axis=1)
    lengths, inner = lax.psum((lengths_local, inner_local), ("row", "col"))
    theta = inner / lengths
    resid = (image - theta[:, None] * vectors_f).astype(jnp.bfloat16)
    search = jnp.einsum(
        "nab,knb->kna",
        precond,
        resid.reshape(vec_count, owned, block_len),
        preferred_element_type=jnp.float32,
    )
    return (image, search.reshape(vec_count, owned * block_len).astype(jnp.bfloat16))


def solution(mesh):
    placed = (
        P(None, ("row", "col")),
        P("row", "col", None, None, None),
        P("row", "col", None),
        P("row", "col", None),
        P("row", "col"),
        P(("row", "col"), None, None),
        P(("row", "col"), None, None),
    )
    return jax.shard_map(
        per_device,
        mesh=mesh,
        in_specs=placed,
        out_specs=(P(None, ("row", "col")), P(None, ("row", "col"))),
        check_vma=False,
    )
```

profile of v0, /device:TPU:0, one launch (start us, length us, event | category | flops | bytes accessed | tf_op | source)
XLA Modules:
  0.0 1169.2 jit_solution(11257969639220290386)
XLA Ops:
  7.2 0.7 all-gather.2.cloned.1.call-update
  7.9 0.0 reduce-scatter.2.cloned.1.call-start
  8.6 0.7 compare_select_fusion
  9.4 0.7 compare_and_fusion
  10.1 312.6 %all-gather.2.cloned.1.call-done = bf16[16,262144]{1,0:T(8,128)(2,1)} async-done(((bf16[16,2048]{1,0:T(8,128)(2,1)}), bf16[16,262144]{1,0:T(8,128)(2,1)}) %all-gather.2.cloned.1.call-update) | async-done | bytes 8388624 | tf_op jit(solution)/shard_map/all_gather | solution.py:20
  322.6 8.1 copy.31
  330.7 1.1 constant_dynamic-slice_fusion
  331.8 1.5 constant_dynamic-slice_fusion.1
  333.3 1.7 copy.25
  335.0 0.3 copy.26
  335.3 0.8 gather_fusion.1
  336.1 4.1 fusion
  340.2 2.9 convolution_bitcast_fusion
  343.1 1.7 broadcast_in_dim.39
  344.9 2.0 gather_fusion
  346.9 5.5 fusion.2
  352.4 2.3 fusion.9
  354.7 2.3 broadcast_in_dim.37
  357.0 3.3 copy.15
  360.3 7.9 broadcast_in_dim.34
  368.1 20.5 %dynamic_update_slice.10 = f32[16,16,8,2048]{3,1,0,2:T(8,128)} dynamic-update-slice(f32[16,16,8,2048]{3,1,0,2:T(8,128)} %broadcast_in_dim.34, f32[16,1,8,2048]{3,1,0,2:T(1,128)} %copy.15, s32[]{:T(128)} %constant.42.clone.1, s32[]{:T(128)S(6)} %select_n.55, s32[]{:T(128)} %constant.42.clone.1, s32[]{:T(128)} %constant.42.clone.1) | dynamic-update-slice | bytes 2097156 | tf_op jit(solution)/shard_map/jit(dynamic_update_index_in_dim)/dynamic_update_slice | solution.py:54
  388.6 3.3 add_dynamic-update-slice_fusion
  391.9 15.5 %copy.17 = f32[16,16,8,2048]{3,2,1,0:T(8,128)S(1)} copy(f32[16,16,8,2048]{3,1,0,2:T(8,128)} %add_dynamic-update-slice_fusion) | data formatting | bytes 33554432 | tf_op jit(solution)/shard_map/add | solution.py:60
  407.4 20.1 %copy.32 = f32[2,8,128,2048]{3,1,2,0:T(8,128)} copy(f32[2,8,128,2048]{3,2,1,0:T(8,128)S(1)} %bitcast.82) | data formatting | bytes 33554432
  427.5 0.8 copy-done.1
  428.3 0.4 fusion.38
  428.7 0.3 fusion.12
  428.9 668.7 %reduce-scatter.2.cloned.1.call-done = f32[16,2048]{1,0:T(8,128)} async-done(((f32[16,262144]{1,0:T(8,128)}), f32[16,2048]{1,0:T(8,128)}) %reduce-scatter.2.cloned.1.call-update) | async-done | bytes 131088 | tf_op jit(solution)/shard_map/reduce_scatter | solution.py:66
  1097.7 1.0 fusion.26
  1098.7 62.5 %all-reduce = (f32[16]{0:T(128)S(1)}, f32[16]{0:T(128)S(1)}) all-reduce(f32[16]{0:T(128)S(1)} %get-tuple-element.3, f32[16]{0:T(128)S(1)} %get-tuple-element.2), channel_id=1, replica_groups=mesh['row'=16,'col'=8] {'row','col'}, use_global_device_ids=true, to_apply=%region_2.3 | all-reduce | flops 32 | bytes 256 | tf_op jit(solution)/shard_map/psum | solution.py:79
  1161.3 0.4 fusion.13
  1161.7 0.7 copy.58
  (17 shorter events, 0.1 us)
Async XLA Ops:
  7.2 420.3 %copy-start = (bf16[16,128,128]{2,1,0:T(8,128)(2,1)S(1)}, bf16[16,128,128]{2,1,0:T(8,128)(2,1)}, u32[]{:S(2)}) copy-start(bf16[16,128,128]{2,1,0:T(8,128)(2,1)} %param.12) | copy-start | bytes 1572868
  7.2 315.5 %all-gather.2.cloned.1.call-start = ((), (), s32[]{:S(2)}) async-start(), calls=%async_computation.1 | async-start | bytes 8454144 | tf_op jit(solution)/shard_map/all_gather | solution.py:20
  7.9 1089.8 %reduce-scatter.2.cloned.1.call-start = ((), (), s32[]{:S(2)}) async-start(), calls=%async_computation.2 | async-start | bytes 16908288 | tf_op jit(solution)/shard_map/reduce_scatter | solution.py:66
  333.3 6.9 copy-start.4
  343.1 9.2 copy-start.5
  427.5 0.8 copy-start.1
  427.5 733.8 %copy-start.2 = (bf16[16,128,128]{2,1,0:T(8,128)(2,1)S(1)}, bf16[16,128,128]{2,1,0:T(8,128)(2,1)}, u32[]{:S(2)}) copy-start(bf16[16,128,128]{2,1,0:T(8,128)(2,1)} %param.13) | copy-start | bytes 1572868
  1098.7 63.6 %copy-start.3 = (f32[16,2048]{1,0:T(8,128)}, f32[16,2048]{1,0:T(8,128)S(1)}, u32[]{:S(2)}) copy-start(f32[16,2048]{1,0:T(8,128)S(1)} %get-tuple-element.6) | copy-start | bytes 393220
Sparse Core Ops, SparseCore 0:
  9.7 312.8 all-gather.1
  427.6 670.0 reduce-scatter.1
where the time goes:
time: 1170 us
  waiting for transfers between devices  982 us (84%)
  local copies, waits for them, and re-layouts  88.2 us (8%)
  blocking collectives  62.5 us (5%)
  matrix products  15.8 us (1%)
  between operations  14.8 us (1%)
    reduce_scatter x1, waiting for transfers between devices, per_device(): lax.psum_scatter(term.reshape(vec_count, row_devs * col_devs * owned * bl...  669 us
    all_gather x1, waiting for transfers between devices, per_device(): everything = lax.all_gather(vectors, ('row', 'col'), axis=1, tiled=True)  313 us
    psum x1, blocking collectives, per_device(): lengths, inner = lax.psum((lengths_local, inner_local), ('row', 'col'))  62.5 us
    unnamed x16, local copies, waits for them, and re-layouts  31 us
  transfers between devices with their start and end apart: 2, of which 2 were waited for; matrix products, arithmetic and copies ran while one was open for 0% of the time, Pallas kernels for 0%

commit v1 on v0

v1 whole, which is shorter than its diff:
```python
import functools
import jax
import jax.numpy as jnp
from jax import lax
from jax.experimental import pallas as pl
from jax.experimental.pallas import tpu as pltpu
from jax.sharding import PartitionSpec as P

CHUNK = 16
GROUP = 8
LANES = 128
F32 = jnp.float32
BF16 = jnp.bfloat16


def split_tile(xy, xx, width):
    lane = lax.broadcasted_iota(jnp.int32, (width, LANES), 1)
    v = jnp.where(lane % 2 == 0, xy, xx)
    hi = v.astype(BF16).astype(F32)
    mid = (v - hi).astype(BF16).astype(F32)
    low = v - hi - mid
    tile = jnp.where(lane < 2, hi, jnp.where(lane < 4, mid, jnp.where(lane < 6, low, 0.0)))
    return tile.astype(BF16)


def join_tile(tile):
    lane = lax.broadcasted_iota(jnp.int32, tile.shape, 1)
    xy = jnp.sum(jnp.where(lane % 2 == 0, tile, 0.0), axis=1, keepdims=True)
    xx = jnp.sum(jnp.where(lane % 2 == 1, tile, 0.0), axis=1, keepdims=True)
    return xy, xx


def block_kernel(count_ref, rows_ref, cols_ref, x_ref, xrow_ref, xcol_ref, diag_ref, stiff_ref,
                 out_row, out_col, out_diag, acc_row, acc_col, buf, sems):
    slots = stiff_ref.shape[0]
    chunks = slots // CHUNK
    n_row, width, span = xrow_ref.shape
    n_col = xcol_ref.shape[0]
    owned = span // LANES
    copies = [
        pltpu.make_async_copy(stiff_ref.at[pl.ds(c * CHUNK, CHUNK)], buf.at[pl.ds(c * CHUNK, CHUNK)], sems.at[c])
        for c in range(chunks)
    ]
    for copy in copies:
        copy.start()
    acc_row[...] = jnp.zeros_like(acc_row)
    acc_col[...] = jnp.zeros_like(acc_col)
    xy = jnp.zeros((width, LANES), F32)
    xx = jnp.zeros((width, LANES), F32)
    for g in range(owned):
        here = slice(g * LANES, (g + 1) * LANES)
        xg = x_ref[:, here]
        d = diag_ref[g]
        term = lax.dot_general(xg, d, (((1,), (1,)), ((), ())), preferred_element_type=F32)
        term = term + lax.dot_general(xg, d, (((1,), (0,)), ((), ())), preferred_element_type=F32)
        out_diag[:, here] = term
        xf = xg.astype(F32)
        xy = xy + xf * term
        xx = xx + xf * xf
    count = count_ref[0]
    for c in range(chunks):
        copies[c].wait()

        @pl.when(c * CHUNK < count)
        def _():
            for h in range(CHUNK // GROUP):
                found = []
                for u in range(GROUP):
                    n = c * CHUNK + h * GROUP + u
                    i = rows_ref[n]
                    j = cols_ref[n]
                    b = buf[n]
                    xc = xcol_ref[j // owned, :, pl.ds(pl.multiple_of((j % owned) * LANES, LANES), LANES)]
                    xr = xrow_ref[i // owned, :, pl.ds(pl.multiple_of((i % owned) * LANES, LANES), LANES)]
                    to_row = lax.dot_general(xc, b, (((1,), (1,)), ((), ())), preferred_element_type=F32)
                    to_col = lax.dot_general(xr, b, (((1,), (0,)), ((), ())), preferred_element_type=F32)
                    live = n < count
                    found.append((jnp.where(live, i, n_row * owned), jnp.where(live, j, n_col * owned), to_row, to_col))
                for i, j, to_row, to_col in found:
                    acc_row[i] += to_row
                    acc_col[j] += to_col

    part = jnp.zeros((width, LANES), F32)
    for d in range(n_row):
        for t in range(owned):
            here = slice(t * LANES, (t + 1) * LANES)
            a = acc_row[d * owned + t]
            part = part + a * xrow_ref[d, :, here].astype(F32)
            out_row[d, :, here] = a.astype(BF16)
    xy = jnp.sum(xy + 2.0 * part, axis=1, keepdims=True)
    xx = jnp.sum(xx, axis=1, keepdims=True)
    tile = split_tile(xy, xx, width)
    for d in range(n_col):
        for t in range(owned):
            out_col[d, :, t * LANES:(t + 1) * LANES] = acc_col[d * owned + t].astype(BF16)
        out_col[d, :, span:] = tile
    for d in range(n_row):
        out_row[d, :, span:] = tile


def middle_kernel(col_ref, diag_ref, row_in, sum_ref, row_ref):
    n_col, width, wide = col_ref.shape
    span = wide - LANES
    for t in range(span // LANES):
        here = slice(t * LANES, (t + 1) * LANES)
        total = diag_ref[:, here]
        for d in range(n_col):
            total = total + col_ref[d, :, here].astype(F32)
        sum_ref[:, here] = total
    tile = col_ref[0, :, span:].astype(F32)
    for d in range(1, n_col):
        tile = tile + col_ref[d, :, span:].astype(F32)
    xy, xx = join_tile(tile)
    out = split_tile(xy, xx, width)
    for d in range(row_ref.shape[0]):
        row_ref[d, :, :span] = row_in[d, :, :span]
        row_ref[d, :, span:] = out


def final_kernel(row_ref, sum_ref, x_ref, pre_ref, image_ref, search_ref):
    n_row, width, wide = row_ref.shape
    span = wide - LANES
    tile = row_ref[0, :, span:].astype(F32)
    for d in range(1, n_row):
        tile = tile + row_ref[d, :, span:].astype(F32)
    xy, xx = join_tile(tile)
    theta = xy / xx
    for t in range(span // LANES):
        here = slice(t * LANES, (t + 1) * LANES)
        total = sum_ref[:, here]
        for d in range(n_row):
            total = total + row_ref[d, :, here].astype(F32)
        image_ref[:, here] = total
        resid = (total - theta * x_ref[:, here].astype(F32)).astype(BF16)
        out = lax.dot_general(resid, pre_ref[t], (((1,), (1,)), ((), ())), preferred_element_type=F32)
        search_ref[:, here] = out.astype(BF16)


VM = pl.BlockSpec(memory_space=pltpu.VMEM)
SM = pl.BlockSpec(memory_space=pltpu.SMEM)


def spread(x, axis, count):
    return lax.all_to_all(jnp.broadcast_to(x[None], (count, *x.shape)), axis, 0, 0, tiled=True)


def per_device(vectors, stiffness, block_row, block_col, block_count, diag_blocks, precond):
    width, span = vectors.shape
    owned, block_len, _ = diag_blocks.shape
    slots = stiffness.shape[2]
    row_devs = lax.axis_size("row")
    col_devs = lax.axis_size("col")
    xrow = spread(vectors, "col", col_devs)
    xcol = spread(vectors, "row", row_devs)
    wide = span + LANES
    out_row, out_col, diag_term = pl.pallas_call(
        block_kernel,
        out_shape=(
            jax.ShapeDtypeStruct((col_devs, width, wide), BF16),
            jax.ShapeDtypeStruct((row_devs, width, wide), BF16),
            jax.ShapeDtypeStruct((width, span), F32),
        ),
        in_specs=[SM, SM, SM, VM, VM, VM, VM, pl.BlockSpec(memory_space=pl.ANY)],
        out_specs=(VM, VM, VM),
        scratch_shapes=[
            pltpu.VMEM((col_devs * owned + 1, width, LANES), F32),
            pltpu.VMEM((row_devs * owned + 1, width, LANES), F32),
            pltpu.VMEM((slots, block_len, block_len), BF16),
            pltpu.SemaphoreType.DMA((slots // CHUNK,)),
        ],
        compiler_params=pltpu.CompilerParams(vmem_limit_bytes=40 << 20),
    )(block_count.reshape(1), block_row.reshape(slots), block_col.reshape(slots), vectors, xrow, xcol,
      diag_blocks, stiffness.reshape(slots, block_len, block_len))
    got_col = lax.all_to_all(out_col, "row", 0, 0, tiled=True)
    part, out_row = pl.pallas_call(
        middle_kernel,
        out_shape=(jax.ShapeDtypeStruct((width, span), F32), jax.ShapeDtypeStruct((col_devs, width, wide), BF16)),
        in_specs=[VM] * 3,
        out_specs=(VM, VM),
        compiler_params=pltpu.CompilerParams(vmem_limit_bytes=24 << 20),
    )(got_col, diag_term, out_row)
    got_row = lax.all_to_all(out_row, "col", 0, 0, tiled=True)
    return pl.pallas_call(
        final_kernel,
        out_shape=(jax.ShapeDtypeStruct((width, span), F32), jax.ShapeDtypeStruct((width, span), BF16)),
        in_specs=[VM] * 4,
        out_specs=(VM, VM),
        compiler_params=pltpu.CompilerParams(vmem_limit_bytes=24 << 20),
    )(got_row, part, vectors, precond)


def solution(mesh):
    placed = (
        P(None, ("row", "col")),
        P("row", "col", None, None, None),
        P("row", "col", None),
        P("row", "col", None),
        P("row", "col"),
        P(("row", "col"), None, None),
        P(("row", "col"), None, None),
    )
    return jax.shard_map(
        per_device,
        mesh=mesh,
        in_specs=placed,
        out_specs=(P(None, ("row", "col")), P(None, ("row", "col"))),
        check_vma=False,
    )
```

time: 1170 us -> 92.5 us (0.08)
  waiting for transfers between devices: 982 us -> 17.3 us
  local copies, waits for them, and re-layouts: 88.2 us -> 4.83 us
  matrix products: 15.8 us -> 0 us
  between operations: 14.8 us -> 1.33 us
    reduce_scatter x1 -> x0, waiting for transfers between devices: 669 us -> none  [per_device(): lax.psum_scatter(term.reshape(vec_count, row_devs * col_devs * owned * bl...]
    all_gather x1 -> x0, waiting for transfers between devices: 313 us -> none  [per_device(): everything = lax.all_gather(vectors, ('row', 'col'), axis=1, tiled=True)]
    psum x1 -> x0, blocking collectives: 62.5 us -> none  [per_device(): lengths, inner = lax.psum((lengths_local, inner_local), ('row', 'col'))]
    all_to_all x0 -> x3, blocking collectives: none -> 54.3 us  [the longest x1 25 us: per_device(): got_col = lax.all_to_all(out_col, 'row', 0, 0, tiled=True)]
    unnamed x16 -> x12, local copies, waits for them, and re-layouts: 31 us -> 2.8 us
    dynamic_update_slice x1 -> x0, local copies, waits for them, and re-layouts: 20.5 us -> none  [per_device(): lax.dynamic_update_index_in_dim(zero_term, row_partial.reshape(vec_count,...]
    all_to_all x0 -> x1, waiting for transfers between devices: none -> 17.3 us  [spread(): lax.all_to_all(jnp.broadcast_to(x[None], (count, *x.shape)), axis, 0, 0,...]
    dot_general x7 -> x0, matrix products: 15.8 us -> none  [the longest x1 5.47 us: per_device(): jnp.einsum('knb,nab->kna', picked_col, blocks, preferred_element_type=jnp...]
  transfers between devices with their start and end apart: 2 -> 1, of which waited for: 2 -> 1; matrix products, arithmetic and copies ran while one was open for 0% -> 0% of each run, Pallas kernels for 0% -> 0%
where the time goes in v1:
time: 92.5 us; the launch traced here: 92 us
  blocking collectives  54.3 us (59%)
  waiting for transfers between devices  17.3 us (19%)
  starting transfers between devices  7.55 us (8%)
  Pallas kernels  6.64 us (7%)
  local copies, waits for them, and re-layouts  4.83 us (5%)
  between operations  1.33 us (1%)
    all_to_all x1, blocking collectives, per_device(): got_col = lax.all_to_all(out_col, 'row', 0, 0, tiled=True)  25 us
    all_to_all x1, waiting for transfers between devices, spread(): lax.all_to_all(jnp.broadcast_to(x[None], (count, *x.shape)), axis, 0, 0,...  17.3 us
    all_to_all x1, blocking collectives, spread(): lax.all_to_all(jnp.broadcast_to(x[None], (count, *x.shape)), axis, 0, 0,...  15.8 us
    all_to_all x1, blocking collectives, per_device(): got_row = lax.all_to_all(out_row, 'col', 0, 0, tiled=True)  13.6 us
    all_to_all x1, starting transfers between devices, spread(): lax.all_to_all(jnp.broadcast_to(x[None], (count, *x.shape)), axis, 0, 0,...  7.55 us
    pallas_call x1, Pallas kernels, per_device(): pl.pallas_call(block_kernel, out_shape=(jax.ShapeDtypeStruct((col_devs, w...  5.37 us
    unnamed x12, local copies, waits for them, and re-layouts  2.8 us
    broadcast_in_dim x2, local copies, waits for them, and re-layouts, spread(): jnp.broadcast_to(x[None], (count, *x.shape))  2.03 us
  transfers between devices with their start and end apart: 1, of which 1 were waited for; matrix products, arithmetic and copies ran while one was open for 0% of the time, Pallas kernels for 0%

profile of v1, /device:TPU:0, one launch (start us, length us, event | category | flops | bytes accessed | tf_op | source)
XLA Modules:
  0.0 92.0 jit_solution(6804050779442145481)
XLA Ops:
  0.6 0.0 copy-start.1
  0.6 0.9 %broadcast_in_dim.4 = bf16[8,16,2048]{2,1,0:T(8,128)(2,1)S(1)} broadcast(bf16[16,2048]{1,0:T(8,128)(2,1)} %x_ref.3), dimensions={1,2} | broadcast | bytes 589824 | tf_op jit(solution)/shard_map/broadcast_in_dim | solution.py:144
  1.6 15.8 %all_to_all.20.xrow_ref = bf16[8,16,2048]{2,1,0:T(8,128)(2,1)S(1)} all-to-all(bf16[8,16,2048]{2,1,0:T(8,128)(2,1)S(1)} %broadcast_in_dim.4), channel_id=1, replica_groups=mesh['row'=16,'col'=8] {'col'}, dimensions={0} | all-to-all | bytes 1048576 | tf_op jit(solution)/shard_map/all_to_all | solution.py:144
  17.4 0.0 copy-done.1
  17.4 1.1 %broadcast_in_dim.5 = bf16[16,16,2048]{2,1,0:T(8,128)(2,1)} broadcast(bf16[16,2048]{1,0:T(8,128)(2,1)S(1)} %copy-done.1), dimensions={1,2} | broadcast | bytes 1114112 | tf_op jit(solution)/shard_map/broadcast_in_dim | solution.py:144
  18.5 0.0 copy-start.2
  18.5 0.0 copy-start.4
  18.5 0.0 copy-start.5
  18.5 7.6 %all-to-all-start.1 = ((bf16[16,16,2048]{2,1,0:T(8,128)(2,1)}), bf16[16,16,2048]{2,1,0:T(8,128)(2,1)S(1)}, u32[]{:S(2)}, u32[]{:S(2)}) async-start(bf16[16,16,2048]{2,1,0:T(8,128)(2,1)} %broadcast_in_dim.5), calls=%async_computation.1 | async-start | bytes 2097152 | tf_op jit(solution)/shard_map/all_to_all | solution.py:144
  26.7 17.3 %all-to-all-done.1.xcol_ref = bf16[16,16,2048]{2,1,0:T(8,128)(2,1)S(1)} async-done(((bf16[16,16,2048]{2,1,0:T(8,128)(2,1)}), bf16[16,16,2048]{2,1,0:T(8,128)(2,1)S(1)}, u32[]{:S(2)}, u32[]{:S(2)}) %all-to-all-start.1) | async-done | bytes 1048608 | tf_op jit(solution)/shard_map/all_to_all | solution.py:144
  44.0 0.0 copy-done.2
  44.0 0.0 copy-done.4
  44.0 0.0 copy-done.5
  44.0 0.0 copy-start
  44.0 2.8 %copy-done = bf16[1,1,192,128,128]{4,3,2,1,0:T(8,128)(2,1)S(1)} copy-done((bf16[1,1,192,128,128]{4,3,2,1,0:T(8,128)(2,1)S(1)}, bf16[1,1,192,128,128]{4,3,2,1,0:T(8,128)(2,1)}, u32[]{:S(2)}) %copy-start) | copy-done | bytes 6291480
  46.8 5.4 %shard_map.86 = (bf16[8,16,2176]{2,1,0:T(8,128)(2,1)S(1)}, bf16[16,16,2176]{2,1,0:T(8,128)(2,1)S(1)}, f32[16,2048]{1,0:T(8,128)S(1)}) custom-call(s32[1]{0:T(128)} %bitcast.4.count_ref, s32[192]{0:T(256)S(1)} %bitcast.6, s32[192]{0:T(256)S(1)} %bitcast.7, bf16[16,2048]{1,0:T(8,128)(2,1)S(1)} %copy-done.1, bf16[8,16,2048]{2,1,0:T(8,128)(2,1)S(1)} %all_to_all.20.xrow_ref, ...), custom_call_target="tpu_custom_call" | custom-call | tf_op jit(solution)/shard_map/pallas_call | solution.py:156
  52.2 25.0 %all_to_all.21.col_ref = bf16[16,16,2176]{2,1,0:T(8,128)(2,1)S(1)} all-to-all(bf16[16,16,2176]{2,1,0:T(8,128)(2,1)S(1)} %get-tuple-element.7), channel_id=1, replica_groups=mesh['row'=16,'col'=8] {'row'}, dimensions={0} | all-to-all | bytes 2228224 | tf_op jit(solution)/shard_map/all_to_all | solution.py:174
  77.2 0.0 copy-start.3
  77.2 0.2 shard_map.87
  77.3 13.6 %all_to_all.22.row_ref = bf16[8,16,2176]{2,1,0:T(8,128)(2,1)S(1)} all-to-all(bf16[8,16,2176]{2,1,0:T(8,128)(2,1)S(1)} %get-tuple-element.10), channel_id=1, replica_groups=mesh['row'=16,'col'=8] {'col'}, dimensions={0} | all-to-all | bytes 1114112 | tf_op jit(solution)/shard_map/all_to_all | solution.py:182
  90.9 0.0 copy-done.3
  90.9 1.1 %shard_map.88 = (f32[16,2048]{1,0:T(8,128)}, bf16[16,2048]{1,0:T(8,128)(2,1)}) custom-call(bf16[8,16,2176]{2,1,0:T(8,128)(2,1)S(1)} %all_to_all.22.row_ref, f32[16,2048]{1,0:T(8,128)S(1)} %get-tuple-element.11.sum_ref, bf16[16,2048]{1,0:T(8,128)(2,1)S(1)} %copy-done.1, bf16[16,128,128]{2,1,0:T(8,128)(2,1)S(1)} %copy-done.3), custom_call_target="tpu_custom_call" | custom-call | tf_op jit(solution)/shard_map/pallas_call | solution.py:183
Async XLA Ops:
  0.6 16.8 %copy-start.1 = (bf16[16,2048]{1,0:T(8,128)(2,1)S(1)}, bf16[16,2048]{1,0:T(8,128)(2,1)}, u32[]{:S(2)}) copy-start(bf16[16,2048]{1,0:T(8,128)(2,1)} %x_ref.3) | copy-start | bytes 196612
  18.5 25.6 %copy-start.2 = (bf16[16,128,128]{2,1,0:T(8,128)(2,1)S(1)}, bf16[16,128,128]{2,1,0:T(8,128)(2,1)}, u32[]{:S(2)}) copy-start(bf16[16,128,128]{2,1,0:T(8,128)(2,1)} %diag_ref.1) | copy-start | bytes 1572868
  18.5 25.6 %copy-start.4 = (s32[1,1,192]{2,1,0:T(1,128)S(1)}, s32[1,1,192]{2,1,0:T(1,128)}, u32[]{:S(2)}) copy-start(s32[1,1,192]{2,1,0:T(1,128)} %param.9) | copy-start | bytes 2308
  18.5 25.6 %copy-start.5 = (s32[1,1,192]{2,1,0:T(1,128)S(1)}, s32[1,1,192]{2,1,0:T(1,128)}, u32[]{:S(2)}) copy-start(s32[1,1,192]{2,1,0:T(1,128)} %param.10) | copy-start | bytes 2308
  18.5 25.5 %all-to-all-start.1 = ((bf16[16,16,2048]{2,1,0:T(8,128)(2,1)}), bf16[16,16,2048]{2,1,0:T(8,128)(2,1)S(1)}, u32[]{:S(2)}, u32[]{:S(2)}) async-start(bf16[16,16,2048]{2,1,0:T(8,128)(2,1)} %broadcast_in_dim.5), calls=%async_computation.1 | async-start | bytes 2097152 | tf_op jit(solution)/shard_map/all_to_all | solution.py:144
  44.0 2.8 %copy-start = (bf16[1,1,192,128,128]{4,3,2,1,0:T(8,128)(2,1)S(1)}, bf16[1,1,192,128,128]{4,3,2,1,0:T(8,128)(2,1)}, u32[]{:S(2)}) copy-start(bf16[1,1,192,128,128]{4,3,2,1,0:T(8,128)(2,1)} %param.8) | copy-start | bytes 18874372
  77.2 13.8 %copy-start.3 = (bf16[16,128,128]{2,1,0:T(8,128)(2,1)S(1)}, bf16[16,128,128]{2,1,0:T(8,128)(2,1)}, u32[]{:S(2)}) copy-start(bf16[16,128,128]{2,1,0:T(8,128)(2,1)} %pre_ref.1) | copy-start | bytes 1572868

commit v2 on v1

v2 whole, which is shorter than its diff:
```python
import functools
import jax
import jax.numpy as jnp
from jax import lax
from jax.experimental import pallas as pl
from jax.experimental.pallas import tpu as pltpu
from jax.sharding import PartitionSpec as P

CHUNK = 16
LANES = 128
F32 = jnp.float32
BF16 = jnp.bfloat16


def split_tile(xy, xx, width):
    lane = lax.broadcasted_iota(jnp.int32, (width, LANES), 1)
    v = jnp.where(lane % 2 == 0, xy, xx)
    hi = v.astype(BF16).astype(F32)
    mid = (v - hi).astype(BF16).astype(F32)
    low = v - hi - mid
    tile = jnp.where(lane < 2, hi, jnp.where(lane < 4, mid, jnp.where(lane < 6, low, 0.0)))
    return tile.astype(BF16)


def join_tile(tile):
    lane = lax.broadcasted_iota(jnp.int32, tile.shape, 1)
    xy = jnp.sum(jnp.where(lane % 2 == 0, tile, 0.0), axis=1, keepdims=True)
    xx = jnp.sum(jnp.where(lane % 2 == 1, tile, 0.0), axis=1, keepdims=True)
    return xy, xx


def fetch(stiff_ref, buf, sems, count):
    copies = []
    for c in range(stiff_ref.shape[0] // CHUNK):
        here = pl.ds(c * CHUNK, CHUNK)
        copies.append(pltpu.make_async_copy(stiff_ref.at[here], buf.at[here], sems.at[c]))
    for c, copy in enumerate(copies):
        pl.when(c * CHUNK < count)(copy.start)
    return copies


def pair_products(xa, xb, blocks, turned):
    none = jnp.zeros_like(xa)
    x = jnp.concatenate([jnp.concatenate([xa, none], axis=1), jnp.concatenate([none, xb], axis=1)], axis=0)
    if turned:
        b = jnp.concatenate([blocks[0], blocks[1]], axis=1)
        dims = ((1,), (1,))
    else:
        b = blocks.reshape(2 * blocks.shape[1], blocks.shape[2])
        dims = ((1,), (0,))
    out = lax.dot_general(x, b, (dims, ((), ())), preferred_element_type=F32)
    return out[:xa.shape[0]], out[xa.shape[0]:]


def add_blocks(copies, count, take_ref, give_ref, x_blocks, turned, buf, acc):
    spare = acc.shape[0] - 1
    for c, copy in enumerate(copies):

        @pl.when(c * CHUNK < count)
        def _():
            copy.wait()
            found = []
            for n in range(c * CHUNK, (c + 1) * CHUNK, 2):
                terms = pair_products(x_blocks[take_ref[n]], x_blocks[take_ref[n + 1]], buf[n:n + 2], turned)
                for k in range(2):
                    found.append((jnp.where(n + k < count, give_ref[n + k], spare), terms[k]))
            for g, term in found:
                acc[g] += term


def first_kernel(count_ref, rows_ref, cols_ref, x_ref, z_ref, *refs):
    (*pair_refs, diag_ref, stiff_ref, out_col, out_diag, x_row, acc, buf, sems) = refs
    copies = fetch(stiff_ref, buf, sems, count_ref[0, 0])
    width, span = x_ref.shape
    owned = span // LANES
    runs = len(pair_refs) + 1
    place = lax.axis_index("col")
    zl = place // runs
    y = place % runs
    for s in range(runs):
        for k in range(2):
            dev = ((zl + k) % 2) * runs + (y + runs - s) % runs
            for t in range(owned):
                here = slice(t * LANES, (t + 1) * LANES)
                piece = (x_ref if k == 0 else z_ref)[:, here] if s == 0 else pair_refs[s - 1][k, :, here]
                x_row[dev * owned + t] = piece
    acc[...] = jnp.zeros_like(acc)
    for g in range(owned):
        here = slice(g * LANES, (g + 1) * LANES)
        xg = x_ref[:, here]
        d = diag_ref[g]
        term = lax.dot_general(xg, d, (((1,), (1,)), ((), ())), preferred_element_type=F32)
        out_diag[:, here] = term + lax.dot_general(xg, d, (((1,), (0,)), ((), ())), preferred_element_type=F32)
    add_blocks(copies, count_ref[0, 0], rows_ref, cols_ref, x_row, False, buf, acc)
    for d in range(out_col.shape[0]):
        for t in range(owned):
            out_col[d, :, t * LANES:(t + 1) * LANES] = acc[d * owned + t].astype(BF16)


def second_kernel(count_ref, rows_ref, cols_ref, x_ref, diag_ref, x_row, xcol_ref, stiff_ref, col_in,
                  out_row, out_col, x_col, acc, buf, sems):
    copies = fetch(stiff_ref, buf, sems, count_ref[0, 0])
    width, span = x_ref.shape
    owned = span // LANES
    for d in range(xcol_ref.shape[0]):
        for t in range(owned):
            x_col[d * owned + t] = xcol_ref[d, :, t * LANES:(t + 1) * LANES]
    acc[...] = jnp.zeros_like(acc)
    add_blocks(copies, count_ref[0, 0], cols_ref, rows_ref, x_col, True, buf, acc)
    part = jnp.zeros((width, LANES), F32)
    for d in range(out_row.shape[0]):
        for t in range(owned):
            a = acc[d * owned + t]
            part = part + a * x_row[d * owned + t].astype(F32)
            out_row[d, :, t * LANES:(t + 1) * LANES] = a.astype(BF16)
    xy = 2.0 * part
    xx = jnp.zeros((width, LANES), F32)
    for t in range(owned):
        here = slice(t * LANES, (t + 1) * LANES)
        xf = x_ref[:, here].astype(F32)
        xy = xy + xf * diag_ref[:, here]
        xx = xx + xf * xf
    tile = split_tile(jnp.sum(xy, axis=1, keepdims=True), jnp.sum(xx, axis=1, keepdims=True), width)
    for d in range(out_col.shape[0]):
        out_col[d, :, :span] = col_in[d]
        out_col[d, :, span:] = tile


def pair_kernel(x_ref, z_ref, many_in, out_ref, many_ref):
    out_ref[0] = x_ref[...]
    out_ref[1] = z_ref[...]


def copies_kernel(x_ref, out_ref):
    for d in range(out_ref.shape[0]):
        out_ref[d] = x_ref[...]


def middle_kernel(col_ref, diag_ref, row_in, sum_ref, row_ref):
    n_col, width, wide = col_ref.shape
    span = wide - LANES
    for t in range(span // LANES):
        here = slice(t * LANES, (t + 1) * LANES)
        total = diag_ref[:, here]
        for d in range(n_col):
            total = total + col_ref[d, :, here].astype(F32)
        sum_ref[:, here] = total
    tile = col_ref[0, :, span:].astype(F32)
    for d in range(1, n_col):
        tile = tile + col_ref[d, :, span:].astype(F32)
    xy, xx = join_tile(tile)
    out = split_tile(xy, xx, width)
    for d in range(row_ref.shape[0]):
        row_ref[d, :, :span] = row_in[d]
        row_ref[d, :, span:] = out


def final_kernel(row_ref, sum_ref, x_ref, pre_ref, image_ref, search_ref):
    n_row, width, wide = row_ref.shape
    span = wide - LANES
    tile = row_ref[0, :, span:].astype(F32)
    for d in range(1, n_row):
        tile = tile + row_ref[d, :, span:].astype(F32)
    xy, xx = join_tile(tile)
    theta = xy / xx
    for t in range(span // LANES):
        here = slice(t * LANES, (t + 1) * LANES)
        total = sum_ref[:, here]
        for d in range(n_row):
            total = total + row_ref[d, :, here].astype(F32)
        image_ref[:, here] = total
        resid = (total - theta * x_ref[:, here].astype(F32)).astype(BF16)
        out = lax.dot_general(resid, pre_ref[t], (((1,), (1,)), ((), ())), preferred_element_type=F32)
        search_ref[:, here] = out.astype(BF16)


VM = pl.BlockSpec(memory_space=pltpu.VMEM)
SM = pl.BlockSpec(memory_space=pltpu.SMEM)
ANY = pl.BlockSpec(memory_space=pl.ANY)
HBM = pl.BlockSpec(memory_space=pltpu.HBM)


def near(x):
    return pltpu.with_memory_space_constraint(x, pltpu.VMEM)


def params(mib):
    return pltpu.CompilerParams(vmem_limit_bytes=mib << 20)


def cost(flops, moved):
    return pl.CostEstimate(flops=flops, bytes_accessed=moved, transcendentals=0)


def per_device(vectors, stiffness, block_row, block_col, block_count, diag_blocks, precond):
    width, span = vectors.shape
    owned, block_len, _ = diag_blocks.shape
    slots = stiffness.shape[2]
    row_devs = lax.axis_size("row")
    col_devs = lax.axis_size("col")
    runs = col_devs // 2
    wide = span + LANES
    count = block_count
    rows = block_row.reshape(slots)
    cols = block_col.reshape(slots)
    block_scratch = [pltpu.VMEM((slots, block_len, block_len), BF16), pltpu.SemaphoreType.DMA((slots // CHUNK,))]
    blocks = pltpu.with_memory_space_constraint(stiffness.reshape(slots, block_len, block_len), pltpu.HBM)

    beside = near(lax.ppermute(vectors, "col", [(i, (i + runs) % col_devs) for i in range(col_devs)]))
    many = pl.pallas_call(
        copies_kernel,
        out_shape=jax.ShapeDtypeStruct((row_devs, width, span), BF16),
        in_specs=[VM],
        out_specs=VM,
        cost_estimate=cost(0, 4 << 20),
    )(vectors)
    pair, many = pl.pallas_call(
        pair_kernel,
        out_shape=(
            jax.ShapeDtypeStruct((2, width, span), BF16),
            jax.ShapeDtypeStruct((row_devs, width, span), BF16),
        ),
        in_specs=[VM, VM, ANY],
        out_specs=(VM, ANY),
        input_output_aliases={2: 1},
    )(vectors, beside, many)
    pair = near(pair)
    xcol = lax.all_to_all(many, "row", 0, 0, tiled=True)
    turned = [
        near(lax.ppermute(pair, "col", [(i, i // runs * runs + (i + s) % runs) for i in range(col_devs)]))
        for s in range(1, runs)
    ]
    out_col, diag_term, x_row = pl.pallas_call(
        first_kernel,
        out_shape=(
            jax.ShapeDtypeStruct((row_devs, width, span), BF16),
            jax.ShapeDtypeStruct((width, span), F32),
            jax.ShapeDtypeStruct((col_devs * owned, width, LANES), BF16),
        ),
        in_specs=[SM] * 3 + [VM] * (runs + 2) + [HBM],
        out_specs=(VM, VM, VM),
        scratch_shapes=[pltpu.VMEM((row_devs * owned + 1, width, LANES), F32)] + block_scratch,
        compiler_params=params(24),
        cost_estimate=cost(4 << 30, 8 << 20),
    )(count, rows, cols, vectors, beside, *turned, diag_blocks, blocks)
    out_row, out_col = pl.pallas_call(
        second_kernel,
        out_shape=(
            jax.ShapeDtypeStruct((col_devs, width, span), BF16),
            jax.ShapeDtypeStruct((row_devs, width, wide), BF16),
        ),
        in_specs=[SM] * 3 + [VM] * 4 + [HBM, VM],
        out_specs=(VM, VM),
        scratch_shapes=[
            pltpu.VMEM((row_devs * owned, width, LANES), BF16),
            pltpu.VMEM((col_devs * owned + 1, width, LANES), F32),
        ] + block_scratch,
        compiler_params=params(24),
    )(count, rows, cols, vectors, diag_term, x_row, xcol, blocks, out_col)
    got_col = lax.all_to_all(out_col, "row", 0, 0, tiled=True)
    part, out_row = pl.pallas_call(
        middle_kernel,
        out_shape=(jax.ShapeDtypeStruct((width, span), F32), jax.ShapeDtypeStruct((col_devs, width, wide), BF16)),
        in_specs=[VM] * 3,
        out_specs=(VM, VM),
        compiler_params=params(16),
    )(got_col, diag_term, out_row)
    got_row = lax.all_to_all(out_row, "col", 0, 0, tiled=True)
    return pl.pallas_call(
        final_kernel,
        out_shape=(jax.ShapeDtypeStruct((width, span), F32), jax.ShapeDtypeStruct((width, span), BF16)),
        in_specs=[VM] * 4,
        out_specs=(VM, VM),
        compiler_params=params(16),
    )(got_row, part, vectors, precond)


def solution(mesh):
    placed = (
        P(None, ("row", "col")),
        P("row", "col", None, None, None),
        P("row", "col", None),
        P("row", "col", None),
        P("row", "col"),
        P(("row", "col"), None, None),
        P(("row", "col"), None, None),
    )
    return jax.shard_map(
        per_device,
        mesh=mesh,
        in_specs=placed,
        out_specs=(P(None, ("row", "col")), P(None, ("row", "col"))),
        check_vma=False,
    )
```

time: 92.5 us -> 78.6 us (0.85)
  blocking collectives: 54.3 us -> 38.2 us
  waiting for transfers between devices: 17.3 us -> 8.17 us
  Pallas kernels: 6.64 us -> 15.2 us
  starting transfers between devices: 7.55 us -> 14.7 us
  local copies, waits for them, and re-layouts: 4.83 us -> 0.02 us
    all_to_all x1, waiting for transfers between devices: 17.3 us -> 0.01 us  [per_device(): xcol = lax.all_to_all(many, 'row', 0, 0, tiled=True)]
    all_to_all x1 -> x0, blocking collectives: 15.8 us -> none  [spread(): lax.all_to_all(jnp.broadcast_to(x[None], (count, *x.shape)), axis, 0, 0,...]
    pallas_call x1 -> x4, Pallas kernels: 5.37 us -> 14 us  [the longest x1 5.52 us: per_device(): pl.pallas_call(second_kernel, out_shape=(jax.ShapeDtypeStruct((col_devs,...]
    ppermute x0 -> x4, waiting for transfers between devices: none -> 8.16 us  [the longest x3 7.61 us: per_device(): lax.ppermute(pair, 'col', [(i, i // runs * runs + (i + s) % runs) for i i...]
    ppermute x0 -> x4, starting transfers between devices: none -> 6.76 us  [the longest x3 4.68 us: per_device(): lax.ppermute(pair, 'col', [(i, i // runs * runs + (i + s) % runs) for i i...]
    unnamed x12, local copies, waits for them, and re-layouts: 2.8 us -> 0.02 us
    all_to_all x1, blocking collectives: 25 us -> 22.8 us  [per_device(): got_col = lax.all_to_all(out_col, 'row', 0, 0, tiled=True)]
    broadcast_in_dim x2 -> x0, local copies, waits for them, and re-layouts: 2.03 us -> none  [spread(): jnp.broadcast_to(x[None], (count, *x.shape))]
  transfers between devices with their start and end apart: 1 -> 5, of which waited for: 1 -> 4; matrix products, arithmetic and copies ran while one was open for 0% -> 0% of each run, Pallas kernels for 0% -> 9%
where the time goes in v2:
time: 78.6 us; the launch traced here: 77.6 us
  blocking collectives  38.2 us (49%)
  Pallas kernels  15.2 us (19%)
  starting transfers between devices  14.7 us (19%)
  waiting for transfers between devices  8.17 us (10%)
  between operations  1.35 us (2%)
    all_to_all x1, blocking collectives, per_device(): got_col = lax.all_to_all(out_col, 'row', 0, 0, tiled=True)  22.8 us
    all_to_all x1, blocking collectives, per_device(): got_row = lax.all_to_all(out_row, 'col', 0, 0, tiled=True)  15.4 us
    all_to_all x1, starting transfers between devices, per_device(): xcol = lax.all_to_all(many, 'row', 0, 0, tiled=True)  7.94 us
    ppermute x3, waiting for transfers between devices, per_device(): lax.ppermute(pair, 'col', [(i, i // runs * runs + (i + s) % runs) for i i...  7.61 us
    pallas_call x1, Pallas kernels, per_device(): pl.pallas_call(second_kernel, out_shape=(jax.ShapeDtypeStruct((col_devs,...  5.52 us
    pallas_call x1, Pallas kernels, per_device(): pl.pallas_call(first_kernel, out_shape=(jax.ShapeDtypeStruct((row_devs, w...  5.02 us
    ppermute x3, starting transfers between devices, per_device(): lax.ppermute(pair, 'col', [(i, i // runs * runs + (i + s) % runs) for i i...  4.68 us
    ppermute x1, starting transfers between devices, per_device(): lax.ppermute(vectors, 'col', [(i, (i + runs) % col_devs) for i in range(c...  2.08 us
  transfers between devices with their start and end apart: 5, of which 4 were waited for; matrix products, arithmetic and copies ran while one was open for 0% of the time, Pallas kernels for 9%

profile of v2, /device:TPU:0, one launch (start us, length us, event | category | flops | bytes accessed | tf_op | source)
XLA Modules:
  0.0 77.6 jit_solution(9551124355488222638)
XLA Ops:
  0.6 2.1 %collective-permute-start = (bf16[16,2048]{1,0:T(8,128)(2,1)}, bf16[16,2048]{1,0:T(8,128)(2,1)S(1)}, u32[]{:S(2)}, u32[]{:S(2)}) collective-permute-start(bf16[16,2048]{1,0:T(8,128)(2,1)} %x_ref.9), channel_id=1, source_target_pairs={{0,4},{1,5},{2,6},{3,7},{4,0},{5,1},{6,2},{7,3},{8,12},{9,13},{10,... | collective-permute-start | bytes 196616 | tf_op jit(solution)/shard_map/ppermute | solution.py:209
  2.7 1.9 %shard_map.86.many_in = bf16[16,16,2048]{2,1,0:T(8,128)(2,1)} custom-call(bf16[16,2048]{1,0:T(8,128)(2,1)} %x_ref.9), custom_call_target="tpu_custom_call" | custom-call | bytes 4194304 | tf_op jit(solution)/shard_map/pallas_call | solution.py:210
  4.6 0.6 collective-permute-done.z_ref
  5.2 1.5 %shard_map.87 = (bf16[2,16,2048]{2,1,0:T(8,128)(2,1)}, bf16[16,16,2048]{2,1,0:T(8,128)(2,1)}) custom-call(bf16[16,2048]{1,0:T(8,128)(2,1)} %x_ref.9, bf16[16,2048]{1,0:T(8,128)(2,1)S(1)} %collective-permute-done.z_ref, bf16[16,16,2048]{2,1,0:T(8,128)(2,1)} %shard_map.86.many_in), custom_call_target="tpu_custom_call", output_to_operand_aliasing={{1}: (2, {})} | custom-call | tf_op jit(solution)/shard_map/pallas_call | solution.py:217
  6.7 0.0 copy-start.5
  6.7 0.0 copy-start
  6.7 0.0 copy-start.2
  6.7 0.0 copy-start.3
  6.7 0.0 copy-start.4
  6.7 7.9 %all-to-all-start = ((bf16[16,16,2048]{2,1,0:T(8,128)(2,1)}), bf16[16,16,2048]{2,1,0:T(8,128)(2,1)S(1)}, u32[]{:S(2)}, u32[]{:S(2)}) async-start(bf16[16,16,2048]{2,1,0:T(8,128)(2,1)} %get-tuple-element.14), calls=%async_computation | async-start | bytes 2097152 | tf_op jit(solution)/shard_map/all_to_all | solution.py:228
  14.7 0.0 copy-done.5
  14.7 3.1 %collective-permute-start.3 = (bf16[2,16,2048]{2,1,0:T(8,128)(2,1)S(1)}, bf16[2,16,2048]{2,1,0:T(8,128)(2,1)S(1)}, u32[]{:S(2)}, u32[]{:S(2)}) collective-permute-start(bf16[2,16,2048]{2,1,0:T(8,128)(2,1)S(1)} %copy-done.5), channel_id=1, source_target_pairs={{0,3},{1,0},{2,1},{3,2},{4,7},{5,4},{6,5},{7,6},{8,11},{9,8},{10,9... | collective-permute-start | bytes 393224 | tf_op jit(solution)/shard_map/ppermute | solution.py:230
  17.8 0.6 collective-permute-start.2
  18.4 1.0 %collective-permute-start.1 = (bf16[2,16,2048]{2,1,0:T(8,128)(2,1)S(1)}, bf16[2,16,2048]{2,1,0:T(8,128)(2,1)S(1)}, u32[]{:S(2)}, u32[]{:S(2)}) collective-permute-start(bf16[2,16,2048]{2,1,0:T(8,128)(2,1)S(1)} %copy-done.5), channel_id=1, source_target_pairs={{0,1},{1,2},{2,3},{3,0},{4,5},{5,6},{6,7},{7,4},{8,9},{9,10},{10,1... | collective-permute-start | bytes 393224 | tf_op jit(solution)/shard_map/ppermute | solution.py:230
  20.0 3.9 %collective-permute-done.3.refs_2_ = bf16[2,16,2048]{2,1,0:T(8,128)(2,1)S(1)} collective-permute-done((bf16[2,16,2048]{2,1,0:T(8,128)(2,1)S(1)}, bf16[2,16,2048]{2,1,0:T(8,128)(2,1)S(1)}, u32[]{:S(2)}, u32[]{:S(2)}) %collective-permute-start.3) | collective-permute-done | bytes 131104 | tf_op jit(solution)/shard_map/ppermute | solution.py:230
  23.9 1.7 %collective-permute-done.2.refs_1_ = bf16[2,16,2048]{2,1,0:T(8,128)(2,1)S(1)} collective-permute-done((bf16[2,16,2048]{2,1,0:T(8,128)(2,1)S(1)}, bf16[2,16,2048]{2,1,0:T(8,128)(2,1)S(1)}, u32[]{:S(2)}, u32[]{:S(2)}) %collective-permute-start.2) | collective-permute-done | bytes 131104 | tf_op jit(solution)/shard_map/ppermute | solution.py:230
  25.6 2.0 %collective-permute-done.1.refs_0_ = bf16[2,16,2048]{2,1,0:T(8,128)(2,1)S(1)} collective-permute-done((bf16[2,16,2048]{2,1,0:T(8,128)(2,1)S(1)}, bf16[2,16,2048]{2,1,0:T(8,128)(2,1)S(1)}, u32[]{:S(2)}, u32[]{:S(2)}) %collective-permute-start.1) | collective-permute-done | bytes 131104 | tf_op jit(solution)/shard_map/ppermute | solution.py:230
  27.6 0.0 copy-done
  27.6 0.0 copy-done.2
  27.6 0.0 copy-done.3
  27.6 0.0 copy-done.4
  27.6 5.0 %shard_map.88 = (bf16[16,16,2048]{2,1,0:T(8,128)(2,1)S(1)}, f32[16,2048]{1,0:T(8,128)S(1)}, bf16[128,16,128]{2,1,0:T(8,128)(2,1)S(1)}) custom-call(s32[1,1]{1,0:T(1,128)S(6)} %copy.11.count_ref, s32[192]{0:T(256)S(1)} %bitcast.3, s32[192]{0:T(256)S(1)} %bitcast.5, bf16[16,2048]{1,0:T(8,128)(2,1)S(1)} %copy-done, ...), custom_call_target="tpu_custom_call" | custom-call | flops 4294967296 | bytes 8388608 | tf_op jit(solution)/shard_map/pallas_call | solution.py:233
  32.7 0.0 all-to-all-done.xcol_ref
  32.7 5.5 %shard_map.89 = (bf16[8,16,2048]{2,1,0:T(8,128)(2,1)S(1)}, bf16[16,16,2176]{2,1,0:T(8,128)(2,1)S(1)}) custom-call(s32[1,1]{1,0:T(1,128)S(6)} %copy.11.count_ref, s32[192]{0:T(256)S(1)} %bitcast.4, s32[192]{0:T(256)S(1)} %bitcast.6, bf16[16,2048]{1,0:T(8,128)(2,1)S(1)} %copy-done, f32[16,2048]{1,0:T(8,128)S(1)} %get-tuple-element.12.diag_ref, ...), custom_call_target="tpu_custom_call" | custom-call | tf_op jit(solution)/shard_map/pallas_call | solution.py:246
  38.2 22.8 %all_to_all.15.col_ref = bf16[16,16,2176]{2,1,0:T(8,128)(2,1)S(1)} all-to-all(bf16[16,16,2176]{2,1,0:T(8,128)(2,1)S(1)} %get-tuple-element.16), channel_id=1, replica_groups=mesh['row'=16,'col'=8] {'row'}, dimensions={0} | all-to-all | bytes 2228224 | tf_op jit(solution)/shard_map/all_to_all | solution.py:260
  61.0 0.0 copy-start.1
  61.0 0.2 shard_map.90
  61.1 15.4 %all_to_all.16.row_ref = bf16[8,16,2176]{2,1,0:T(8,128)(2,1)S(1)} all-to-all(bf16[8,16,2176]{2,1,0:T(8,128)(2,1)S(1)} %get-tuple-element.18), channel_id=1, replica_groups=mesh['row'=16,'col'=8] {'col'}, dimensions={0} | all-to-all | bytes 1114112 | tf_op jit(solution)/shard_map/all_to_all | solution.py:268
  76.6 0.0 copy-done.1
  76.6 1.1 %shard_map.91 = (f32[16,2048]{1,0:T(8,128)}, bf16[16,2048]{1,0:T(8,128)(2,1)}) custom-call(bf16[8,16,2176]{2,1,0:T(8,128)(2,1)S(1)} %all_to_all.16.row_ref, f32[16,2048]{1,0:T(8,128)S(1)} %get-tuple-element.19.sum_ref, bf16[16,2048]{1,0:T(8,128)(2,1)S(1)} %copy-done, bf16[16,128,128]{2,1,0:T(8,128)(2,1)S(1)} %copy-done.1), custom_call_target="tpu_custom_call" | custom-call | tf_op jit(solution)/shard_map/pallas_call | solution.py:269
Async XLA Ops:
  0.6 4.6 %collective-permute-start = (bf16[16,2048]{1,0:T(8,128)(2,1)}, bf16[16,2048]{1,0:T(8,128)(2,1)S(1)}, u32[]{:S(2)}, u32[]{:S(2)}) collective-permute-start(bf16[16,2048]{1,0:T(8,128)(2,1)} %x_ref.9), channel_id=1, source_target_pairs={{0,4},{1,5},{2,6},{3,7},{4,0},{5,1},{6,2},{7,3},{8,12},{9,13},{10,... | collective-permute-start | bytes 196616 | tf_op jit(solution)/shard_map/ppermute | solution.py:209
  6.7 8.0 %copy-start.5 = (bf16[2,16,2048]{2,1,0:T(8,128)(2,1)S(1)}, bf16[2,16,2048]{2,1,0:T(8,128)(2,1)}, u32[]{:S(2)}) copy-start(bf16[2,16,2048]{2,1,0:T(8,128)(2,1)} %get-tuple-element.11) | copy-start | bytes 393220
  6.7 20.9 %copy-start = (bf16[16,2048]{1,0:T(8,128)(2,1)S(1)}, bf16[16,2048]{1,0:T(8,128)(2,1)}, u32[]{:S(2)}) copy-start(bf16[16,2048]{1,0:T(8,128)(2,1)} %x_ref.9) | copy-start | bytes 196612
  6.7 20.9 %copy-start.2 = (s32[1,1,192]{2,1,0:T(1,128)S(1)}, s32[1,1,192]{2,1,0:T(1,128)}, u32[]{:S(2)}) copy-start(s32[1,1,192]{2,1,0:T(1,128)} %param.9) | copy-start | bytes 2308
  6.7 20.9 %copy-start.3 = (s32[1,1,192]{2,1,0:T(1,128)S(1)}, s32[1,1,192]{2,1,0:T(1,128)}, u32[]{:S(2)}) copy-start(s32[1,1,192]{2,1,0:T(1,128)} %param.10) | copy-start | bytes 2308
  6.7 20.9 %copy-start.4 = (bf16[16,128,128]{2,1,0:T(8,128)(2,1)S(1)}, bf16[16,128,128]{2,1,0:T(8,128)(2,1)}, u32[]{:S(2)}) copy-start(bf16[16,128,128]{2,1,0:T(8,128)(2,1)} %refs_3_.1) | copy-start | bytes 1572868
  6.7 26.0 %all-to-all-start = ((bf16[16,16,2048]{2,1,0:T(8,128)(2,1)}), bf16[16,16,2048]{2,1,0:T(8,128)(2,1)S(1)}, u32[]{:S(2)}, u32[]{:S(2)}) async-start(bf16[16,16,2048]{2,1,0:T(8,128)(2,1)} %get-tuple-element.14), calls=%async_computation | async-start | bytes 2097152 | tf_op jit(solution)/shard_map/all_to_all | solution.py:228
  14.7 9.2 %collective-permute-start.3 = (bf16[2,16,2048]{2,1,0:T(8,128)(2,1)S(1)}, bf16[2,16,2048]{2,1,0:T(8,128)(2,1)S(1)}, u32[]{:S(2)}, u32[]{:S(2)}) collective-permute-start(bf16[2,16,2048]{2,1,0:T(8,128)(2,1)S(1)} %copy-done.5), channel_id=1, source_target_pairs={{0,3},{1,0},{2,1},{3,2},{4,7},{5,4},{6,5},{7,6},{8,11},{9,8},{10,9... | collective-permute-start | bytes 393224 | tf_op jit(solution)/shard_map/ppermute | solution.py:230
  17.8 7.9 %collective-permute-start.2 = (bf16[2,16,2048]{2,1,0:T(8,128)(2,1)S(1)}, bf16[2,16,2048]{2,1,0:T(8,128)(2,1)S(1)}, u32[]{:S(2)}, u32[]{:S(2)}) collective-permute-start(bf16[2,16,2048]{2,1,0:T(8,128)(2,1)S(1)} %copy-done.5), channel_id=1, source_target_pairs={{0,2},{1,3},{2,0},{3,1},{4,6},{5,7},{6,4},{7,5},{8,10},{9,11},{10,... | collective-permute-start | bytes 393224 | tf_op jit(solution)/shard_map/ppermute | solution.py:230
  18.4 9.2 %collective-permute-start.1 = (bf16[2,16,2048]{2,1,0:T(8,128)(2,1)S(1)}, bf16[2,16,2048]{2,1,0:T(8,128)(2,1)S(1)}, u32[]{:S(2)}, u32[]{:S(2)}) collective-permute-start(bf16[2,16,2048]{2,1,0:T(8,128)(2,1)S(1)} %copy-done.5), channel_id=1, source_target_pairs={{0,1},{1,2},{2,3},{3,0},{4,5},{5,6},{6,7},{7,4},{8,9},{9,10},{10,1... | collective-permute-start | bytes 393224 | tf_op jit(solution)/shard_map/ppermute | solution.py:230
  61.0 15.6 %copy-start.1 = (bf16[16,128,128]{2,1,0:T(8,128)(2,1)S(1)}, bf16[16,128,128]{2,1,0:T(8,128)(2,1)}, u32[]{:S(2)}) copy-start(bf16[16,128,128]{2,1,0:T(8,128)(2,1)} %pre_ref.1) | copy-start | bytes 1572868

commit v3 on v2

--- a/solution.py
+++ b/solution.py
@@ -7,6 +7,7 @@
 from jax.sharding import PartitionSpec as P
 
 CHUNK = 16
+GROUP = 8
 LANES = 128
 F32 = jnp.float32
 BF16 = jnp.bfloat16
@@ -52,27 +53,27 @@
     return out[:xa.shape[0]], out[xa.shape[0]:]
 
 
-def add_blocks(copies, count, take_ref, give_ref, x_blocks, turned, buf, acc):
-    spare = acc.shape[0] - 1
-    for c, copy in enumerate(copies):
-
-        @pl.when(c * CHUNK < count)
-        def _():
-            copy.wait()
-            found = []
-            for n in range(c * CHUNK, (c + 1) * CHUNK, 2):
-                terms = pair_products(x_blocks[take_ref[n]], x_blocks[take_ref[n + 1]], buf[n:n + 2], turned)
-                for k in range(2):
-                    found.append((jnp.where(n + k < count, give_ref[n + k], spare), terms[k]))
-            for g, term in found:
-                acc[g] += term
-
-
-def first_kernel(count_ref, rows_ref, cols_ref, x_ref, z_ref, *refs):
-    (*pair_refs, diag_ref, stiff_ref, out_col, out_diag, x_row, acc, buf, sems) = refs
-    copies = fetch(stiff_ref, buf, sems, count_ref[0, 0])
+def diag_kernel(x_ref, diag_ref, term_ref, stats_ref):
     width, span = x_ref.shape
-    owned = span // LANES
+    xy = jnp.zeros((width, LANES), F32)
+    xx = jnp.zeros((width, LANES), F32)
+    for g in range(span // LANES):
+        here = slice(g * LANES, (g + 1) * LANES)
+        xg = x_ref[:, here]
+        d = diag_ref[g]
+        term = lax.dot_general(xg, d, (((1,), (1,)), ((), ())), preferred_element_type=F32)
+        term = term + lax.dot_general(xg, d, (((1,), (0,)), ((), ())), preferred_element_type=F32)
+        term_ref[:, here] = term
+        xf = xg.astype(F32)
+        xy = xy + xf * term
+        xx = xx + xf * xf
+    stats_ref[0] = xy
+    stats_ref[1] = xx
+
+
+def rows_kernel(x_ref, z_ref, *refs):
+    (*pair_refs, after_ref, x_row) = refs
+    owned = x_ref.shape[1] // LANES
     runs = len(pair_refs) + 1
     place = lax.axis_index("col")
     zl = place // runs
@@ -84,56 +85,58 @@
                 here = slice(t * LANES, (t + 1) * LANES)
                 piece = (x_ref if k == 0 else z_ref)[:, here] if s == 0 else pair_refs[s - 1][k, :, here]
                 x_row[dev * owned + t] = piece
-    acc[...] = jnp.zeros_like(acc)
-    for g in range(owned):
-        here = slice(g * LANES, (g + 1) * LANES)
-        xg = x_ref[:, here]
-        d = diag_ref[g]
-        term = lax.dot_general(xg, d, (((1,), (1,)), ((), ())), preferred_element_type=F32)
-        out_diag[:, here] = term + lax.dot_general(xg, d, (((1,), (0,)), ((), ())), preferred_element_type=F32)
-    add_blocks(copies, count_ref[0, 0], rows_ref, cols_ref, x_row, False, buf, acc)
-    for d in range(out_col.shape[0]):
-        for t in range(owned):
-            out_col[d, :, t * LANES:(t + 1) * LANES] = acc[d * owned + t].astype(BF16)
-
-
-def second_kernel(count_ref, rows_ref, cols_ref, x_ref, diag_ref, x_row, xcol_ref, stiff_ref, col_in,
-                  out_row, out_col, x_col, acc, buf, sems):
-    copies = fetch(stiff_ref, buf, sems, count_ref[0, 0])
-    width, span = x_ref.shape
+
+
+def block_kernel(count_ref, rows_ref, cols_ref, x_row, xcol_ref, twin_ref, stats_ref, stiff_ref,
+                 out_row, out_col, x_col, acc_row, acc_col, buf, sems):
+    count = count_ref[0, 0]
+    copies = fetch(stiff_ref, buf, sems, count)
+    width, span = xcol_ref.shape[2:]
     owned = span // LANES
-    for d in range(xcol_ref.shape[0]):
-        for t in range(owned):
-            x_col[d * owned + t] = xcol_ref[d, :, t * LANES:(t + 1) * LANES]
-    acc[...] = jnp.zeros_like(acc)
-    add_blocks(copies, count_ref[0, 0], cols_ref, rows_ref, x_col, True, buf, acc)
+    acc_row[...] = jnp.zeros_like(acc_row)
+    acc_col[...] = jnp.zeros_like(acc_col)
+    place = lax.axis_index("row")
+    high = (place // 2) % 2
+    core = place % 2
+    for line in range(xcol_ref.shape[0]):
+        for k in range(2):
+            for ref, twin in ((xcol_ref, 0), (twin_ref, 1)):
+                dev = line * 4 + (high + k) % 2 * 2 + (core + twin) % 2
+                for t in range(owned):
+                    x_col[dev * owned + t] = ref[line, k, :, t * LANES:(t + 1) * LANES]
+    for c, copy in enumerate(copies):
+
+        @pl.when(c * CHUNK < count)
+        def _():
+            copy.wait()
+            for h in range(0, CHUNK, GROUP):
+                found = []
+                for n in range(c * CHUNK + h, c * CHUNK + h + GROUP, 2):
+                    i = [rows_ref[n + k] for k in range(2)]
+                    j = [cols_ref[n + k] for k in range(2)]
+                    to_row = pair_products(x_col[j[0]], x_col[j[1]], buf[n:n + 2], True)
+                    to_col = pair_products(x_row[i[0]], x_row[i[1]], buf[n:n + 2], False)
+                    for k in range(2):
+                        live = n + k < count
+                        found.append((acc_row, jnp.where(live, i[k], acc_row.shape[0] - 1), to_row[k]))
+                        found.append((acc_col, jnp.where(live, j[k], acc_col.shape[0] - 1), to_col[k]))
+                for acc, g, term in found:
+                    acc[g] += term
+
     part = jnp.zeros((width, LANES), F32)
     for d in range(out_row.shape[0]):
         for t in range(owned):
-            a = acc[d * owned + t]
+            a = acc_row[d * owned + t]
             part = part + a * x_row[d * owned + t].astype(F32)
             out_row[d, :, t * LANES:(t + 1) * LANES] = a.astype(BF16)
-    xy = 2.0 * part
-    xx = jnp.zeros((width, LANES), F32)
-    for t in range(owned):
-        here = slice(t * LANES, (t + 1) * LANES)
-        xf = x_ref[:, here].astype(F32)
-        xy = xy + xf * diag_ref[:, here]
-        xx = xx + xf * xf
-    tile = split_tile(jnp.sum(xy, axis=1, keepdims=True), jnp.sum(xx, axis=1, keepdims=True), width)
+    xy = 2.0 * part + stats_ref[0]
+    tile = split_tile(
+        jnp.sum(xy, axis=1, keepdims=True), jnp.sum(stats_ref[1], axis=1, keepdims=True), width
+    )
     for d in range(out_col.shape[0]):
-        out_col[d, :, :span] = col_in[d]
+        for t in range(owned):
+            out_col[d, :, t * LANES:(t + 1) * LANES] = acc_col[d * owned + t].astype(BF16)
         out_col[d, :, span:] = tile
-
-
-def pair_kernel(x_ref, z_ref, many_in, out_ref, many_ref):
-    out_ref[0] = x_ref[...]
-    out_ref[1] = z_ref[...]
-
-
-def copies_kernel(x_ref, out_ref):
-    for d in range(out_ref.shape[0]):
-        out_ref[d] = x_ref[...]
 
 
 def middle_kernel(col_ref, diag_ref, row_in, sum_ref, row_ref):
@@ -174,6 +177,14 @@
         search_ref[:, here] = out.astype(BF16)
 
 
+def prepare_kernel(x_ref, z_ref, h_ref, pair_ref, lines_ref):
+    pair_ref[0] = x_ref[...]
+    pair_ref[1] = z_ref[...]
+    for d in range(lines_ref.shape[0]):
+        lines_ref[d, 0] = x_ref[...]
+        lines_ref[d, 1] = h_ref[...]
+
+
 VM = pl.BlockSpec(memory_space=pltpu.VMEM)
 SM = pl.BlockSpec(memory_space=pltpu.SMEM)
 ANY = pl.BlockSpec(memory_space=pl.ANY)
@@ -207,63 +218,65 @@
     blocks = pltpu.with_memory_space_constraint(stiffness.reshape(slots, block_len, block_len), pltpu.HBM)
 
     beside = near(lax.ppermute(vectors, "col", [(i, (i + runs) % col_devs) for i in range(col_devs)]))
-    many = pl.pallas_call(
-        copies_kernel,
-        out_shape=jax.ShapeDtypeStruct((row_devs, width, span), BF16),
-        in_specs=[VM],
-        out_specs=VM,
-        cost_estimate=cost(0, 4 << 20),
-    )(vectors)
-    pair, many = pl.pallas_call(
-        pair_kernel,
+    above = near(lax.ppermute(vectors, "row", [(i, i ^ 2) for i in range(row_devs)]))
+    lines = row_devs // 4
+    pair, spread = pl.pallas_call(
+        prepare_kernel,
         out_shape=(
             jax.ShapeDtypeStruct((2, width, span), BF16),
-            jax.ShapeDtypeStruct((row_devs, width, span), BF16),
+            jax.ShapeDtypeStruct((lines, 2, width, span), BF16),
         ),
-        in_specs=[VM, VM, ANY],
-        out_specs=(VM, ANY),
-        input_output_aliases={2: 1},
-    )(vectors, beside, many)
+        in_specs=[VM, VM, VM],
+        out_specs=(VM, VM),
+        compiler_params=params(4),
+    )(vectors, beside, above)
     pair = near(pair)
-    xcol = lax.all_to_all(many, "row", 0, 0, tiled=True)
+    same_line = [[x * 4 + k for x in range(lines)] for k in range(4)]
+    xcol = lax.all_to_all(spread, "row", 0, 0, axis_index_groups=same_line, tiled=True)
+    xcol_twin = near(lax.ppermute(xcol, "row", [(i, i ^ 1) for i in range(row_devs)]))
     turned = [
         near(lax.ppermute(pair, "col", [(i, i // runs * runs + (i + s) % runs) for i in range(col_devs)]))
         for s in range(1, runs)
     ]
-    out_col, diag_term, x_row = pl.pallas_call(
-        first_kernel,
-        out_shape=(
-            jax.ShapeDtypeStruct((row_devs, width, span), BF16),
-            jax.ShapeDtypeStruct((width, span), F32),
-            jax.ShapeDtypeStruct((col_devs * owned, width, LANES), BF16),
-        ),
-        in_specs=[SM] * 3 + [VM] * (runs + 2) + [HBM],
-        out_specs=(VM, VM, VM),
-        scratch_shapes=[pltpu.VMEM((row_devs * owned + 1, width, LANES), F32)] + block_scratch,
-        compiler_params=params(24),
+    diag_term, stats = pl.pallas_call(
+        diag_kernel,
+        out_shape=(jax.ShapeDtypeStruct((width, span), F32), jax.ShapeDtypeStruct((2, width, LANES), F32)),
+        in_specs=[VM, VM],
+        out_specs=(VM, VM),
+        compiler_params=params(4),
+        cost_estimate=cost(1 << 28, 1 << 20),
+    )(vectors, diag_blocks)
+    diag_term, stats = near(diag_term), near(stats)
+    x_row = near(pl.pallas_call(
+        rows_kernel,
+        out_shape=jax.ShapeDtypeStruct((col_devs * owned, width, LANES), BF16),
+        in_specs=[VM] * (runs + 1) + [ANY],
+        out_specs=VM,
+        compiler_params=params(4),
         cost_estimate=cost(4 << 30, 8 << 20),
-    )(count, rows, cols, vectors, beside, *turned, diag_blocks, blocks)
+    )(vectors, beside, *turned, xcol))
     out_row, out_col = pl.pallas_call(
-        second_kernel,
+        block_kernel,
         out_shape=(
             jax.ShapeDtypeStruct((col_devs, width, span), BF16),
             jax.ShapeDtypeStruct((row_devs, width, wide), BF16),
         ),
-        in_specs=[SM] * 3 + [VM] * 4 + [HBM, VM],
+        in_specs=[SM] * 3 + [VM] * 4 + [HBM],
         out_specs=(VM, VM),
         scratch_shapes=[
             pltpu.VMEM((row_devs * owned, width, LANES), BF16),
             pltpu.VMEM((col_devs * owned + 1, width, LANES), F32),
+            pltpu.VMEM((row_devs * owned + 1, width, LANES), F32),
         ] + block_scratch,
         compiler_params=params(24),
-    )(count, rows, cols, vectors, diag_term, x_row, xcol, blocks, out_col)
+    )(count, rows, cols, x_row, xcol, xcol_twin, stats, blocks)
     got_col = lax.all_to_all(out_col, "row", 0, 0, tiled=True)
     part, out_row = pl.pallas_call(
         middle_kernel,
         out_shape=(jax.ShapeDtypeStruct((width, span), F32), jax.ShapeDtypeStruct((col_devs, width, wide), BF16)),
         in_specs=[VM] * 3,
         out_specs=(VM, VM),
-        compiler_params=params(16),
+        compiler_params=params(8),
     )(got_col, diag_term, out_row)
     got_row = lax.all_to_all(out_row, "col", 0, 0, tiled=True)
     return pl.pallas_call(
@@ -271,7 +284,7 @@
         out_shape=(jax.ShapeDtypeStruct((width, span), F32), jax.ShapeDtypeStruct((width, span), BF16)),
         in_specs=[VM] * 4,
         out_specs=(VM, VM),
-        compiler_params=params(16),
+        compiler_params=params(8),
     )(got_row, part, vectors, precond)
 
 

time: 78.6 us -> 72.2 us (0.919)
  Pallas kernels: 15.2 us -> 5.88 us
  blocking collectives: 38.2 us -> 40.7 us
  local copies, waits for them, and re-layouts: 0.02 us -> 0.86 us
    pallas_call x4, Pallas kernels: 14 us -> 4.61 us  [the longest x1 3.14 us: per_device(): pl.pallas_call(block_kernel, out_shape=(jax.ShapeDtypeStruct((col_devs, w...]
    ppermute x3, waiting for transfers between devices: 7.61 us -> 1.29 us  [per_device(): lax.ppermute(pair, 'col', [(i, i // runs * runs + (i + s) % runs) for i i...]
    ppermute x0 -> x2, starting transfers between devices: none -> 4.04 us  [the longest x1 4.04 us: per_device(): lax.ppermute(vectors, 'row', [(i, i ^ 2) for i in range(row_devs)])]
    all_to_all x1, waiting for transfers between devices: 0.01 us -> 3.81 us  [per_device(): lax.all_to_all(spread, 'row', 0, 0, axis_index_groups=same_line, tiled=True)]
    all_to_all x1, starting transfers between devices: 7.94 us -> 4.29 us  [per_device(): lax.all_to_all(spread, 'row', 0, 0, axis_index_groups=same_line, tiled=True)]
    all_to_all x1, blocking collectives: 22.8 us -> 24.6 us  [per_device(): got_col = lax.all_to_all(out_col, 'row', 0, 0, tiled=True)]
    ppermute x1, waiting for transfers between devices: 0.55 us -> 2.02 us  [per_device(): lax.ppermute(vectors, 'col', [(i, (i + runs) % col_devs) for i in range(c...]
    ppermute x0 -> x2, waiting for transfers between devices: none -> 1.44 us  [the longest x1 1.44 us: per_device(): lax.ppermute(vectors, 'row', [(i, i ^ 2) for i in range(row_devs)])]
  transfers between devices with their start and end apart: 5 -> 7, of which waited for: 4 -> 4; matrix products, arithmetic and copies ran while one was open for 0% -> 0% of each run, Pallas kernels for 9% -> 1%
where the time goes in v3:
time: 72.2 us; the launch traced here: 71.3 us
  blocking collectives  40.7 us (56%)
  starting transfers between devices  14 us (19%)
  waiting for transfers between devices  8.56 us (12%)
  Pallas kernels  5.88 us (8%)
  between operations  1.37 us (2%)
  local copies, waits for them, and re-layouts  0.86 us (1%)
    all_to_all x1, blocking collectives, per_device(): got_col = lax.all_to_all(out_col, 'row', 0, 0, tiled=True)  24.6 us
    all_to_all x1, blocking collectives, per_device(): got_row = lax.all_to_all(out_row, 'col', 0, 0, tiled=True)  16.1 us
    ppermute x3, starting transfers between devices, per_device(): lax.ppermute(pair, 'col', [(i, i // runs * runs + (i + s) % runs) for i i...  4.61 us
    all_to_all x1, starting transfers between devices, per_device(): lax.all_to_all(spread, 'row', 0, 0, axis_index_groups=same_line, tiled=True)  4.29 us
    ppermute x1, starting transfers between devices, per_device(): lax.ppermute(vectors, 'row', [(i, i ^ 2) for i in range(row_devs)])  4.04 us
    all_to_all x1, waiting for transfers between devices, per_device(): lax.all_to_all(spread, 'row', 0, 0, axis_index_groups=same_line, tiled=True)  3.81 us
    pallas_call x1, Pallas kernels, per_device(): pl.pallas_call(block_kernel, out_shape=(jax.ShapeDtypeStruct((col_devs, w...  3.14 us
    ppermute x1, waiting for transfers between devices, per_device(): lax.ppermute(vectors, 'col', [(i, (i + runs) % col_devs) for i in range(c...  2.02 us
  transfers between devices with their start and end apart: 7, of which 4 were waited for; matrix products, arithmetic and copies ran while one was open for 0% of the time, Pallas kernels for 1%

profile of v3, /device:TPU:0, one launch (start us, length us, event | category | flops | bytes accessed | tf_op | source)
XLA Modules:
  0.0 71.3 jit_solution(1502918857683095745)
XLA Ops:
  0.6 4.0 %collective-permute-start.1 = (bf16[16,2048]{1,0:T(8,128)(2,1)}, bf16[16,2048]{1,0:T(8,128)(2,1)S(1)}, u32[]{:S(2)}, u32[]{:S(2)}) collective-permute-start(bf16[16,2048]{1,0:T(8,128)(2,1)} %x_ref.7), channel_id=1, source_target_pairs={{0,16},{8,24},{16,0},{24,8},{32,48},{40,56},{48,32},{56,40},{64,80... | collective-permute-start | bytes 196616 | tf_op jit(solution)/shard_map/ppermute | solution.py:221
  4.7 1.0 %collective-permute-start = (bf16[16,2048]{1,0:T(8,128)(2,1)}, bf16[16,2048]{1,0:T(8,128)(2,1)S(1)}, u32[]{:S(2)}, u32[]{:S(2)}) collective-permute-start(bf16[16,2048]{1,0:T(8,128)(2,1)} %x_ref.7), channel_id=1, source_target_pairs={{0,4},{1,5},{2,6},{3,7},{4,0},{5,1},{6,2},{7,3},{8,12},{9,13},{10,... | collective-permute-start | bytes 196616 | tf_op jit(solution)/shard_map/ppermute | solution.py:220
  5.7 1.4 %collective-permute-done.1.h_ref = bf16[16,2048]{1,0:T(8,128)(2,1)S(1)} collective-permute-done((bf16[16,2048]{1,0:T(8,128)(2,1)}, bf16[16,2048]{1,0:T(8,128)(2,1)S(1)}, u32[]{:S(2)}, u32[]{:S(2)}) %collective-permute-start.1) | collective-permute-done | bytes 65568 | tf_op jit(solution)/shard_map/ppermute | solution.py:221
  7.1 2.0 %collective-permute-done.z_ref = bf16[16,2048]{1,0:T(8,128)(2,1)S(1)} collective-permute-done((bf16[16,2048]{1,0:T(8,128)(2,1)}, bf16[16,2048]{1,0:T(8,128)(2,1)S(1)}, u32[]{:S(2)}, u32[]{:S(2)}) %collective-permute-start) | collective-permute-done | bytes 65568 | tf_op jit(solution)/shard_map/ppermute | solution.py:220
  9.1 0.0 copy-start.1
  9.1 0.8 %copy-done.1 = bf16[16,2048]{1,0:T(8,128)(2,1)S(1)} copy-done((bf16[16,2048]{1,0:T(8,128)(2,1)S(1)}, bf16[16,2048]{1,0:T(8,128)(2,1)}, u32[]{:S(2)}) %copy-start.1) | copy-done | bytes 65560
  10.0 0.0 copy-start.2
  10.0 0.0 copy-start.5
  10.0 0.8 %shard_map.86 = (bf16[2,16,2048]{2,1,0:T(8,128)(2,1)S(1)}, bf16[4,2,16,2048]{3,2,1,0:T(8,128)(2,1)}) custom-call(bf16[16,2048]{1,0:T(8,128)(2,1)S(1)} %copy-done.1, bf16[16,2048]{1,0:T(8,128)(2,1)S(1)} %collective-permute-done.z_ref, bf16[16,2048]{1,0:T(8,128)(2,1)S(1)} %collective-permute-done.1.h_ref), custom_call_target="tpu_custom_call" | custom-call | tf_op jit(solution)/shard_map/pallas_call | solution.py:223
  10.8 4.3 %all-to-all-start = ((bf16[4,2,16,2048]{3,2,1,0:T(8,128)(2,1)}), bf16[4,2,16,2048]{3,2,1,0:T(8,128)(2,1)S(1)}, u32[]{:S(2)}, u32[]{:S(2)}) async-start(bf16[4,2,16,2048]{3,2,1,0:T(8,128)(2,1)} %get-tuple-element.11), calls=%async_computation | async-start | bytes 1048576 | tf_op jit(solution)/shard_map/all_to_all | solution.py:235
  15.1 3.0 %collective-permute-start.4 = (bf16[2,16,2048]{2,1,0:T(8,128)(2,1)S(1)}, bf16[2,16,2048]{2,1,0:T(8,128)(2,1)S(1)}, u32[]{:S(2)}, u32[]{:S(2)}) collective-permute-start(bf16[2,16,2048]{2,1,0:T(8,128)(2,1)S(1)} %get-tuple-element.10), channel_id=1, source_target_pairs={{0,3},{1,0},{2,1},{3,2},{4,7},{5,4},{6,5},{7,6},{8,11},{9,8},{10,9... | collective-permute-start | bytes 393224 | tf_op jit(solution)/shard_map/ppermute | solution.py:238
  18.1 0.6 collective-permute-start.3
  18.8 1.0 %collective-permute-start.2 = (bf16[2,16,2048]{2,1,0:T(8,128)(2,1)S(1)}, bf16[2,16,2048]{2,1,0:T(8,128)(2,1)S(1)}, u32[]{:S(2)}, u32[]{:S(2)}) collective-permute-start(bf16[2,16,2048]{2,1,0:T(8,128)(2,1)S(1)} %get-tuple-element.10), channel_id=1, source_target_pairs={{0,1},{1,2},{2,3},{3,0},{4,5},{5,6},{6,7},{7,4},{8,9},{9,10},{10,1... | collective-permute-start | bytes 393224 | tf_op jit(solution)/shard_map/ppermute | solution.py:238
  19.7 3.8 %all-to-all-done.refs_3_.xcol_ref = bf16[4,2,16,2048]{3,2,1,0:T(8,128)(2,1)S(1)} async-done(((bf16[4,2,16,2048]{3,2,1,0:T(8,128)(2,1)}), bf16[4,2,16,2048]{3,2,1,0:T(8,128)(2,1)S(1)}, u32[]{:S(2)}, u32[]{:S(2)}) %all-to-all-start) | async-done | bytes 524320 | tf_op jit(solution)/shard_map/all_to_all | solution.py:235
  23.5 0.0 collective-permute-start.5
  24.2 0.0 copy-done.2
  24.2 0.0 copy-done.5
  24.2 0.5 shard_map.88
  24.8 0.0 copy-start.3
  24.8 0.0 collective-permute-done.4.refs_2_
  24.8 0.0 collective-permute-done.3.refs_1_
  24.8 1.3 %collective-permute-done.2.refs_0_ = bf16[2,16,2048]{2,1,0:T(8,128)(2,1)S(1)} collective-permute-done((bf16[2,16,2048]{2,1,0:T(8,128)(2,1)S(1)}, bf16[2,16,2048]{2,1,0:T(8,128)(2,1)S(1)}, u32[]{:S(2)}, u32[]{:S(2)}) %collective-permute-start.2) | collective-permute-done | bytes 131104 | tf_op jit(solution)/shard_map/ppermute | solution.py:238
  26.1 0.1 shard_map.87.x_row
  26.2 0.0 collective-permute-done.5.twin_ref
  26.2 0.0 copy-done.3
  26.2 0.0 copy-done.4
  26.2 3.1 %shard_map.89 = (bf16[8,16,2048]{2,1,0:T(8,128)(2,1)S(1)}, bf16[16,16,2176]{2,1,0:T(8,128)(2,1)S(1)}) custom-call(s32[1,1]{1,0:T(1,128)S(6)} %copy.9.count_ref, s32[192]{0:T(256)S(1)} %bitcast.3, s32[192]{0:T(256)S(1)} %bitcast.4, bf16[128,16,128]{2,1,0:T(8,128)(2,1)S(1)} %shard_map.87.x_row, bf16[4,2,16,2048]{3,2,1,0:T(8,128)(2,1)S(1)} %all-to-all-done.refs_3_.xcol_ref, ...), custom_call_target="tpu_custom_call" | custom-call | tf_op jit(solution)/shard_map/pallas_call | solution.py:258
  29.4 24.6 %all_to_all.15.col_ref = bf16[16,16,2176]{2,1,0:T(8,128)(2,1)S(1)} all-to-all(bf16[16,16,2176]{2,1,0:T(8,128)(2,1)S(1)} %get-tuple-element.13), channel_id=1, replica_groups=mesh['row'=16,'col'=8] {'row'}, dimensions={0} | all-to-all | bytes 2228224 | tf_op jit(solution)/shard_map/all_to_all | solution.py:273
  54.0 0.2 shard_map.90
  54.2 16.1 %all_to_all.16.row_ref = bf16[8,16,2176]{2,1,0:T(8,128)(2,1)S(1)} all-to-all(bf16[8,16,2176]{2,1,0:T(8,128)(2,1)S(1)} %get-tuple-element.16), channel_id=1, replica_groups=mesh['row'=16,'col'=8] {'col'}, dimensions={0} | all-to-all | bytes 1114112 | tf_op jit(solution)/shard_map/all_to_all | solution.py:281
  70.3 0.0 copy-done
  70.3 1.1 %shard_map.91 = (f32[16,2048]{1,0:T(8,128)}, bf16[16,2048]{1,0:T(8,128)(2,1)}) custom-call(bf16[8,16,2176]{2,1,0:T(8,128)(2,1)S(1)} %all_to_all.16.row_ref, f32[16,2048]{1,0:T(8,128)S(1)} %get-tuple-element.17.sum_ref, bf16[16,2048]{1,0:T(8,128)(2,1)S(1)} %copy-done.2, bf16[16,128,128]{2,1,0:T(8,128)(2,1)S(1)} %copy-done), custom_call_target="tpu_custom_call" | custom-call | tf_op jit(solution)/shard_map/pallas_call | solution.py:282
  (2 shorter events, 0.0 us)
Async XLA Ops:
  0.6 6.5 %collective-permute-start.1 = (bf16[16,2048]{1,0:T(8,128)(2,1)}, bf16[16,2048]{1,0:T(8,128)(2,1)S(1)}, u32[]{:S(2)}, u32[]{:S(2)}) collective-permute-start(bf16[16,2048]{1,0:T(8,128)(2,1)} %x_ref.7), channel_id=1, source_target_pairs={{0,16},{8,24},{16,0},{24,8},{32,48},{40,56},{48,32},{56,40},{64,80... | collective-permute-start | bytes 196616 | tf_op jit(solution)/shard_map/ppermute | solution.py:221
  4.7 4.5 %collective-permute-start = (bf16[16,2048]{1,0:T(8,128)(2,1)}, bf16[16,2048]{1,0:T(8,128)(2,1)S(1)}, u32[]{:S(2)}, u32[]{:S(2)}) collective-permute-start(bf16[16,2048]{1,0:T(8,128)(2,1)} %x_ref.7), channel_id=1, source_target_pairs={{0,4},{1,5},{2,6},{3,7},{4,0},{5,1},{6,2},{7,3},{8,12},{9,13},{10,... | collective-permute-start | bytes 196616 | tf_op jit(solution)/shard_map/ppermute | solution.py:220
  9.1 0.8 %copy-start.1 = (bf16[16,2048]{1,0:T(8,128)(2,1)S(1)}, bf16[16,2048]{1,0:T(8,128)(2,1)}, u32[]{:S(2)}) copy-start(bf16[16,2048]{1,0:T(8,128)(2,1)} %x_ref.7) | copy-start | bytes 196612
  10.0 14.2 %copy-start.2 = (bf16[16,2048]{1,0:T(8,128)(2,1)S(1)}, bf16[16,2048]{1,0:T(8,128)(2,1)}, u32[]{:S(2)}) copy-start(bf16[16,2048]{1,0:T(8,128)(2,1)} %x_ref.7) | copy-start | bytes 196612
  10.0 14.2 %copy-start.5 = (bf16[16,128,128]{2,1,0:T(8,128)(2,1)S(1)}, bf16[16,128,128]{2,1,0:T(8,128)(2,1)}, u32[]{:S(2)}) copy-start(bf16[16,128,128]{2,1,0:T(8,128)(2,1)} %diag_ref.1) | copy-start | bytes 1572868
  10.8 12.7 %all-to-all-start = ((bf16[4,2,16,2048]{3,2,1,0:T(8,128)(2,1)}), bf16[4,2,16,2048]{3,2,1,0:T(8,128)(2,1)S(1)}, u32[]{:S(2)}, u32[]{:S(2)}) async-start(bf16[4,2,16,2048]{3,2,1,0:T(8,128)(2,1)} %get-tuple-element.11), calls=%async_computation | async-start | bytes 1048576 | tf_op jit(solution)/shard_map/all_to_all | solution.py:235
  15.1 9.7 %collective-permute-start.4 = (bf16[2,16,2048]{2,1,0:T(8,128)(2,1)S(1)}, bf16[2,16,2048]{2,1,0:T(8,128)(2,1)S(1)}, u32[]{:S(2)}, u32[]{:S(2)}) collective-permute-start(bf16[2,16,2048]{2,1,0:T(8,128)(2,1)S(1)} %get-tuple-element.10), channel_id=1, source_target_pairs={{0,3},{1,0},{2,1},{3,2},{4,7},{5,4},{6,5},{7,6},{8,11},{9,8},{10,9... | collective-permute-start | bytes 393224 | tf_op jit(solution)/shard_map/ppermute | solution.py:238
  18.1 6.6 %collective-permute-start.3 = (bf16[2,16,2048]{2,1,0:T(8,128)(2,1)S(1)}, bf16[2,16,2048]{2,1,0:T(8,128)(2,1)S(1)}, u32[]{:S(2)}, u32[]{:S(2)}) collective-permute-start(bf16[2,16,2048]{2,1,0:T(8,128)(2,1)S(1)} %get-tuple-element.10), channel_id=1, source_target_pairs={{0,2},{1,3},{2,0},{3,1},{4,6},{5,7},{6,4},{7,5},{8,10},{9,11},{10,... | collective-permute-start | bytes 393224 | tf_op jit(solution)/shard_map/ppermute | solution.py:238
  18.8 7.3 %collective-permute-start.2 = (bf16[2,16,2048]{2,1,0:T(8,128)(2,1)S(1)}, bf16[2,16,2048]{2,1,0:T(8,128)(2,1)S(1)}, u32[]{:S(2)}, u32[]{:S(2)}) collective-permute-start(bf16[2,16,2048]{2,1,0:T(8,128)(2,1)S(1)} %get-tuple-element.10), channel_id=1, source_target_pairs={{0,1},{1,2},{2,3},{3,0},{4,5},{5,6},{6,7},{7,4},{8,9},{9,10},{10,1... | collective-permute-start | bytes 393224 | tf_op jit(solution)/shard_map/ppermute | solution.py:238
  23.5 2.6 %collective-permute-start.5 = (bf16[4,2,16,2048]{3,2,1,0:T(8,128)(2,1)S(1)}, bf16[4,2,16,2048]{3,2,1,0:T(8,128)(2,1)S(1)}, u32[]{:S(2)}, u32[]{:S(2)}) collective-permute-start(bf16[4,2,16,2048]{3,2,1,0:T(8,128)(2,1)S(1)} %all-to-all-done.refs_3_.xcol_ref), channel_id=1, source_target_pairs={{0,8},{8,0},{16,24},{24,16},{32,40},{40,32},{48,56},{56,48},{64,72... | collective-permute-start | bytes 1572872 | tf_op jit(solution)/shard_map/ppermute | solution.py:236
  24.8 1.4 %copy-start.3 = (s32[1,1,192]{2,1,0:T(1,128)S(1)}, s32[1,1,192]{2,1,0:T(1,128)}, u32[]{:S(2)}) copy-start(s32[1,1,192]{2,1,0:T(1,128)} %param.9) | copy-start | bytes 2308
  24.8 1.4 %copy-start.4 = (s32[1,1,192]{2,1,0:T(1,128)S(1)}, s32[1,1,192]{2,1,0:T(1,128)}, u32[]{:S(2)}) copy-start(s32[1,1,192]{2,1,0:T(1,128)} %param.10) | copy-start | bytes 2308
  54.0 16.3 %copy-start = (bf16[16,128,128]{2,1,0:T(8,128)(2,1)S(1)}, bf16[16,128,128]{2,1,0:T(8,128)(2,1)}, u32[]{:S(2)}) copy-start(bf16[16,128,128]{2,1,0:T(8,128)(2,1)} %pre_ref.1) | copy-start | bytes 1572868

commit v4 on v3

--- a/solution.py
+++ b/solution.py
@@ -87,8 +87,8 @@
                 x_row[dev * owned + t] = piece
 
 
-def block_kernel(count_ref, rows_ref, cols_ref, x_row, xcol_ref, twin_ref, stats_ref, stiff_ref,
-                 out_row, out_col, x_col, acc_row, acc_col, buf, sems):
+def block_kernel(count_ref, rows_ref, cols_ref, x_row, xcol_ref, twin_ref, stats_ref, stiff_ref, *refs):
+    (*ring_refs, row_keep, col_keep, core_out, x_col, acc_row, acc_col, buf, sems) = refs
     count = count_ref[0, 0]
     copies = fetch(stiff_ref, buf, sems, count)
     width, span = xcol_ref.shape[2:]
@@ -123,54 +123,99 @@
                 for acc, g, term in found:
                     acc[g] += term
 
+    runs = len(ring_refs) + 1
+    place = lax.axis_index("col")
     part = jnp.zeros((width, LANES), F32)
-    for d in range(out_row.shape[0]):
-        for t in range(owned):
-            a = acc_row[d * owned + t]
-            part = part + a * x_row[d * owned + t].astype(F32)
-            out_row[d, :, t * LANES:(t + 1) * LANES] = a.astype(BF16)
-    xy = 2.0 * part + stats_ref[0]
-    tile = split_tile(
-        jnp.sum(xy, axis=1, keepdims=True), jnp.sum(stats_ref[1], axis=1, keepdims=True), width
-    )
-    for d in range(out_col.shape[0]):
-        for t in range(owned):
-            out_col[d, :, t * LANES:(t + 1) * LANES] = acc_col[d * owned + t].astype(BF16)
-        out_col[d, :, span:] = tile
-
-
-def middle_kernel(col_ref, diag_ref, row_in, sum_ref, row_ref):
-    n_col, width, wide = col_ref.shape
-    span = wide - LANES
-    for t in range(span // LANES):
+    for s in range(runs):
+        for k in range(2):
+            dev = (place // runs + k) % 2 * runs + (place + s) % runs
+            for t in range(owned):
+                here = slice(t * LANES, (t + 1) * LANES)
+                a = acc_row[dev * owned + t]
+                part = part + a * x_row[dev * owned + t].astype(F32)
+                if s == 0:
+                    row_keep[k, :, here] = a
+                else:
+                    ring_refs[s - 1][k, :, here] = a.astype(BF16)
+    place = lax.axis_index("row")
+    lines = xcol_ref.shape[0]
+    for s in range(lines):
+        for k in range(2):
+            dev = (place // 4 + s) % lines * 4 + (place // 2 + k) % 2 * 2
+            for t in range(owned):
+                here = slice(t * LANES, (t + 1) * LANES)
+                col_keep[2 * s + k, :, here] = acc_col[(dev + place % 2) * owned + t]
+                core_out[2 * s + k, :, here] = acc_col[(dev + (place + 1) % 2) * owned + t].astype(BF16)
+    xy = jnp.sum(2.0 * part + stats_ref[0], axis=1, keepdims=True)
+    xx = jnp.sum(stats_ref[1], axis=1, keepdims=True)
+    core_out[2 * lines, :, :LANES] = split_tile(xy, xx, width)
+    core_out[2 * lines, :, LANES:] = jnp.zeros((width, span - LANES), BF16)
+
+
+def tile_sum(first, *more):
+    total = first.astype(F32)
+    for tile in more:
+        total = total + tile.astype(F32)
+    return split_tile(*join_tile(total), first.shape[0])
+
+
+def core_kernel(own_ref, got_ref, keep_ref, *refs):
+    (*line_refs, col_keep, tile_ref) = refs
+    span = own_ref.shape[2]
+    last = keep_ref.shape[0]
+    tile = tile_sum(own_ref[last, :, :LANES], got_ref[last, :, :LANES])
+    tile_ref[...] = tile
+    for n in range(keep_ref.shape[0]):
+        s, k = divmod(n, 2)
+        for t in range(span // LANES):
+            here = slice(t * LANES, (t + 1) * LANES)
+            total = keep_ref[n, :, here] + got_ref[n, :, here].astype(F32)
+            if s == 0:
+                col_keep[k, :, here] = total
+            else:
+                line_refs[s - 1][k, :, here] = total.astype(BF16)
+        if s > 0:
+            line_refs[s - 1][k, :, span:] = tile
+
+
+def line_tile_kernel(tile_ref, *refs):
+    *got, out = refs
+    span = got[0].shape[2] - LANES
+    out[...] = tile_sum(tile_ref[...], *[ref[0, :, span:] for ref in got])
+
+
+def ring_tile_kernel(*refs):
+    *tiles, col_raw, row_raw, col_out, row_out, out = refs
+    span = col_raw.shape[1]
+    tile = tile_sum(*[ref[...] for ref in tiles])
+    out[...] = tile
+    for raw, ref in ((col_raw, col_out), (row_raw, row_out)):
+        ref[:, :span] = raw[...]
+        ref[:, span:] = tile
+
+
+def sums_kernel(diag_ref, col_keep, row_keep, *refs):
+    (*got, own_ref, col_raw, row_raw) = refs
+    half = len(got) // 2
+    for t in range(own_ref.shape[1] // LANES):
         here = slice(t * LANES, (t + 1) * LANES)
-        total = diag_ref[:, here]
-        for d in range(n_col):
-            total = total + col_ref[d, :, here].astype(F32)
-        sum_ref[:, here] = total
-    tile = col_ref[0, :, span:].astype(F32)
-    for d in range(1, n_col):
-        tile = tile + col_ref[d, :, span:].astype(F32)
-    xy, xx = join_tile(tile)
-    out = split_tile(xy, xx, width)
-    for d in range(row_ref.shape[0]):
-        row_ref[d, :, :span] = row_in[d]
-        row_ref[d, :, span:] = out
-
-
-def final_kernel(row_ref, sum_ref, x_ref, pre_ref, image_ref, search_ref):
-    n_row, width, wide = row_ref.shape
-    span = wide - LANES
-    tile = row_ref[0, :, span:].astype(F32)
-    for d in range(1, n_row):
-        tile = tile + row_ref[d, :, span:].astype(F32)
-    xy, xx = join_tile(tile)
+        total = [[keep[k, :, here] for k in range(2)] for keep in (col_keep, row_keep)]
+        for g, ref in enumerate(got):
+            for k in range(2):
+                total[g // half][k] = total[g // half][k] + ref[k, :, here].astype(F32)
+        own_ref[:, here] = diag_ref[:, here] + total[0][0] + total[1][0]
+        col_raw[:, here] = total[0][1].astype(BF16)
+        row_raw[:, here] = total[1][1].astype(BF16)
+
+
+def final_kernel(own_ref, col_ref, row_ref, tile_ref, across_ref, x_ref, pre_ref, image_ref, search_ref):
+    span = own_ref.shape[1]
+    tile = tile_ref[...].astype(F32) + across_ref[...].astype(F32)
+    xy, xx = join_tile(tile + col_ref[:, span:].astype(F32) + row_ref[:, span:].astype(F32))
     theta = xy / xx
     for t in range(span // LANES):
         here = slice(t * LANES, (t + 1) * LANES)
-        total = sum_ref[:, here]
-        for d in range(n_row):
-            total = total + row_ref[d, :, here].astype(F32)
+        total = own_ref[:, here] + col_ref[:, here].astype(F32) + row_ref[:, here].astype(F32)
         image_ref[:, here] = total
         resid = (total - theta * x_ref[:, here].astype(F32)).astype(BF16)
         out = lax.dot_general(resid, pre_ref[t], (((1,), (1,)), ((), ())), preferred_element_type=F32)
@@ -255,14 +300,34 @@
         compiler_params=params(4),
         cost_estimate=cost(4 << 30, 8 << 20),
     )(vectors, beside, *turned, xcol))
-    out_row, out_col = pl.pallas_call(
+    def shape(*dims, dtype=BF16):
+        return jax.ShapeDtypeStruct(dims, dtype)
+
+    def along_y(x, s):
+        return near(lax.ppermute(x, "col", [(i, i // runs * runs + (i + s) % runs) for i in range(col_devs)]))
+
+    def along_x(x, s):
+        return near(lax.ppermute(x, "row", [(i, (i + 4 * s) % row_devs) for i in range(row_devs)]))
+
+    def call(kernel, out_shape, *args):
+        return pl.pallas_call(
+            kernel,
+            out_shape=out_shape,
+            in_specs=[VM] * len(args),
+            out_specs=jax.tree.map(lambda _: VM, out_shape),
+            compiler_params=params(4),
+        )(*args)
+
+    *ring, row_keep, col_keep, core_out = pl.pallas_call(
         block_kernel,
         out_shape=(
-            jax.ShapeDtypeStruct((col_devs, width, span), BF16),
-            jax.ShapeDtypeStruct((row_devs, width, wide), BF16),
+            *[shape(2, width, span)] * (runs - 1),
+            shape(2, width, span, dtype=F32),
+            shape(2 * lines, width, span, dtype=F32),
+            shape(2 * lines + 1, width, span),
         ),
         in_specs=[SM] * 3 + [VM] * 4 + [HBM],
-        out_specs=(VM, VM),
+        out_specs=(VM,) * (runs + 2),
         scratch_shapes=[
             pltpu.VMEM((row_devs * owned, width, LANES), BF16),
             pltpu.VMEM((col_devs * owned + 1, width, LANES), F32),
@@ -270,22 +335,39 @@
         ] + block_scratch,
         compiler_params=params(24),
     )(count, rows, cols, x_row, xcol, xcol_twin, stats, blocks)
-    got_col = lax.all_to_all(out_col, "row", 0, 0, tiled=True)
-    part, out_row = pl.pallas_call(
-        middle_kernel,
-        out_shape=(jax.ShapeDtypeStruct((width, span), F32), jax.ShapeDtypeStruct((col_devs, width, wide), BF16)),
-        in_specs=[VM] * 3,
-        out_specs=(VM, VM),
-        compiler_params=params(8),
-    )(got_col, diag_term, out_row)
-    got_row = lax.all_to_all(out_row, "col", 0, 0, tiled=True)
+    got_core = near(lax.ppermute(core_out, "row", [(i, i ^ 1) for i in range(row_devs)]))
+    *line, col_keep, tile = call(
+        core_kernel,
+        (*[shape(2, width, wide)] * (lines - 1), shape(2, width, span, dtype=F32), shape(width, LANES)),
+        core_out, got_core, col_keep,
+    )
+    line = [along_x(part, s + 1) for s, part in enumerate(line)]
+    ring = [along_y(part, s + 1) for s, part in enumerate(ring)]
+    tile = call(line_tile_kernel, shape(width, LANES), tile, *line)
+    tiles = [along_y(tile, s) for s in range(1, runs)]
+    own, col_raw, row_raw = call(
+        sums_kernel,
+        (shape(width, span, dtype=F32), shape(width, span), shape(width, span)),
+        diag_term, col_keep, row_keep, *line, *ring,
+    )
+    col_out, row_out, tile = call(
+        ring_tile_kernel,
+        (shape(width, wide), shape(width, wide), shape(width, LANES)),
+        tile, *tiles, col_raw, row_raw,
+    )
+    got_col = near(lax.ppermute(col_out, "row", [(i, i ^ 2) for i in range(row_devs)]))
+    got_row = near(lax.ppermute(row_out, "col", [(i, (i + runs) % col_devs) for i in range(col_devs)]))
+    across = near(lax.ppermute(
+        tile, ("row", "col"),
+        [(r * col_devs + c, (r ^ 2) * col_devs + (c + runs) % col_devs) for r in range(row_devs) for c in range(col_devs)],
+    ))
     return pl.pallas_call(
         final_kernel,
-        out_shape=(jax.ShapeDtypeStruct((width, span), F32), jax.ShapeDtypeStruct((width, span), BF16)),
-        in_specs=[VM] * 4,
+        out_shape=(shape(width, span, dtype=F32), shape(width, span)),
+        in_specs=[VM] * 7,
         out_specs=(VM, VM),
-        compiler_params=params(8),
-    )(got_row, part, vectors, precond)
+        compiler_params=params(4),
+    )(own, got_col, got_row, tile, across, vectors, precond)
 
 
 def solution(mesh):

time: 72.2 us -> 63.6 us (0.88); the launches traced: 71.3 us -> 63.7 us
  blocking collectives: 40.7 us -> 0 us
  starting transfers between devices: 14 us -> 37.5 us
  waiting for transfers between devices: 8.56 us -> 15.6 us
  local copies, waits for them, and re-layouts: 0.86 us -> 3.25 us
    all_to_all x2 -> x0, blocking collectives: 40.7 us -> none  [the longest x1 24.6 us: per_device(): got_col = lax.all_to_all(out_col, 'row', 0, 0, tiled=True)]
    ppermute x0 -> x13, starting transfers between devices: none -> 23.6 us  [the longest x6 11.3 us: along_y(): lax.ppermute(x, 'col', [(i, i // runs * runs + (i + s) % runs) for i in r...]
    ppermute x0 -> x13, waiting for transfers between devices: none -> 8.35 us  [the longest x6 3.38 us: along_y(): lax.ppermute(x, 'col', [(i, i // runs * runs + (i + s) % runs) for i in r...]
    unnamed x12 -> x14, local copies, waits for them, and re-layouts: 0.86 us -> 3.25 us
    ppermute x3, waiting for transfers between devices: 1.29 us -> 0.01 us  [per_device(): lax.ppermute(pair, 'col', [(i, i // runs * runs + (i + s) % runs) for i i...]
    pallas_call x3 -> x6, Pallas kernels: 4.41 us -> 4.37 us  [the longest x1 2.82 us: per_device(): pl.pallas_call(block_kernel, out_shape=(*[shape(2, width, span)] * (runs...]
  transfers between devices with their start and end apart: 7 -> 20, of which waited for: 4 -> 6; matrix products, arithmetic and copies ran while one was open for 0% -> 0% of each run, Pallas kernels for 1% -> 1%
where the time goes in v4:
time: 63.6 us; the launch traced here: 63.7 us
  starting transfers between devices  37.5 us (59%)
  waiting for transfers between devices  15.6 us (25%)
  Pallas kernels  5.86 us (9%)
  local copies, waits for them, and re-layouts  3.25 us (5%)
  between operations  1.4 us (2%)
    ppermute x6, starting transfers between devices, along_y(): lax.ppermute(x, 'col', [(i, i // runs * runs + (i + s) % runs) for i in r...  11.3 us
    ppermute x3, starting transfers between devices, along_x(): lax.ppermute(x, 'row', [(i, (i + 4 * s) % row_devs) for i in range(row_de...  5.96 us
    ppermute x3, starting transfers between devices, per_device(): lax.ppermute(pair, 'col', [(i, i // runs * runs + (i + s) % runs) for i i...  4.61 us
    all_to_all x1, starting transfers between devices, per_device(): lax.all_to_all(spread, 'row', 0, 0, axis_index_groups=same_line, tiled=True)  4.29 us
    ppermute x1, starting transfers between devices, per_device(): lax.ppermute(vectors, 'row', [(i, i ^ 2) for i in range(row_devs)])  4.04 us
    all_to_all x1, waiting for transfers between devices, per_device(): lax.all_to_all(spread, 'row', 0, 0, axis_index_groups=same_line, tiled=True)  3.81 us
    ppermute x6, waiting for transfers between devices, along_y(): lax.ppermute(x, 'col', [(i, i // runs * runs + (i + s) % runs) for i in r...  3.38 us
    ppermute x1, waiting for transfers between devices, per_device(): lax.ppermute(tile, ('row', 'col'), [(r * col_devs + c, (r ^ 2) * col_devs...  3.33 us
  transfers between devices with their start and end apart: 20, of which 6 were waited for; matrix products, arithmetic and copies ran while one was open for 0% of the time, Pallas kernels for 1%

profile of v4, /device:TPU:0, one launch (start us, length us, event | category | flops | bytes accessed | tf_op | source)
XLA Modules:
  0.0 63.7 jit_solution(17684693542027323383)
XLA Ops:
  0.6 4.0 %collective-permute-start.1 = (bf16[16,2048]{1,0:T(8,128)(2,1)}, bf16[16,2048]{1,0:T(8,128)(2,1)S(1)}, u32[]{:S(2)}, u32[]{:S(2)}) collective-permute-start(bf16[16,2048]{1,0:T(8,128)(2,1)} %x_ref.7), channel_id=1, source_target_pairs={{0,16},{8,24},{16,0},{24,8},{32,48},{40,56},{48,32},{56,40},{64,80... | collective-permute-start | bytes 196616 | tf_op jit(solution)/shard_map/ppermute | solution.py:266
  4.7 1.0 %collective-permute-start = (bf16[16,2048]{1,0:T(8,128)(2,1)}, bf16[16,2048]{1,0:T(8,128)(2,1)S(1)}, u32[]{:S(2)}, u32[]{:S(2)}) collective-permute-start(bf16[16,2048]{1,0:T(8,128)(2,1)} %x_ref.7), channel_id=1, source_target_pairs={{0,4},{1,5},{2,6},{3,7},{4,0},{5,1},{6,2},{7,3},{8,12},{9,13},{10,... | collective-permute-start | bytes 196616 | tf_op jit(solution)/shard_map/ppermute | solution.py:265
  5.7 1.4 %collective-permute-done.1.h_ref = bf16[16,2048]{1,0:T(8,128)(2,1)S(1)} collective-permute-done((bf16[16,2048]{1,0:T(8,128)(2,1)}, bf16[16,2048]{1,0:T(8,128)(2,1)S(1)}, u32[]{:S(2)}, u32[]{:S(2)}) %collective-permute-start.1) | collective-permute-done | bytes 65568 | tf_op jit(solution)/shard_map/ppermute | solution.py:266
  7.1 2.0 %collective-permute-done.z_ref = bf16[16,2048]{1,0:T(8,128)(2,1)S(1)} collective-permute-done((bf16[16,2048]{1,0:T(8,128)(2,1)}, bf16[16,2048]{1,0:T(8,128)(2,1)S(1)}, u32[]{:S(2)}, u32[]{:S(2)}) %collective-permute-start) | collective-permute-done | bytes 65568 | tf_op jit(solution)/shard_map/ppermute | solution.py:265
  9.1 0.8 %copy-done.1 = bf16[16,2048]{1,0:T(8,128)(2,1)S(1)} copy-done((bf16[16,2048]{1,0:T(8,128)(2,1)S(1)}, bf16[16,2048]{1,0:T(8,128)(2,1)}, u32[]{:S(2)}) %copy-start.1) | copy-done | bytes 65560
  10.0 0.8 %shard_map.87 = (bf16[2,16,2048]{2,1,0:T(8,128)(2,1)S(1)}, bf16[4,2,16,2048]{3,2,1,0:T(8,128)(2,1)}) custom-call(bf16[16,2048]{1,0:T(8,128)(2,1)S(1)} %copy-done.1, bf16[16,2048]{1,0:T(8,128)(2,1)S(1)} %collective-permute-done.z_ref, bf16[16,2048]{1,0:T(8,128)(2,1)S(1)} %collective-permute-done.1.h_ref), custom_call_target="tpu_custom_call" | custom-call | tf_op jit(solution)/shard_map/pallas_call | solution.py:268
  10.8 4.3 %all-to-all-start = ((bf16[4,2,16,2048]{3,2,1,0:T(8,128)(2,1)}), bf16[4,2,16,2048]{3,2,1,0:T(8,128)(2,1)S(1)}, u32[]{:S(2)}, u32[]{:S(2)}) async-start(bf16[4,2,16,2048]{3,2,1,0:T(8,128)(2,1)} %get-tuple-element.25), calls=%async_computation | async-start | bytes 1048576 | tf_op jit(solution)/shard_map/all_to_all | solution.py:280
  15.1 3.0 %collective-permute-start.4 = (bf16[2,16,2048]{2,1,0:T(8,128)(2,1)S(1)}, bf16[2,16,2048]{2,1,0:T(8,128)(2,1)S(1)}, u32[]{:S(2)}, u32[]{:S(2)}) collective-permute-start(bf16[2,16,2048]{2,1,0:T(8,128)(2,1)S(1)} %get-tuple-element.24), channel_id=1, source_target_pairs={{0,3},{1,0},{2,1},{3,2},{4,7},{5,4},{6,5},{7,6},{8,11},{9,8},{10,9... | collective-permute-start | bytes 393224 | tf_op jit(solution)/shard_map/ppermute | solution.py:283
  18.1 0.6 collective-permute-start.3
  18.8 1.0 %collective-permute-start.2 = (bf16[2,16,2048]{2,1,0:T(8,128)(2,1)S(1)}, bf16[2,16,2048]{2,1,0:T(8,128)(2,1)S(1)}, u32[]{:S(2)}, u32[]{:S(2)}) collective-permute-start(bf16[2,16,2048]{2,1,0:T(8,128)(2,1)S(1)} %get-tuple-element.24), channel_id=1, source_target_pairs={{0,1},{1,2},{2,3},{3,0},{4,5},{5,6},{6,7},{7,4},{8,9},{9,10},{10,1... | collective-permute-start | bytes 393224 | tf_op jit(solution)/shard_map/ppermute | solution.py:283
  19.7 3.8 %all-to-all-done.refs_3_.xcol_ref = bf16[4,2,16,2048]{3,2,1,0:T(8,128)(2,1)S(1)} async-done(((bf16[4,2,16,2048]{3,2,1,0:T(8,128)(2,1)}), bf16[4,2,16,2048]{3,2,1,0:T(8,128)(2,1)S(1)}, u32[]{:S(2)}, u32[]{:S(2)}) %all-to-all-start) | async-done | bytes 524320 | tf_op jit(solution)/shard_map/all_to_all | solution.py:280
  24.2 0.8 %copy-done.2 = bf16[16,2048]{1,0:T(8,128)(2,1)S(1)} copy-done((bf16[16,2048]{1,0:T(8,128)(2,1)S(1)}, bf16[16,2048]{1,0:T(8,128)(2,1)}, u32[]{:S(2)}) %copy-start.2) | copy-done | bytes 65560
  25.0 1.0 %copy-done.6 = bf16[16,128,128]{2,1,0:T(8,128)(2,1)S(1)} copy-done((bf16[16,128,128]{2,1,0:T(8,128)(2,1)S(1)}, bf16[16,128,128]{2,1,0:T(8,128)(2,1)}, u32[]{:S(2)}) %copy-start.6) | copy-done | bytes 524312
  26.1 0.5 shard_map.86
  26.8 0.5 copy-done.4
  27.3 2.8 %shard_map.89 = (bf16[2,16,2048]{2,1,0:T(8,128)(2,1)S(1)}, bf16[2,16,2048]{2,1,0:T(8,128)(2,1)S(1)}, bf16[2,16,2048]{2,1,0:T(8,128)(2,1)S(1)}, f32[2,16,2048]{2,...) custom-call(s32[1,1]{1,0:T(1,128)S(6)} %copy.9.count_ref, s32[192]{0:T(256)S(1)} %bitcast.3, ...), custom_call_target="tpu_custom_call" | custom-call | tf_op jit(solution)/shard_map/pallas_call | solution.py:321
  30.1 0.9 %collective-permute-start.6 = (bf16[9,16,2048]{2,1,0:T(8,128)(2,1)S(1)}, bf16[9,16,2048]{2,1,0:T(8,128)(2,1)S(1)}, u32[]{:S(2)}, u32[]{:S(2)}) collective-permute-start(bf16[9,16,2048]{2,1,0:T(8,128)(2,1)S(1)} %get-tuple-element.27.own_ref), channel_id=1, source_target_pairs={{0,8},{8,0},{16,24},{24,16},{32,40},{40,32},{48,56},{56,48},{64,72... | collective-permute-start | bytes 1769480 | tf_op jit(solution)/shard_map/ppermute | solution.py:338
  31.1 1.6 %collective-permute-done.6.got_ref = bf16[9,16,2048]{2,1,0:T(8,128)(2,1)S(1)} collective-permute-done((bf16[9,16,2048]{2,1,0:T(8,128)(2,1)S(1)}, bf16[9,16,2048]{2,1,0:T(8,128)(2,1)S(1)}, u32[]{:S(2)}, u32[]{:S(2)}) %collective-permute-start.6) | collective-permute-done | bytes 589856 | tf_op jit(solution)/shard_map/ppermute | solution.py:338
  32.8 0.8 %collective-permute-start.7 = (bf16[2,16,2176]{2,1,0:T(8,128)(2,1)S(1)}, bf16[2,16,2176]{2,1,0:T(8,128)(2,1)S(1)}, u32[]{:S(2)}, u32[]{:S(2)}) collective-permute-start(bf16[2,16,2176]{2,1,0:T(8,128)(2,1)S(1)} %get-tuple-element.31), channel_id=1, source_target_pairs={{0,32},{8,40},{16,48},{24,56},{32,64},{40,72},{48,80},{56,88},{64,... | collective-permute-start | bytes 417800 | tf_op jit(solution)/shard_map/ppermute | solution.py:310
  33.7 3.7 %collective-permute-start.8 = (bf16[2,16,2176]{2,1,0:T(8,128)(2,1)S(1)}, bf16[2,16,2176]{2,1,0:T(8,128)(2,1)S(1)}, u32[]{:S(2)}, u32[]{:S(2)}) collective-permute-start(bf16[2,16,2176]{2,1,0:T(8,128)(2,1)S(1)} %get-tuple-element.32), channel_id=1, source_target_pairs={{0,64},{8,72},{16,80},{24,88},{32,96},{40,104},{48,112},{56,120},{... | collective-permute-start | bytes 417800 | tf_op jit(solution)/shard_map/ppermute | solution.py:310
  37.3 1.5 %collective-permute-start.9 = (bf16[2,16,2176]{2,1,0:T(8,128)(2,1)S(1)}, bf16[2,16,2176]{2,1,0:T(8,128)(2,1)S(1)}, u32[]{:S(2)}, u32[]{:S(2)}) collective-permute-start(bf16[2,16,2176]{2,1,0:T(8,128)(2,1)S(1)} %get-tuple-element.33), channel_id=1, source_target_pairs={{0,96},{8,104},{16,112},{24,120},{32,0},{40,8},{48,16},{56,24},{64... | collective-permute-start | bytes 417800 | tf_op jit(solution)/shard_map/ppermute | solution.py:310
  38.8 1.9 %collective-permute-start.10 = (bf16[2,16,2048]{2,1,0:T(8,128)(2,1)S(1)}, bf16[2,16,2048]{2,1,0:T(8,128)(2,1)S(1)}, u32[]{:S(2)}, u32[]{:S(2)}) collective-permute-start(bf16[2,16,2048]{2,1,0:T(8,128)(2,1)S(1)} %get-tuple-element.34), channel_id=1, source_target_pairs={{0,1},{1,2},{2,3},{3,0},{4,5},{5,6},{6,7},{7,4},{8,9},{9,10},{10,1... | collective-permute-start | bytes 393224 | tf_op jit(solution)/shard_map/ppermute | solution.py:307
  40.7 2.4 %collective-permute-start.11 = (bf16[2,16,2048]{2,1,0:T(8,128)(2,1)S(1)}, bf16[2,16,2048]{2,1,0:T(8,128)(2,1)S(1)}, u32[]{:S(2)}, u32[]{:S(2)}) collective-permute-start(bf16[2,16,2048]{2,1,0:T(8,128)(2,1)S(1)} %get-tuple-element.35), channel_id=1, source_target_pairs={{0,2},{1,3},{2,0},{3,1},{4,6},{5,7},{6,4},{7,5},{8,10},{9,11},{10,... | collective-permute-start | bytes 393224 | tf_op jit(solution)/shard_map/ppermute | solution.py:307
  43.1 1.3 %collective-permute-start.12 = (bf16[2,16,2048]{2,1,0:T(8,128)(2,1)S(1)}, bf16[2,16,2048]{2,1,0:T(8,128)(2,1)S(1)}, u32[]{:S(2)}, u32[]{:S(2)}) collective-permute-start(bf16[2,16,2048]{2,1,0:T(8,128)(2,1)S(1)} %get-tuple-element.36), channel_id=1, source_target_pairs={{0,3},{1,0},{2,1},{3,2},{4,7},{5,4},{6,5},{7,6},{8,11},{9,8},{10,9... | collective-permute-start | bytes 393224 | tf_op jit(solution)/shard_map/ppermute | solution.py:307
  44.6 4.1 %collective-permute-start.15 = (bf16[16,128]{1,0:T(8,128)(2,1)S(1)}, bf16[16,128]{1,0:T(8,128)(2,1)S(1)}, u32[]{:S(2)}, u32[]{:S(2)}) collective-permute-start(bf16[16,128]{1,0:T(8,128)(2,1)S(1)} %shard_map.92.refs_0_), channel_id=1, source_target_pairs={{0,3},{1,0},{2,1},{3,2},{4,7},{5,4},{6,5},{7,6},{8,11},{9,8},{10,9... | collective-permute-start | bytes 12296 | tf_op jit(solution)/shard_map/ppermute | solution.py:307
  48.9 1.3 %collective-permute-start.13 = (bf16[16,128]{1,0:T(8,128)(2,1)S(1)}, bf16[16,128]{1,0:T(8,128)(2,1)S(1)}, u32[]{:S(2)}, u32[]{:S(2)}) collective-permute-start(bf16[16,128]{1,0:T(8,128)(2,1)S(1)} %shard_map.92.refs_0_), channel_id=1, source_target_pairs={{0,1},{1,2},{2,3},{3,0},{4,5},{5,6},{6,7},{7,4},{8,9},{9,10},{10,1... | collective-permute-start | bytes 12296 | tf_op jit(solution)/shard_map/ppermute | solution.py:307
  50.4 3.4 %collective-permute-done.14.refs_2_ = bf16[16,128]{1,0:T(8,128)(2,1)S(1)} collective-permute-done((bf16[16,128]{1,0:T(8,128)(2,1)S(1)}, bf16[16,128]{1,0:T(8,128)(2,1)S(1)}, u32[]{:S(2)}, u32[]{:S(2)}) %collective-permute-start.14) | collective-permute-done | bytes 4128 | tf_op jit(solution)/shard_map/ppermute | solution.py:307
  53.9 2.8 %collective-permute-start.16 = (bf16[16,2176]{1,0:T(8,128)(2,1)S(1)}, bf16[16,2176]{1,0:T(8,128)(2,1)S(1)}, u32[]{:S(2)}, u32[]{:S(2)}) collective-permute-start(bf16[16,2176]{1,0:T(8,128)(2,1)S(1)} %get-tuple-element.41), channel_id=1, source_target_pairs={{0,16},{8,24},{16,0},{24,8},{32,48},{40,56},{48,32},{56,40},{64,80... | collective-permute-start | bytes 208904 | tf_op jit(solution)/shard_map/ppermute | solution.py:358
  56.7 1.1 %collective-permute-start.17 = (bf16[16,2176]{1,0:T(8,128)(2,1)S(1)}, bf16[16,2176]{1,0:T(8,128)(2,1)S(1)}, u32[]{:S(2)}, u32[]{:S(2)}) collective-permute-start(bf16[16,2176]{1,0:T(8,128)(2,1)S(1)} %get-tuple-element.42), channel_id=1, source_target_pairs={{0,4},{1,5},{2,6},{3,7},{4,0},{5,1},{6,2},{7,3},{8,12},{9,13},{10,... | collective-permute-start | bytes 208904 | tf_op jit(solution)/shard_map/ppermute | solution.py:359
  57.8 1.5 %collective-permute-start.18 = (bf16[16,128]{1,0:T(8,128)(2,1)S(1)}, bf16[16,128]{1,0:T(8,128)(2,1)S(1)}, u32[]{:S(2)}, u32[]{:S(2)}) collective-permute-start(bf16[16,128]{1,0:T(8,128)(2,1)S(1)} %get-tuple-element.43.tile_ref), channel_id=1, source_target_pairs={{0,20},{1,21},{2,22},{3,23},{4,16},{5,17},{6,18},{7,19},{8,28},{9,... | collective-permute-start | bytes 12296 | tf_op jit(solution)/shard_map/ppermute | solution.py:360
  59.2 3.3 %collective-permute-done.18.across_ref = bf16[16,128]{1,0:T(8,128)(2,1)S(1)} collective-permute-done((bf16[16,128]{1,0:T(8,128)(2,1)S(1)}, bf16[16,128]{1,0:T(8,128)(2,1)S(1)}, u32[]{:S(2)}, u32[]{:S(2)}) %collective-permute-start.18) | collective-permute-done | bytes 4128 | tf_op jit(solution)/shard_map/ppermute | solution.py:360
  62.6 1.1 %shard_map.94 = (f32[16,2048]{1,0:T(8,128)}, bf16[16,2048]{1,0:T(8,128)(2,1)}) custom-call(f32[16,2048]{1,0:T(8,128)S(1)} %get-tuple-element.37.own_ref, bf16[16,2176]{1,0:T(8,128)(2,1)S(1)} %collective-permute-done.16.col_ref, bf16[16,2176]{1,0:T(8,128)(2,1)S(1)} %collective-permute-done.17.row_ref, bf16[16,128]{1,0:T(8,128)(2,1)S(1)} %get-tuple-element.43.tile_ref, ...), custom_call_target="tpu_custom_call" | custom-call | tf_op jit(solution)/shard_map/pallas_call | solution.py:364
  (31 shorter events, 0.9 us)
Async XLA Ops:
  0.6 6.5 %collective-permute-start.1 = (bf16[16,2048]{1,0:T(8,128)(2,1)}, bf16[16,2048]{1,0:T(8,128)(2,1)S(1)}, u32[]{:S(2)}, u32[]{:S(2)}) collective-permute-start(bf16[16,2048]{1,0:T(8,128)(2,1)} %x_ref.7), channel_id=1, source_target_pairs={{0,16},{8,24},{16,0},{24,8},{32,48},{40,56},{48,32},{56,40},{64,80... | collective-permute-start | bytes 196616 | tf_op jit(solution)/shard_map/ppermute | solution.py:266
  4.7 4.5 %collective-permute-start = (bf16[16,2048]{1,0:T(8,128)(2,1)}, bf16[16,2048]{1,0:T(8,128)(2,1)S(1)}, u32[]{:S(2)}, u32[]{:S(2)}) collective-permute-start(bf16[16,2048]{1,0:T(8,128)(2,1)} %x_ref.7), channel_id=1, source_target_pairs={{0,4},{1,5},{2,6},{3,7},{4,0},{5,1},{6,2},{7,3},{8,12},{9,13},{10,... | collective-permute-start | bytes 196616 | tf_op jit(solution)/shard_map/ppermute | solution.py:265
  9.1 0.8 %copy-start.1 = (bf16[16,2048]{1,0:T(8,128)(2,1)S(1)}, bf16[16,2048]{1,0:T(8,128)(2,1)}, u32[]{:S(2)}) copy-start(bf16[16,2048]{1,0:T(8,128)(2,1)} %x_ref.7) | copy-start | bytes 196612
  10.8 12.7 %all-to-all-start = ((bf16[4,2,16,2048]{3,2,1,0:T(8,128)(2,1)}), bf16[4,2,16,2048]{3,2,1,0:T(8,128)(2,1)S(1)}, u32[]{:S(2)}, u32[]{:S(2)}) async-start(bf16[4,2,16,2048]{3,2,1,0:T(8,128)(2,1)} %get-tuple-element.25), calls=%async_computation | async-start | bytes 1048576 | tf_op jit(solution)/shard_map/all_to_all | solution.py:280
  15.1 11.5 %collective-permute-start.4 = (bf16[2,16,2048]{2,1,0:T(8,128)(2,1)S(1)}, bf16[2,16,2048]{2,1,0:T(8,128)(2,1)S(1)}, u32[]{:S(2)}, u32[]{:S(2)}) collective-permute-start(bf16[2,16,2048]{2,1,0:T(8,128)(2,1)S(1)} %get-tuple-element.24), channel_id=1, source_target_pairs={{0,3},{1,0},{2,1},{3,2},{4,7},{5,4},{6,5},{7,6},{8,11},{9,8},{10,9... | collective-permute-start | bytes 393224 | tf_op jit(solution)/shard_map/ppermute | solution.py:283
  18.1 8.5 %collective-permute-start.3 = (bf16[2,16,2048]{2,1,0:T(8,128)(2,1)S(1)}, bf16[2,16,2048]{2,1,0:T(8,128)(2,1)S(1)}, u32[]{:S(2)}, u32[]{:S(2)}) collective-permute-start(bf16[2,16,2048]{2,1,0:T(8,128)(2,1)S(1)} %get-tuple-element.24), channel_id=1, source_target_pairs={{0,2},{1,3},{2,0},{3,1},{4,6},{5,7},{6,4},{7,5},{8,10},{9,11},{10,... | collective-permute-start | bytes 393224 | tf_op jit(solution)/shard_map/ppermute | solution.py:283
  18.8 7.9 %collective-permute-start.2 = (bf16[2,16,2048]{2,1,0:T(8,128)(2,1)S(1)}, bf16[2,16,2048]{2,1,0:T(8,128)(2,1)S(1)}, u32[]{:S(2)}, u32[]{:S(2)}) collective-permute-start(bf16[2,16,2048]{2,1,0:T(8,128)(2,1)S(1)} %get-tuple-element.24), channel_id=1, source_target_pairs={{0,1},{1,2},{2,3},{3,0},{4,5},{5,6},{6,7},{7,4},{8,9},{9,10},{10,1... | collective-permute-start | bytes 393224 | tf_op jit(solution)/shard_map/ppermute | solution.py:283
  23.5 3.3 %collective-permute-start.5 = (bf16[4,2,16,2048]{3,2,1,0:T(8,128)(2,1)S(1)}, bf16[4,2,16,2048]{3,2,1,0:T(8,128)(2,1)S(1)}, u32[]{:S(2)}, u32[]{:S(2)}) collective-permute-start(bf16[4,2,16,2048]{3,2,1,0:T(8,128)(2,1)S(1)} %all-to-all-done.refs_3_.xcol_ref), channel_id=1, source_target_pairs={{0,8},{8,0},{16,24},{24,16},{32,40},{40,32},{48,56},{56,48},{64,72... | collective-permute-start | bytes 1572872 | tf_op jit(solution)/shard_map/ppermute | solution.py:281
  24.2 0.8 %copy-start.2 = (bf16[16,2048]{1,0:T(8,128)(2,1)S(1)}, bf16[16,2048]{1,0:T(8,128)(2,1)}, u32[]{:S(2)}) copy-start(bf16[16,2048]{1,0:T(8,128)(2,1)} %x_ref.7) | copy-start | bytes 196612
  25.0 1.0 %copy-start.6 = (bf16[16,128,128]{2,1,0:T(8,128)(2,1)S(1)}, bf16[16,128,128]{2,1,0:T(8,128)(2,1)}, u32[]{:S(2)}) copy-start(bf16[16,128,128]{2,1,0:T(8,128)(2,1)} %diag_ref.1) | copy-start | bytes 1572868
  26.6 0.7 %copy-start.4 = (s32[1,1,192]{2,1,0:T(1,128)S(1)}, s32[1,1,192]{2,1,0:T(1,128)}, u32[]{:S(2)}) copy-start(s32[1,1,192]{2,1,0:T(1,128)} %param.9) | copy-start | bytes 2308
  26.6 0.7 %copy-start.5 = (s32[1,1,192]{2,1,0:T(1,128)S(1)}, s32[1,1,192]{2,1,0:T(1,128)}, u32[]{:S(2)}) copy-start(s32[1,1,192]{2,1,0:T(1,128)} %param.10) | copy-start | bytes 2308
  26.8 35.8 %copy-start = (bf16[16,128,128]{2,1,0:T(8,128)(2,1)S(1)}, bf16[16,128,128]{2,1,0:T(8,128)(2,1)}, u32[]{:S(2)}) copy-start(bf16[16,128,128]{2,1,0:T(8,128)(2,1)} %pre_ref.1) | copy-start | bytes 1572868
  26.8 35.8 %copy-start.3 = (bf16[16,2048]{1,0:T(8,128)(2,1)S(1)}, bf16[16,2048]{1,0:T(8,128)(2,1)}, u32[]{:S(2)}) copy-start(bf16[16,2048]{1,0:T(8,128)(2,1)} %x_ref.7) | copy-start | bytes 196612
  30.1 2.6 %collective-permute-start.6 = (bf16[9,16,2048]{2,1,0:T(8,128)(2,1)S(1)}, bf16[9,16,2048]{2,1,0:T(8,128)(2,1)S(1)}, u32[]{:S(2)}, u32[]{:S(2)}) collective-permute-start(bf16[9,16,2048]{2,1,0:T(8,128)(2,1)S(1)} %get-tuple-element.27.own_ref), channel_id=1, source_target_pairs={{0,8},{8,0},{16,24},{24,16},{32,40},{40,32},{48,56},{56,48},{64,72... | collective-permute-start | bytes 1769480 | tf_op jit(solution)/shard_map/ppermute | solution.py:338
  32.8 10.3 %collective-permute-start.7 = (bf16[2,16,2176]{2,1,0:T(8,128)(2,1)S(1)}, bf16[2,16,2176]{2,1,0:T(8,128)(2,1)S(1)}, u32[]{:S(2)}, u32[]{:S(2)}) collective-permute-start(bf16[2,16,2176]{2,1,0:T(8,128)(2,1)S(1)} %get-tuple-element.31), channel_id=1, source_target_pairs={{0,32},{8,40},{16,48},{24,56},{32,64},{40,72},{48,80},{56,88},{64,... | collective-permute-start | bytes 417800 | tf_op jit(solution)/shard_map/ppermute | solution.py:310
  33.7 10.8 %collective-permute-start.8 = (bf16[2,16,2176]{2,1,0:T(8,128)(2,1)S(1)}, bf16[2,16,2176]{2,1,0:T(8,128)(2,1)S(1)}, u32[]{:S(2)}, u32[]{:S(2)}) collective-permute-start(bf16[2,16,2176]{2,1,0:T(8,128)(2,1)S(1)} %get-tuple-element.32), channel_id=1, source_target_pairs={{0,64},{8,72},{16,80},{24,88},{32,96},{40,104},{48,112},{56,120},{... | collective-permute-start | bytes 417800 | tf_op jit(solution)/shard_map/ppermute | solution.py:310
  37.3 7.1 %collective-permute-start.9 = (bf16[2,16,2176]{2,1,0:T(8,128)(2,1)S(1)}, bf16[2,16,2176]{2,1,0:T(8,128)(2,1)S(1)}, u32[]{:S(2)}, u32[]{:S(2)}) collective-permute-start(bf16[2,16,2176]{2,1,0:T(8,128)(2,1)S(1)} %get-tuple-element.33), channel_id=1, source_target_pairs={{0,96},{8,104},{16,112},{24,120},{32,0},{40,8},{48,16},{56,24},{64... | collective-permute-start | bytes 417800 | tf_op jit(solution)/shard_map/ppermute | solution.py:310
  38.8 10.1 %collective-permute-start.10 = (bf16[2,16,2048]{2,1,0:T(8,128)(2,1)S(1)}, bf16[2,16,2048]{2,1,0:T(8,128)(2,1)S(1)}, u32[]{:S(2)}, u32[]{:S(2)}) collective-permute-start(bf16[2,16,2048]{2,1,0:T(8,128)(2,1)S(1)} %get-tuple-element.34), channel_id=1, source_target_pairs={{0,1},{1,2},{2,3},{3,0},{4,5},{5,6},{6,7},{7,4},{8,9},{9,10},{10,1... | collective-permute-start | bytes 393224 | tf_op jit(solution)/shard_map/ppermute | solution.py:307
  40.7 9.5 %collective-permute-start.11 = (bf16[2,16,2048]{2,1,0:T(8,128)(2,1)S(1)}, bf16[2,16,2048]{2,1,0:T(8,128)(2,1)S(1)}, u32[]{:S(2)}, u32[]{:S(2)}) collective-permute-start(bf16[2,16,2048]{2,1,0:T(8,128)(2,1)S(1)} %get-tuple-element.35), channel_id=1, source_target_pairs={{0,2},{1,3},{2,0},{3,1},{4,6},{5,7},{6,4},{7,5},{8,10},{9,11},{10,... | collective-permute-start | bytes 393224 | tf_op jit(solution)/shard_map/ppermute | solution.py:307
  43.1 7.1 %collective-permute-start.12 = (bf16[2,16,2048]{2,1,0:T(8,128)(2,1)S(1)}, bf16[2,16,2048]{2,1,0:T(8,128)(2,1)S(1)}, u32[]{:S(2)}, u32[]{:S(2)}) collective-permute-start(bf16[2,16,2048]{2,1,0:T(8,128)(2,1)S(1)} %get-tuple-element.36), channel_id=1, source_target_pairs={{0,3},{1,0},{2,1},{3,2},{4,7},{5,4},{6,5},{7,6},{8,11},{9,8},{10,9... | collective-permute-start | bytes 393224 | tf_op jit(solution)/shard_map/ppermute | solution.py:307
  44.6 5.8 %collective-permute-start.15 = (bf16[16,128]{1,0:T(8,128)(2,1)S(1)}, bf16[16,128]{1,0:T(8,128)(2,1)S(1)}, u32[]{:S(2)}, u32[]{:S(2)}) collective-permute-start(bf16[16,128]{1,0:T(8,128)(2,1)S(1)} %shard_map.92.refs_0_), channel_id=1, source_target_pairs={{0,3},{1,0},{2,1},{3,2},{4,7},{5,4},{6,5},{7,6},{8,11},{9,8},{10,9... | collective-permute-start | bytes 12296 | tf_op jit(solution)/shard_map/ppermute | solution.py:307
  48.7 5.1 %collective-permute-start.14 = (bf16[16,128]{1,0:T(8,128)(2,1)S(1)}, bf16[16,128]{1,0:T(8,128)(2,1)S(1)}, u32[]{:S(2)}, u32[]{:S(2)}) collective-permute-start(bf16[16,128]{1,0:T(8,128)(2,1)S(1)} %shard_map.92.refs_0_), channel_id=1, source_target_pairs={{0,2},{1,3},{2,0},{3,1},{4,6},{5,7},{6,4},{7,5},{8,10},{9,11},{10,... | collective-permute-start | bytes 12296 | tf_op jit(solution)/shard_map/ppermute | solution.py:307
  48.9 4.9 %collective-permute-start.13 = (bf16[16,128]{1,0:T(8,128)(2,1)S(1)}, bf16[16,128]{1,0:T(8,128)(2,1)S(1)}, u32[]{:S(2)}, u32[]{:S(2)}) collective-permute-start(bf16[16,128]{1,0:T(8,128)(2,1)S(1)} %shard_map.92.refs_0_), channel_id=1, source_target_pairs={{0,1},{1,2},{2,3},{3,0},{4,5},{5,6},{6,7},{7,4},{8,9},{9,10},{10,1... | collective-permute-start | bytes 12296 | tf_op jit(solution)/shard_map/ppermute | solution.py:307
  53.9 8.7 %collective-permute-start.16 = (bf16[16,2176]{1,0:T(8,128)(2,1)S(1)}, bf16[16,2176]{1,0:T(8,128)(2,1)S(1)}, u32[]{:S(2)}, u32[]{:S(2)}) collective-permute-start(bf16[16,2176]{1,0:T(8,128)(2,1)S(1)} %get-tuple-element.41), channel_id=1, source_target_pairs={{0,16},{8,24},{16,0},{24,8},{32,48},{40,56},{48,32},{56,40},{64,80... | collective-permute-start | bytes 208904 | tf_op jit(solution)/shard_map/ppermute | solution.py:358
  56.7 5.9 %collective-permute-start.17 = (bf16[16,2176]{1,0:T(8,128)(2,1)S(1)}, bf16[16,2176]{1,0:T(8,128)(2,1)S(1)}, u32[]{:S(2)}, u32[]{:S(2)}) collective-permute-start(bf16[16,2176]{1,0:T(8,128)(2,1)S(1)} %get-tuple-element.42), channel_id=1, source_target_pairs={{0,4},{1,5},{2,6},{3,7},{4,0},{5,1},{6,2},{7,3},{8,12},{9,13},{10,... | collective-permute-start | bytes 208904 | tf_op jit(solution)/shard_map/ppermute | solution.py:359
  57.8 4.8 %collective-permute-start.18 = (bf16[16,128]{1,0:T(8,128)(2,1)S(1)}, bf16[16,128]{1,0:T(8,128)(2,1)S(1)}, u32[]{:S(2)}, u32[]{:S(2)}) collective-permute-start(bf16[16,128]{1,0:T(8,128)(2,1)S(1)} %get-tuple-element.43.tile_ref), channel_id=1, source_target_pairs={{0,20},{1,21},{2,22},{3,23},{4,16},{5,17},{6,18},{7,19},{8,28},{9,... | collective-permute-start | bytes 12296 | tf_op jit(solution)/shard_map/ppermute | solution.py:360

commit v5 on v4

--- a/solution.py
+++ b/solution.py
@@ -53,7 +53,7 @@
     return out[:xa.shape[0]], out[xa.shape[0]:]
 
 
-def diag_kernel(x_ref, diag_ref, term_ref, stats_ref):
+def diag_kernel(x_ref, diag_ref, term_ref, stats_ref, near_ref):
     width, span = x_ref.shape
     xy = jnp.zeros((width, LANES), F32)
     xx = jnp.zeros((width, LANES), F32)
@@ -69,6 +69,7 @@
         xx = xx + xf * xf
     stats_ref[0] = xy
     stats_ref[1] = xx
+    near_ref[...] = x_ref[...]
 
 
 def rows_kernel(x_ref, z_ref, *refs):
@@ -87,9 +88,15 @@
                 x_row[dev * owned + t] = piece
 
 
-def block_kernel(count_ref, rows_ref, cols_ref, x_row, xcol_ref, twin_ref, stats_ref, stiff_ref, *refs):
-    (*ring_refs, row_keep, col_keep, core_out, x_col, acc_row, acc_col, buf, sems) = refs
+def block_kernel(count_ref, rows_hbm, cols_hbm, x_row, xcol_ref, twin_ref, stats_ref, stiff_ref, *refs):
+    (*ring_refs, row_keep, col_keep, core_out, x_col, acc_row, acc_col, buf, rows_ref, cols_ref, sems, index_sems) = refs
     count = count_ref[0, 0]
+    index_copies = [
+        pltpu.make_async_copy(rows_hbm, rows_ref, index_sems.at[0]),
+        pltpu.make_async_copy(cols_hbm, cols_ref, index_sems.at[1]),
+    ]
+    for copy in index_copies:
+        copy.start()
     copies = fetch(stiff_ref, buf, sems, count)
     width, span = xcol_ref.shape[2:]
     owned = span // LANES
@@ -104,6 +111,8 @@
                 dev = line * 4 + (high + k) % 2 * 2 + (core + twin) % 2
                 for t in range(owned):
                     x_col[dev * owned + t] = ref[line, k, :, t * LANES:(t + 1) * LANES]
+    for copy in index_copies:
+        copy.wait()
     for c, copy in enumerate(copies):
 
         @pl.when(c * CHUNK < count)
@@ -257,13 +266,37 @@
     runs = col_devs // 2
     wide = span + LANES
     count = block_count
-    rows = block_row.reshape(slots)
-    cols = block_col.reshape(slots)
-    block_scratch = [pltpu.VMEM((slots, block_len, block_len), BF16), pltpu.SemaphoreType.DMA((slots // CHUNK,))]
+    rows = pltpu.with_memory_space_constraint(block_row.reshape(slots), pltpu.HBM)
+    cols = pltpu.with_memory_space_constraint(block_col.reshape(slots), pltpu.HBM)
+    block_scratch = [
+        pltpu.VMEM((slots, block_len, block_len), BF16),
+        pltpu.SMEM((slots,), jnp.int32),
+        pltpu.SMEM((slots,), jnp.int32),
+        pltpu.SemaphoreType.DMA((slots // CHUNK,)),
+        pltpu.SemaphoreType.DMA((2,)),
+    ]
     blocks = pltpu.with_memory_space_constraint(stiffness.reshape(slots, block_len, block_len), pltpu.HBM)
 
     beside = near(lax.ppermute(vectors, "col", [(i, (i + runs) % col_devs) for i in range(col_devs)]))
+    across_z = [
+        (r * col_devs + c, (r ^ 2) * col_devs + (c + runs) % col_devs)
+        for r in range(row_devs)
+        for c in range(col_devs)
+    ]
     above = near(lax.ppermute(vectors, "row", [(i, i ^ 2) for i in range(row_devs)]))
+    diag_term, stats, own_x = pl.pallas_call(
+        diag_kernel,
+        out_shape=(
+            jax.ShapeDtypeStruct((width, span), F32),
+            jax.ShapeDtypeStruct((2, width, LANES), F32),
+            jax.ShapeDtypeStruct((width, span), BF16),
+        ),
+        in_specs=[VM, VM],
+        out_specs=(VM, VM, VM),
+        compiler_params=params(4),
+        cost_estimate=cost(1 << 30, 4 << 20),
+    )(vectors, diag_blocks)
+    diag_term, stats, own_x = near(diag_term), near(stats), near(own_x)
     lines = row_devs // 4
     pair, spread = pl.pallas_call(
         prepare_kernel,
@@ -274,7 +307,7 @@
         in_specs=[VM, VM, VM],
         out_specs=(VM, VM),
         compiler_params=params(4),
-    )(vectors, beside, above)
+    )(own_x, beside, above)
     pair = near(pair)
     same_line = [[x * 4 + k for x in range(lines)] for k in range(4)]
     xcol = lax.all_to_all(spread, "row", 0, 0, axis_index_groups=same_line, tiled=True)
@@ -283,15 +316,6 @@
         near(lax.ppermute(pair, "col", [(i, i // runs * runs + (i + s) % runs) for i in range(col_devs)]))
         for s in range(1, runs)
     ]
-    diag_term, stats = pl.pallas_call(
-        diag_kernel,
-        out_shape=(jax.ShapeDtypeStruct((width, span), F32), jax.ShapeDtypeStruct((2, width, LANES), F32)),
-        in_specs=[VM, VM],
-        out_specs=(VM, VM),
-        compiler_params=params(4),
-        cost_estimate=cost(1 << 28, 1 << 20),
-    )(vectors, diag_blocks)
-    diag_term, stats = near(diag_term), near(stats)
     x_row = near(pl.pallas_call(
         rows_kernel,
         out_shape=jax.ShapeDtypeStruct((col_devs * owned, width, LANES), BF16),
@@ -299,7 +323,7 @@
         out_specs=VM,
         compiler_params=params(4),
         cost_estimate=cost(4 << 30, 8 << 20),
-    )(vectors, beside, *turned, xcol))
+    )(own_x, beside, *turned, xcol))
     def shape(*dims, dtype=BF16):
         return jax.ShapeDtypeStruct(dims, dtype)
 
@@ -326,7 +350,7 @@
             shape(2 * lines, width, span, dtype=F32),
             shape(2 * lines + 1, width, span),
         ),
-        in_specs=[SM] * 3 + [VM] * 4 + [HBM],
+        in_specs=[SM, HBM, HBM] + [VM] * 4 + [HBM],
         out_specs=(VM,) * (runs + 2),
         scratch_shapes=[
             pltpu.VMEM((row_devs * owned, width, LANES), BF16),
@@ -357,17 +381,14 @@
     )
     got_col = near(lax.ppermute(col_out, "row", [(i, i ^ 2) for i in range(row_devs)]))
     got_row = near(lax.ppermute(row_out, "col", [(i, (i + runs) % col_devs) for i in range(col_devs)]))
-    across = near(lax.ppermute(
-        tile, ("row", "col"),
-        [(r * col_devs + c, (r ^ 2) * col_devs + (c + runs) % col_devs) for r in range(row_devs) for c in range(col_devs)],
-    ))
+    across = near(lax.ppermute(tile, ("row", "col"), across_z))
     return pl.pallas_call(
         final_kernel,
         out_shape=(shape(width, span, dtype=F32), shape(width, span)),
         in_specs=[VM] * 7,
         out_specs=(VM, VM),
         compiler_params=params(4),
-    )(own, got_col, got_row, tile, across, vectors, precond)
+    )(own, got_col, got_row, tile, across, own_x, precond)
 
 
 def solution(mesh):

time: 63.6 us -> 60.8 us (0.956); the launches traced: 63.7 us -> 60.1 us
  starting transfers between devices: 37.5 us -> 34 us
  local copies, waits for them, and re-layouts: 3.25 us -> 1.89 us
  Pallas kernels: 5.86 us -> 6.69 us
    ppermute x6, starting transfers between devices: 11.3 us -> 7.27 us  [along_y(): lax.ppermute(x, 'col', [(i, i // runs * runs + (i + s) % runs) for i in r...]
    ppermute x6, waiting for transfers between devices: 3.38 us -> 6.01 us  [along_y(): lax.ppermute(x, 'col', [(i, i // runs * runs + (i + s) % runs) for i in r...]
    ppermute x3, waiting for transfers between devices: 0.01 us -> 1.86 us  [per_device(): lax.ppermute(pair, 'col', [(i, i // runs * runs + (i + s) % runs) for i i...]
    ppermute x1, starting transfers between devices: 2.81 us -> 1.11 us  [per_device(): lax.ppermute(col_out, 'row', [(i, i ^ 2) for i in range(row_devs)])]
    ppermute x1, starting transfers between devices: 1.49 us -> 3.04 us  [per_device(): across = near(lax.ppermute(tile, ('row', 'col'), across_z))]
    ppermute x1, waiting for transfers between devices: 3.33 us -> 1.78 us  [per_device(): across = near(lax.ppermute(tile, ('row', 'col'), across_z))]
    ppermute x1, waiting for transfers between devices: 1.44 us -> 0.01 us  [per_device(): lax.ppermute(vectors, 'row', [(i, i ^ 2) for i in range(row_devs)])]
    unnamed x14 -> x6, local copies, waits for them, and re-layouts: 3.25 us -> 1.89 us
  transfers between devices with their start and end apart: 20 -> 20, of which waited for: 6 -> 11; matrix products, arithmetic and copies ran while one was open for 0% -> 0% of each run, Pallas kernels for 1% -> 1%
where the time goes in v5:
time: 60.8 us; the launch traced here: 60.1 us
  starting transfers between devices  34 us (56%)
  waiting for transfers between devices  16.1 us (26%)
  Pallas kernels  6.69 us (11%)
  local copies, waits for them, and re-layouts  1.89 us (3%)
  between operations  1.36 us (2%)
    ppermute x6, starting transfers between devices, along_y(): lax.ppermute(x, 'col', [(i, i // runs * runs + (i + s) % runs) for i in r...  7.27 us
    ppermute x3, starting transfers between devices, along_x(): lax.ppermute(x, 'row', [(i, (i + 4 * s) % row_devs) for i in range(row_de...  7.21 us
    ppermute x6, waiting for transfers between devices, along_y(): lax.ppermute(x, 'col', [(i, i // runs * runs + (i + s) % runs) for i in r...  6.01 us
    ppermute x3, starting transfers between devices, per_device(): lax.ppermute(pair, 'col', [(i, i // runs * runs + (i + s) % runs) for i i...  4.61 us
    all_to_all x1, starting transfers between devices, per_device(): lax.all_to_all(spread, 'row', 0, 0, axis_index_groups=same_line, tiled=True)  4.29 us
    ppermute x1, starting transfers between devices, per_device(): lax.ppermute(vectors, 'row', [(i, i ^ 2) for i in range(row_devs)])  4.04 us
    all_to_all x1, waiting for transfers between devices, per_device(): lax.all_to_all(spread, 'row', 0, 0, axis_index_groups=same_line, tiled=True)  3.81 us
    pallas_call x1, Pallas kernels, per_device(): pl.pallas_call(block_kernel, out_shape=(*[shape(2, width, span)] * (runs...  3.67 us
  transfers between devices with their start and end apart: 20, of which 11 were waited for; matrix products, arithmetic and copies ran while one was open for 0% of the time, Pallas kernels for 1%

profile of v5, /device:TPU:0, one launch (start us, length us, event | category | flops | bytes accessed | tf_op | source)
XLA Modules:
  0.0 60.1 jit_solution(7356792496420744508)
XLA Ops:
  0.6 4.0 %collective-permute-start.1 = (bf16[16,2048]{1,0:T(8,128)(2,1)}, bf16[16,2048]{1,0:T(8,128)(2,1)S(1)}, u32[]{:S(2)}, u32[]{:S(2)}) collective-permute-start(bf16[16,2048]{1,0:T(8,128)(2,1)} %x_ref.1), channel_id=1, source_target_pairs={{0,16},{8,24},{16,0},{24,8},{32,48},{40,56},{48,32},{56,40},{64,80... | collective-permute-start | bytes 196616 | tf_op jit(solution)/shard_map/ppermute | solution.py:286
  4.7 1.0 %collective-permute-start = (bf16[16,2048]{1,0:T(8,128)(2,1)}, bf16[16,2048]{1,0:T(8,128)(2,1)S(1)}, u32[]{:S(2)}, u32[]{:S(2)}) collective-permute-start(bf16[16,2048]{1,0:T(8,128)(2,1)} %x_ref.1), channel_id=1, source_target_pairs={{0,4},{1,5},{2,6},{3,7},{4,0},{5,1},{6,2},{7,3},{8,12},{9,13},{10,... | collective-permute-start | bytes 196616 | tf_op jit(solution)/shard_map/ppermute | solution.py:280
  5.7 1.0 %copy-done.1 = bf16[16,128,128]{2,1,0:T(8,128)(2,1)S(1)} copy-done((bf16[16,128,128]{2,1,0:T(8,128)(2,1)S(1)}, bf16[16,128,128]{2,1,0:T(8,128)(2,1)}, u32[]{:S(2)}) %copy-start.1) | copy-done | bytes 524312
  6.7 0.8 %copy-done.2 = bf16[16,2048]{1,0:T(8,128)(2,1)S(1)} copy-done((bf16[16,2048]{1,0:T(8,128)(2,1)S(1)}, bf16[16,2048]{1,0:T(8,128)(2,1)}, u32[]{:S(2)}) %copy-start.2) | copy-done | bytes 65560
  7.6 0.5 shard_map.86
  8.1 1.0 %collective-permute-done.z_ref = bf16[16,2048]{1,0:T(8,128)(2,1)S(1)} collective-permute-done((bf16[16,2048]{1,0:T(8,128)(2,1)}, bf16[16,2048]{1,0:T(8,128)(2,1)S(1)}, u32[]{:S(2)}, u32[]{:S(2)}) %collective-permute-start) | collective-permute-done | bytes 65568 | tf_op jit(solution)/shard_map/ppermute | solution.py:280
  9.1 0.9 %shard_map.87 = (bf16[2,16,2048]{2,1,0:T(8,128)(2,1)S(1)}, bf16[4,2,16,2048]{3,2,1,0:T(8,128)(2,1)}) custom-call(bf16[16,2048]{1,0:T(8,128)(2,1)S(1)} %get-tuple-element.25.x_ref, bf16[16,2048]{1,0:T(8,128)(2,1)S(1)} %collective-permute-done.z_ref, bf16[16,2048]{1,0:T(8,128)(2,1)S(1)} %collective-permute-done.1.h_ref), custom_call_target="tpu_custom_call" | custom-call | tf_op jit(solution)/shard_map/pallas_call | solution.py:301
  10.0 4.3 %all-to-all-start = ((bf16[4,2,16,2048]{3,2,1,0:T(8,128)(2,1)}), bf16[4,2,16,2048]{3,2,1,0:T(8,128)(2,1)S(1)}, u32[]{:S(2)}, u32[]{:S(2)}) async-start(bf16[4,2,16,2048]{3,2,1,0:T(8,128)(2,1)} %get-tuple-element.27), calls=%async_computation | async-start | bytes 1048576 | tf_op jit(solution)/shard_map/all_to_all | solution.py:313
  14.3 3.0 %collective-permute-start.4 = (bf16[2,16,2048]{2,1,0:T(8,128)(2,1)S(1)}, bf16[2,16,2048]{2,1,0:T(8,128)(2,1)S(1)}, u32[]{:S(2)}, u32[]{:S(2)}) collective-permute-start(bf16[2,16,2048]{2,1,0:T(8,128)(2,1)S(1)} %get-tuple-element.26), channel_id=1, source_target_pairs={{0,3},{1,0},{2,1},{3,2},{4,7},{5,4},{6,5},{7,6},{8,11},{9,8},{10,9... | collective-permute-start | bytes 393224 | tf_op jit(solution)/shard_map/ppermute | solution.py:316
  17.3 0.6 %collective-permute-start.3 = (bf16[2,16,2048]{2,1,0:T(8,128)(2,1)S(1)}, bf16[2,16,2048]{2,1,0:T(8,128)(2,1)S(1)}, u32[]{:S(2)}, u32[]{:S(2)}) collective-permute-start(bf16[2,16,2048]{2,1,0:T(8,128)(2,1)S(1)} %get-tuple-element.26), channel_id=1, source_target_pairs={{0,2},{1,3},{2,0},{3,1},{4,6},{5,7},{6,4},{7,5},{8,10},{9,11},{10,... | collective-permute-start | bytes 393224 | tf_op jit(solution)/shard_map/ppermute | solution.py:316
  17.9 1.0 %collective-permute-start.2 = (bf16[2,16,2048]{2,1,0:T(8,128)(2,1)S(1)}, bf16[2,16,2048]{2,1,0:T(8,128)(2,1)S(1)}, u32[]{:S(2)}, u32[]{:S(2)}) collective-permute-start(bf16[2,16,2048]{2,1,0:T(8,128)(2,1)S(1)} %get-tuple-element.26), channel_id=1, source_target_pairs={{0,1},{1,2},{2,3},{3,0},{4,5},{5,6},{6,7},{7,4},{8,9},{9,10},{10,1... | collective-permute-start | bytes 393224 | tf_op jit(solution)/shard_map/ppermute | solution.py:316
  18.9 3.8 %all-to-all-done.refs_3_.xcol_ref = bf16[4,2,16,2048]{3,2,1,0:T(8,128)(2,1)S(1)} async-done(((bf16[4,2,16,2048]{3,2,1,0:T(8,128)(2,1)}), bf16[4,2,16,2048]{3,2,1,0:T(8,128)(2,1)S(1)}, u32[]{:S(2)}, u32[]{:S(2)}) %all-to-all-start) | async-done | bytes 524320 | tf_op jit(solution)/shard_map/all_to_all | solution.py:313
  23.4 0.6 collective-permute-done.3.refs_1_
  23.9 1.3 %collective-permute-done.2.refs_0_ = bf16[2,16,2048]{2,1,0:T(8,128)(2,1)S(1)} collective-permute-done((bf16[2,16,2048]{2,1,0:T(8,128)(2,1)S(1)}, bf16[2,16,2048]{2,1,0:T(8,128)(2,1)S(1)}, u32[]{:S(2)}, u32[]{:S(2)}) %collective-permute-start.2) | collective-permute-done | bytes 131104 | tf_op jit(solution)/shard_map/ppermute | solution.py:316
  25.4 3.7 %shard_map.89 = (bf16[2,16,2048]{2,1,0:T(8,128)(2,1)S(1)}, bf16[2,16,2048]{2,1,0:T(8,128)(2,1)S(1)}, bf16[2,16,2048]{2,1,0:T(8,128)(2,1)S(1)}, f32[2,16,2048]{2,...) custom-call(s32[1,1]{1,0:T(1,128)S(6)} %copy.9.count_ref, s32[192]{0:T(256)} %bitcast.4, ...), custom_call_target="tpu_custom_call" | custom-call | tf_op jit(solution)/shard_map/pallas_call | solution.py:345
  29.1 1.4 %collective-permute-start.6 = (bf16[9,16,2048]{2,1,0:T(8,128)(2,1)S(1)}, bf16[9,16,2048]{2,1,0:T(8,128)(2,1)S(1)}, u32[]{:S(2)}, u32[]{:S(2)}) collective-permute-start(bf16[9,16,2048]{2,1,0:T(8,128)(2,1)S(1)} %get-tuple-element.29.own_ref), channel_id=1, source_target_pairs={{0,8},{8,0},{16,24},{24,16},{32,40},{40,32},{48,56},{56,48},{64,72... | collective-permute-start | bytes 1769480 | tf_op jit(solution)/shard_map/ppermute | solution.py:362
  30.5 1.6 %collective-permute-done.6.got_ref = bf16[9,16,2048]{2,1,0:T(8,128)(2,1)S(1)} collective-permute-done((bf16[9,16,2048]{2,1,0:T(8,128)(2,1)S(1)}, bf16[9,16,2048]{2,1,0:T(8,128)(2,1)S(1)}, u32[]{:S(2)}, u32[]{:S(2)}) %collective-permute-start.6) | collective-permute-done | bytes 589856 | tf_op jit(solution)/shard_map/ppermute | solution.py:362
  32.2 3.1 %collective-permute-start.7 = (bf16[2,16,2176]{2,1,0:T(8,128)(2,1)S(1)}, bf16[2,16,2176]{2,1,0:T(8,128)(2,1)S(1)}, u32[]{:S(2)}, u32[]{:S(2)}) collective-permute-start(bf16[2,16,2176]{2,1,0:T(8,128)(2,1)S(1)} %get-tuple-element.33), channel_id=1, source_target_pairs={{0,32},{8,40},{16,48},{24,56},{32,64},{40,72},{48,80},{56,88},{64,... | collective-permute-start | bytes 417800 | tf_op jit(solution)/shard_map/ppermute | solution.py:334
  35.3 1.6 %collective-permute-start.8 = (bf16[2,16,2176]{2,1,0:T(8,128)(2,1)S(1)}, bf16[2,16,2176]{2,1,0:T(8,128)(2,1)S(1)}, u32[]{:S(2)}, u32[]{:S(2)}) collective-permute-start(bf16[2,16,2176]{2,1,0:T(8,128)(2,1)S(1)} %get-tuple-element.34), channel_id=1, source_target_pairs={{0,64},{8,72},{16,80},{24,88},{32,96},{40,104},{48,112},{56,120},{... | collective-permute-start | bytes 417800 | tf_op jit(solution)/shard_map/ppermute | solution.py:334
  36.9 2.5 %collective-permute-start.9 = (bf16[2,16,2176]{2,1,0:T(8,128)(2,1)S(1)}, bf16[2,16,2176]{2,1,0:T(8,128)(2,1)S(1)}, u32[]{:S(2)}, u32[]{:S(2)}) collective-permute-start(bf16[2,16,2176]{2,1,0:T(8,128)(2,1)S(1)} %get-tuple-element.35), channel_id=1, source_target_pairs={{0,96},{8,104},{16,112},{24,120},{32,0},{40,8},{48,16},{56,24},{64... | collective-permute-start | bytes 417800 | tf_op jit(solution)/shard_map/ppermute | solution.py:334
  39.4 0.6 collective-permute-start.11
  40.0 5.4 %collective-permute-start.12 = (bf16[2,16,2048]{2,1,0:T(8,128)(2,1)S(1)}, bf16[2,16,2048]{2,1,0:T(8,128)(2,1)S(1)}, u32[]{:S(2)}, u32[]{:S(2)}) collective-permute-start(bf16[2,16,2048]{2,1,0:T(8,128)(2,1)S(1)} %get-tuple-element.38), channel_id=1, source_target_pairs={{0,3},{1,0},{2,1},{3,2},{4,7},{5,4},{6,5},{7,6},{8,11},{9,8},{10,9... | collective-permute-start | bytes 393224 | tf_op jit(solution)/shard_map/ppermute | solution.py:331
  45.6 0.8 %collective-permute-start.15 = (bf16[16,128]{1,0:T(8,128)(2,1)S(1)}, bf16[16,128]{1,0:T(8,128)(2,1)S(1)}, u32[]{:S(2)}, u32[]{:S(2)}) collective-permute-start(bf16[16,128]{1,0:T(8,128)(2,1)S(1)} %shard_map.92.refs_0_), channel_id=1, source_target_pairs={{0,3},{1,0},{2,1},{3,2},{4,7},{5,4},{6,5},{7,6},{8,11},{9,8},{10,9... | collective-permute-start | bytes 12296 | tf_op jit(solution)/shard_map/ppermute | solution.py:331
  46.3 0.5 collective-permute-start.14
  46.8 1.3 %collective-permute-done.10.refs_3_ = bf16[2,16,2048]{2,1,0:T(8,128)(2,1)S(1)} collective-permute-done((bf16[2,16,2048]{2,1,0:T(8,128)(2,1)S(1)}, bf16[2,16,2048]{2,1,0:T(8,128)(2,1)S(1)}, u32[]{:S(2)}, u32[]{:S(2)}) %collective-permute-start.10) | collective-permute-done | bytes 131104 | tf_op jit(solution)/shard_map/ppermute | solution.py:331
  48.2 0.7 %collective-permute-done.12.refs_5_ = bf16[2,16,2048]{2,1,0:T(8,128)(2,1)S(1)} collective-permute-done((bf16[2,16,2048]{2,1,0:T(8,128)(2,1)S(1)}, bf16[2,16,2048]{2,1,0:T(8,128)(2,1)S(1)}, u32[]{:S(2)}, u32[]{:S(2)}) %collective-permute-start.12) | collective-permute-done | bytes 131104 | tf_op jit(solution)/shard_map/ppermute | solution.py:331
  49.2 2.2 %collective-permute-done.14.refs_2_ = bf16[16,128]{1,0:T(8,128)(2,1)S(1)} collective-permute-done((bf16[16,128]{1,0:T(8,128)(2,1)S(1)}, bf16[16,128]{1,0:T(8,128)(2,1)S(1)}, u32[]{:S(2)}, u32[]{:S(2)}) %collective-permute-start.14) | collective-permute-done | bytes 4128 | tf_op jit(solution)/shard_map/ppermute | solution.py:331
  51.4 1.5 %collective-permute-done.13.refs_1_ = bf16[16,128]{1,0:T(8,128)(2,1)S(1)} collective-permute-done((bf16[16,128]{1,0:T(8,128)(2,1)S(1)}, bf16[16,128]{1,0:T(8,128)(2,1)S(1)}, u32[]{:S(2)}, u32[]{:S(2)}) %collective-permute-start.13) | collective-permute-done | bytes 4128 | tf_op jit(solution)/shard_map/ppermute | solution.py:331
  53.1 1.1 %collective-permute-start.16 = (bf16[16,2176]{1,0:T(8,128)(2,1)S(1)}, bf16[16,2176]{1,0:T(8,128)(2,1)S(1)}, u32[]{:S(2)}, u32[]{:S(2)}) collective-permute-start(bf16[16,2176]{1,0:T(8,128)(2,1)S(1)} %get-tuple-element.43), channel_id=1, source_target_pairs={{0,16},{8,24},{16,0},{24,8},{32,48},{40,56},{48,32},{56,40},{64,80... | collective-permute-start | bytes 208904 | tf_op jit(solution)/shard_map/ppermute | solution.py:382
  54.2 3.0 %collective-permute-start.18 = (bf16[16,128]{1,0:T(8,128)(2,1)S(1)}, bf16[16,128]{1,0:T(8,128)(2,1)S(1)}, u32[]{:S(2)}, u32[]{:S(2)}) collective-permute-start(bf16[16,128]{1,0:T(8,128)(2,1)S(1)} %get-tuple-element.45.tile_ref), channel_id=1, source_target_pairs={{0,20},{1,21},{2,22},{3,23},{4,16},{5,17},{6,18},{7,19},{8,28},{9,... | collective-permute-start | bytes 12296 | tf_op jit(solution)/shard_map/ppermute | solution.py:384
  57.2 1.8 %collective-permute-done.18.across_ref = bf16[16,128]{1,0:T(8,128)(2,1)S(1)} collective-permute-done((bf16[16,128]{1,0:T(8,128)(2,1)S(1)}, bf16[16,128]{1,0:T(8,128)(2,1)S(1)}, u32[]{:S(2)}, u32[]{:S(2)}) %collective-permute-start.18) | collective-permute-done | bytes 4128 | tf_op jit(solution)/shard_map/ppermute | solution.py:384
  59.0 1.1 %shard_map.94 = (f32[16,2048]{1,0:T(8,128)}, bf16[16,2048]{1,0:T(8,128)(2,1)}) custom-call(f32[16,2048]{1,0:T(8,128)S(1)} %get-tuple-element.39.own_ref, bf16[16,2176]{1,0:T(8,128)(2,1)S(1)} %collective-permute-done.16.col_ref, bf16[16,2176]{1,0:T(8,128)(2,1)S(1)} %collective-permute-done.17.row_ref, bf16[16,128]{1,0:T(8,128)(2,1)S(1)} %get-tuple-element.45.tile_ref, ...), custom_call_target="tpu_custom_call" | custom-call | tf_op jit(solution)/shard_map/pallas_call | solution.py:385
  (23 shorter events, 0.8 us)
Async XLA Ops:
  0.6 7.5 %collective-permute-start.1 = (bf16[16,2048]{1,0:T(8,128)(2,1)}, bf16[16,2048]{1,0:T(8,128)(2,1)S(1)}, u32[]{:S(2)}, u32[]{:S(2)}) collective-permute-start(bf16[16,2048]{1,0:T(8,128)(2,1)} %x_ref.1), channel_id=1, source_target_pairs={{0,16},{8,24},{16,0},{24,8},{32,48},{40,56},{48,32},{56,40},{64,80... | collective-permute-start | bytes 196616 | tf_op jit(solution)/shard_map/ppermute | solution.py:286
  4.7 4.5 %collective-permute-start = (bf16[16,2048]{1,0:T(8,128)(2,1)}, bf16[16,2048]{1,0:T(8,128)(2,1)S(1)}, u32[]{:S(2)}, u32[]{:S(2)}) collective-permute-start(bf16[16,2048]{1,0:T(8,128)(2,1)} %x_ref.1), channel_id=1, source_target_pairs={{0,4},{1,5},{2,6},{3,7},{4,0},{5,1},{6,2},{7,3},{8,12},{9,13},{10,... | collective-permute-start | bytes 196616 | tf_op jit(solution)/shard_map/ppermute | solution.py:280
  5.7 1.0 %copy-start.1 = (bf16[16,128,128]{2,1,0:T(8,128)(2,1)S(1)}, bf16[16,128,128]{2,1,0:T(8,128)(2,1)}, u32[]{:S(2)}) copy-start(bf16[16,128,128]{2,1,0:T(8,128)(2,1)} %diag_ref.1) | copy-start | bytes 1572868
  6.7 0.8 %copy-start.2 = (bf16[16,2048]{1,0:T(8,128)(2,1)S(1)}, bf16[16,2048]{1,0:T(8,128)(2,1)}, u32[]{:S(2)}) copy-start(bf16[16,2048]{1,0:T(8,128)(2,1)} %x_ref.1) | copy-start | bytes 196612
  10.0 12.7 %all-to-all-start = ((bf16[4,2,16,2048]{3,2,1,0:T(8,128)(2,1)}), bf16[4,2,16,2048]{3,2,1,0:T(8,128)(2,1)S(1)}, u32[]{:S(2)}, u32[]{:S(2)}) async-start(bf16[4,2,16,2048]{3,2,1,0:T(8,128)(2,1)} %get-tuple-element.27), calls=%async_computation | async-start | bytes 1048576 | tf_op jit(solution)/shard_map/all_to_all | solution.py:313
  14.3 9.1 %collective-permute-start.4 = (bf16[2,16,2048]{2,1,0:T(8,128)(2,1)S(1)}, bf16[2,16,2048]{2,1,0:T(8,128)(2,1)S(1)}, u32[]{:S(2)}, u32[]{:S(2)}) collective-permute-start(bf16[2,16,2048]{2,1,0:T(8,128)(2,1)S(1)} %get-tuple-element.26), channel_id=1, source_target_pairs={{0,3},{1,0},{2,1},{3,2},{4,7},{5,4},{6,5},{7,6},{8,11},{9,8},{10,9... | collective-permute-start | bytes 393224 | tf_op jit(solution)/shard_map/ppermute | solution.py:316
  17.3 6.6 %collective-permute-start.3 = (bf16[2,16,2048]{2,1,0:T(8,128)(2,1)S(1)}, bf16[2,16,2048]{2,1,0:T(8,128)(2,1)S(1)}, u32[]{:S(2)}, u32[]{:S(2)}) collective-permute-start(bf16[2,16,2048]{2,1,0:T(8,128)(2,1)S(1)} %get-tuple-element.26), channel_id=1, source_target_pairs={{0,2},{1,3},{2,0},{3,1},{4,6},{5,7},{6,4},{7,5},{8,10},{9,11},{10,... | collective-permute-start | bytes 393224 | tf_op jit(solution)/shard_map/ppermute | solution.py:316
  17.9 7.3 %collective-permute-start.2 = (bf16[2,16,2048]{2,1,0:T(8,128)(2,1)S(1)}, bf16[2,16,2048]{2,1,0:T(8,128)(2,1)S(1)}, u32[]{:S(2)}, u32[]{:S(2)}) collective-permute-start(bf16[2,16,2048]{2,1,0:T(8,128)(2,1)S(1)} %get-tuple-element.26), channel_id=1, source_target_pairs={{0,1},{1,2},{2,3},{3,0},{4,5},{5,6},{6,7},{7,4},{8,9},{9,10},{10,1... | collective-permute-start | bytes 393224 | tf_op jit(solution)/shard_map/ppermute | solution.py:316
  22.7 2.7 %collective-permute-start.5 = (bf16[4,2,16,2048]{3,2,1,0:T(8,128)(2,1)S(1)}, bf16[4,2,16,2048]{3,2,1,0:T(8,128)(2,1)S(1)}, u32[]{:S(2)}, u32[]{:S(2)}) collective-permute-start(bf16[4,2,16,2048]{3,2,1,0:T(8,128)(2,1)S(1)} %all-to-all-done.refs_3_.xcol_ref), channel_id=1, source_target_pairs={{0,8},{8,0},{16,24},{24,16},{32,40},{40,32},{48,56},{56,48},{64,72... | collective-permute-start | bytes 1572872 | tf_op jit(solution)/shard_map/ppermute | solution.py:314
  25.4 33.7 %copy-start = (bf16[16,128,128]{2,1,0:T(8,128)(2,1)S(1)}, bf16[16,128,128]{2,1,0:T(8,128)(2,1)}, u32[]{:S(2)}) copy-start(bf16[16,128,128]{2,1,0:T(8,128)(2,1)} %pre_ref.1) | copy-start | bytes 1572868
  29.1 3.1 %collective-permute-start.6 = (bf16[9,16,2048]{2,1,0:T(8,128)(2,1)S(1)}, bf16[9,16,2048]{2,1,0:T(8,128)(2,1)S(1)}, u32[]{:S(2)}, u32[]{:S(2)}) collective-permute-start(bf16[9,16,2048]{2,1,0:T(8,128)(2,1)S(1)} %get-tuple-element.29.own_ref), channel_id=1, source_target_pairs={{0,8},{8,0},{16,24},{24,16},{32,40},{40,32},{48,56},{56,48},{64,72... | collective-permute-start | bytes 1769480 | tf_op jit(solution)/shard_map/ppermute | solution.py:362
  32.2 7.8 %collective-permute-start.7 = (bf16[2,16,2176]{2,1,0:T(8,128)(2,1)S(1)}, bf16[2,16,2176]{2,1,0:T(8,128)(2,1)S(1)}, u32[]{:S(2)}, u32[]{:S(2)}) collective-permute-start(bf16[2,16,2176]{2,1,0:T(8,128)(2,1)S(1)} %get-tuple-element.33), channel_id=1, source_target_pairs={{0,32},{8,40},{16,48},{24,56},{32,64},{40,72},{48,80},{56,88},{64,... | collective-permute-start | bytes 417800 | tf_op jit(solution)/shard_map/ppermute | solution.py:334
  35.3 10.2 %collective-permute-start.8 = (bf16[2,16,2176]{2,1,0:T(8,128)(2,1)S(1)}, bf16[2,16,2176]{2,1,0:T(8,128)(2,1)S(1)}, u32[]{:S(2)}, u32[]{:S(2)}) collective-permute-start(bf16[2,16,2176]{2,1,0:T(8,128)(2,1)S(1)} %get-tuple-element.34), channel_id=1, source_target_pairs={{0,64},{8,72},{16,80},{24,88},{32,96},{40,104},{48,112},{56,120},{... | collective-permute-start | bytes 417800 | tf_op jit(solution)/shard_map/ppermute | solution.py:334
  36.9 8.6 %collective-permute-start.9 = (bf16[2,16,2176]{2,1,0:T(8,128)(2,1)S(1)}, bf16[2,16,2176]{2,1,0:T(8,128)(2,1)S(1)}, u32[]{:S(2)}, u32[]{:S(2)}) collective-permute-start(bf16[2,16,2176]{2,1,0:T(8,128)(2,1)S(1)} %get-tuple-element.35), channel_id=1, source_target_pairs={{0,96},{8,104},{16,112},{24,120},{32,0},{40,8},{48,16},{56,24},{64... | collective-permute-start | bytes 417800 | tf_op jit(solution)/shard_map/ppermute | solution.py:334
  39.4 8.7 %collective-permute-start.10 = (bf16[2,16,2048]{2,1,0:T(8,128)(2,1)S(1)}, bf16[2,16,2048]{2,1,0:T(8,128)(2,1)S(1)}, u32[]{:S(2)}, u32[]{:S(2)}) collective-permute-start(bf16[2,16,2048]{2,1,0:T(8,128)(2,1)S(1)} %get-tuple-element.36), channel_id=1, source_target_pairs={{0,1},{1,2},{2,3},{3,0},{4,5},{5,6},{6,7},{7,4},{8,9},{9,10},{10,1... | collective-permute-start | bytes 393224 | tf_op jit(solution)/shard_map/ppermute | solution.py:331
  39.4 8.7 %collective-permute-start.11 = (bf16[2,16,2048]{2,1,0:T(8,128)(2,1)S(1)}, bf16[2,16,2048]{2,1,0:T(8,128)(2,1)S(1)}, u32[]{:S(2)}, u32[]{:S(2)}) collective-permute-start(bf16[2,16,2048]{2,1,0:T(8,128)(2,1)S(1)} %get-tuple-element.37), channel_id=1, source_target_pairs={{0,2},{1,3},{2,0},{3,1},{4,6},{5,7},{6,4},{7,5},{8,10},{9,11},{10,... | collective-permute-start | bytes 393224 | tf_op jit(solution)/shard_map/ppermute | solution.py:331
  40.0 8.8 %collective-permute-start.12 = (bf16[2,16,2048]{2,1,0:T(8,128)(2,1)S(1)}, bf16[2,16,2048]{2,1,0:T(8,128)(2,1)S(1)}, u32[]{:S(2)}, u32[]{:S(2)}) collective-permute-start(bf16[2,16,2048]{2,1,0:T(8,128)(2,1)S(1)} %get-tuple-element.38), channel_id=1, source_target_pairs={{0,3},{1,0},{2,1},{3,2},{4,7},{5,4},{6,5},{7,6},{8,11},{9,8},{10,9... | collective-permute-start | bytes 393224 | tf_op jit(solution)/shard_map/ppermute | solution.py:331
  45.6 3.6 %collective-permute-start.15 = (bf16[16,128]{1,0:T(8,128)(2,1)S(1)}, bf16[16,128]{1,0:T(8,128)(2,1)S(1)}, u32[]{:S(2)}, u32[]{:S(2)}) collective-permute-start(bf16[16,128]{1,0:T(8,128)(2,1)S(1)} %shard_map.92.refs_0_), channel_id=1, source_target_pairs={{0,3},{1,0},{2,1},{3,2},{4,7},{5,4},{6,5},{7,6},{8,11},{9,8},{10,9... | collective-permute-start | bytes 12296 | tf_op jit(solution)/shard_map/ppermute | solution.py:331
  46.3 5.1 %collective-permute-start.14 = (bf16[16,128]{1,0:T(8,128)(2,1)S(1)}, bf16[16,128]{1,0:T(8,128)(2,1)S(1)}, u32[]{:S(2)}, u32[]{:S(2)}) collective-permute-start(bf16[16,128]{1,0:T(8,128)(2,1)S(1)} %shard_map.92.refs_0_), channel_id=1, source_target_pairs={{0,2},{1,3},{2,0},{3,1},{4,6},{5,7},{6,4},{7,5},{8,10},{9,11},{10,... | collective-permute-start | bytes 12296 | tf_op jit(solution)/shard_map/ppermute | solution.py:331
  48.2 4.8 %collective-permute-start.13 = (bf16[16,128]{1,0:T(8,128)(2,1)S(1)}, bf16[16,128]{1,0:T(8,128)(2,1)S(1)}, u32[]{:S(2)}, u32[]{:S(2)}) collective-permute-start(bf16[16,128]{1,0:T(8,128)(2,1)S(1)} %shard_map.92.refs_0_), channel_id=1, source_target_pairs={{0,1},{1,2},{2,3},{3,0},{4,5},{5,6},{6,7},{7,4},{8,9},{9,10},{10,1... | collective-permute-start | bytes 12296 | tf_op jit(solution)/shard_map/ppermute | solution.py:331
  53.1 5.9 %collective-permute-start.16 = (bf16[16,2176]{1,0:T(8,128)(2,1)S(1)}, bf16[16,2176]{1,0:T(8,128)(2,1)S(1)}, u32[]{:S(2)}, u32[]{:S(2)}) collective-permute-start(bf16[16,2176]{1,0:T(8,128)(2,1)S(1)} %get-tuple-element.43), channel_id=1, source_target_pairs={{0,16},{8,24},{16,0},{24,8},{32,48},{40,56},{48,32},{56,40},{64,80... | collective-permute-start | bytes 208904 | tf_op jit(solution)/shard_map/ppermute | solution.py:382
  54.2 4.8 %collective-permute-start.17 = (bf16[16,2176]{1,0:T(8,128)(2,1)S(1)}, bf16[16,2176]{1,0:T(8,128)(2,1)S(1)}, u32[]{:S(2)}, u32[]{:S(2)}) collective-permute-start(bf16[16,2176]{1,0:T(8,128)(2,1)S(1)} %get-tuple-element.44), channel_id=1, source_target_pairs={{0,4},{1,5},{2,6},{3,7},{4,0},{5,1},{6,2},{7,3},{8,12},{9,13},{10,... | collective-permute-start | bytes 208904 | tf_op jit(solution)/shard_map/ppermute | solution.py:383
  54.2 4.8 %collective-permute-start.18 = (bf16[16,128]{1,0:T(8,128)(2,1)S(1)}, bf16[16,128]{1,0:T(8,128)(2,1)S(1)}, u32[]{:S(2)}, u32[]{:S(2)}) collective-permute-start(bf16[16,128]{1,0:T(8,128)(2,1)S(1)} %get-tuple-element.45.tile_ref), channel_id=1, source_target_pairs={{0,20},{1,21},{2,22},{3,23},{4,16},{5,17},{6,18},{7,19},{8,28},{9,... | collective-permute-start | bytes 12296 | tf_op jit(solution)/shard_map/ppermute | solution.py:384

commit v6 on v5

--- a/solution.py
+++ b/solution.py
@@ -6,7 +6,7 @@
 from jax.experimental.pallas import tpu as pltpu
 from jax.sharding import PartitionSpec as P
 
-CHUNK = 16
+CHUNK = 32
 GROUP = 8
 LANES = 128
 F32 = jnp.float32
@@ -103,14 +103,13 @@
     acc_row[...] = jnp.zeros_like(acc_row)
     acc_col[...] = jnp.zeros_like(acc_col)
     place = lax.axis_index("row")
-    high = (place // 2) % 2
-    core = place % 2
-    for line in range(xcol_ref.shape[0]):
+    lines = xcol_ref.shape[0]
+    for s in range(lines):
         for k in range(2):
-            for ref, twin in ((xcol_ref, 0), (twin_ref, 1)):
-                dev = line * 4 + (high + k) % 2 * 2 + (core + twin) % 2
+            for twin, ref in enumerate((xcol_ref, twin_ref)):
+                dev = (place // 4 + lines - s) % lines * 4 + (place // 2 + k) % 2 * 2 + (place + twin) % 2
                 for t in range(owned):
-                    x_col[dev * owned + t] = ref[line, k, :, t * LANES:(t + 1) * LANES]
+                    x_col[dev * owned + t] = ref[s, k, :, t * LANES:(t + 1) * LANES]
     for copy in index_copies:
         copy.wait()
     for c, copy in enumerate(copies):
@@ -231,12 +230,16 @@
         search_ref[:, here] = out.astype(BF16)
 
 
-def prepare_kernel(x_ref, z_ref, h_ref, pair_ref, lines_ref):
-    pair_ref[0] = x_ref[...]
-    pair_ref[1] = z_ref[...]
-    for d in range(lines_ref.shape[0]):
-        lines_ref[d, 0] = x_ref[...]
-        lines_ref[d, 1] = h_ref[...]
+def pairs_kernel(x_ref, z_ref, h_ref, ring_ref, line_ref):
+    for ref, other in ((ring_ref, z_ref), (line_ref, h_ref)):
+        ref[0] = x_ref[...]
+        ref[1] = other[...]
+
+
+def stack_kernel(*refs):
+    *parts, out = refs
+    for s, ref in enumerate(parts):
+        out[s] = ref[...]
 
 
 VM = pl.BlockSpec(memory_space=pltpu.VMEM)
@@ -298,19 +301,25 @@
     )(vectors, diag_blocks)
     diag_term, stats, own_x = near(diag_term), near(stats), near(own_x)
     lines = row_devs // 4
-    pair, spread = pl.pallas_call(
-        prepare_kernel,
-        out_shape=(
-            jax.ShapeDtypeStruct((2, width, span), BF16),
-            jax.ShapeDtypeStruct((lines, 2, width, span), BF16),
-        ),
+    pair, line = pl.pallas_call(
+        pairs_kernel,
+        out_shape=(jax.ShapeDtypeStruct((2, width, span), BF16),) * 2,
         in_specs=[VM, VM, VM],
         out_specs=(VM, VM),
         compiler_params=params(4),
     )(own_x, beside, above)
-    pair = near(pair)
-    same_line = [[x * 4 + k for x in range(lines)] for k in range(4)]
-    xcol = lax.all_to_all(spread, "row", 0, 0, axis_index_groups=same_line, tiled=True)
+    pair, line = near(pair), near(line)
+    passed = [
+        near(lax.ppermute(line, "row", [(i, (i + 4 * s) % row_devs) for i in range(row_devs)])) for s in range(1, lines)
+    ]
+    xcol = near(pl.pallas_call(
+        stack_kernel,
+        out_shape=jax.ShapeDtypeStruct((lines, 2, width, span), BF16),
+        in_specs=[VM] * lines,
+        out_specs=VM,
+        compiler_params=params(4),
+        cost_estimate=cost(0, 1 << 20),
+    )(line, *passed))
     xcol_twin = near(lax.ppermute(xcol, "row", [(i, i ^ 1) for i in range(row_devs)]))
     turned = [
         near(lax.ppermute(pair, "col", [(i, i // runs * runs + (i + s) % runs) for i in range(col_devs)]))

time: 60.8 us -> 59.6 us (0.980); the launches traced: 60.1 us -> 59.9 us
  starting transfers between devices: 34 us -> 29.3 us
  waiting for transfers between devices: 16.1 us -> 20 us
  Pallas kernels: 6.69 us -> 7.32 us
    ppermute x0 -> x3, starting transfers between devices: none -> 4.51 us  [per_device(): lax.ppermute(line, 'row', [(i, (i + 4 * s) % row_devs) for i in range(row...]
    all_to_all x1 -> x0, starting transfers between devices: 4.29 us -> none  [per_device(): lax.all_to_all(spread, 'row', 0, 0, axis_index_groups=same_line, tiled=True)]
    all_to_all x1 -> x0, waiting for transfers between devices: 3.81 us -> none  [per_device(): lax.all_to_all(spread, 'row', 0, 0, axis_index_groups=same_line, tiled=True)]
    ppermute x3, starting transfers between devices: 7.21 us -> 3.88 us  [along_x(): lax.ppermute(x, 'row', [(i, (i + 4 * s) % row_devs) for i in range(row_de...]
    ppermute x3, waiting for transfers between devices: 0.01 us -> 3.05 us  [along_x(): lax.ppermute(x, 'row', [(i, (i + 4 * s) % row_devs) for i in range(row_de...]
    ppermute x1, waiting for transfers between devices: 1.78 us -> 3.94 us  [per_device(): across = near(lax.ppermute(tile, ('row', 'col'), across_z))]
    ppermute x1, starting transfers between devices: 3.04 us -> 0.88 us  [per_device(): across = near(lax.ppermute(tile, ('row', 'col'), across_z))]
    ppermute x0 -> x3, waiting for transfers between devices: none -> 1.91 us  [per_device(): lax.ppermute(line, 'row', [(i, (i + 4 * s) % row_devs) for i in range(row...]
  transfers between devices with their start and end apart: 20 -> 22, of which waited for: 11 -> 13; matrix products, arithmetic and copies ran while one was open for 0% -> 0% of each run, Pallas kernels for 1% -> 2%
where the time goes in v6:
time: 59.6 us; the launch traced here: 59.9 us
  starting transfers between devices  29.3 us (49%)
  waiting for transfers between devices  20 us (34%)
  Pallas kernels  7.32 us (12%)
  local copies, waits for them, and re-layouts  1.89 us (3%)
  between operations  1.39 us (2%)
    ppermute x6, starting transfers between devices, along_y(): lax.ppermute(x, 'col', [(i, i // runs * runs + (i + s) % runs) for i in r...  5.98 us
    pallas_call x1, Pallas kernels, per_device(): pl.pallas_call(block_kernel, out_shape=(*[shape(2, width, span)] * (runs...  5.09 us
    ppermute x3, starting transfers between devices, per_device(): lax.ppermute(pair, 'col', [(i, i // runs * runs + (i + s) % runs) for i i...  4.62 us
    ppermute x6, waiting for transfers between devices, along_y(): lax.ppermute(x, 'col', [(i, i // runs * runs + (i + s) % runs) for i in r...  4.53 us
    ppermute x3, starting transfers between devices, per_device(): lax.ppermute(line, 'row', [(i, (i + 4 * s) % row_devs) for i in range(row...  4.51 us
    ppermute x1, starting transfers between devices, per_device(): lax.ppermute(vectors, 'row', [(i, i ^ 2) for i in range(row_devs)])  4.04 us
    ppermute x1, waiting for transfers between devices, per_device(): across = near(lax.ppermute(tile, ('row', 'col'), across_z))  3.94 us
    ppermute x3, starting transfers between devices, along_x(): lax.ppermute(x, 'row', [(i, (i + 4 * s) % row_devs) for i in range(row_de...  3.88 us
  transfers between devices with their start and end apart: 22, of which 13 were waited for; matrix products, arithmetic and copies ran while one was open for 0% of the time, Pallas kernels for 2%

profile of v6, /device:TPU:0, one launch (start us, length us, event | category | flops | bytes accessed | tf_op | source)
XLA Modules:
  0.0 59.9 jit_solution(17958817572542197022)
XLA Ops:
  0.6 4.0 %collective-permute-start.1 = (bf16[16,2048]{1,0:T(8,128)(2,1)}, bf16[16,2048]{1,0:T(8,128)(2,1)S(1)}, u32[]{:S(2)}, u32[]{:S(2)}) collective-permute-start(bf16[16,2048]{1,0:T(8,128)(2,1)} %x_ref.1), channel_id=1, source_target_pairs={{0,16},{8,24},{16,0},{24,8},{32,48},{40,56},{48,32},{56,40},{64,80... | collective-permute-start | bytes 196616 | tf_op jit(solution)/shard_map/ppermute | solution.py:289
  4.7 1.0 %collective-permute-start = (bf16[16,2048]{1,0:T(8,128)(2,1)}, bf16[16,2048]{1,0:T(8,128)(2,1)S(1)}, u32[]{:S(2)}, u32[]{:S(2)}) collective-permute-start(bf16[16,2048]{1,0:T(8,128)(2,1)} %x_ref.1), channel_id=1, source_target_pairs={{0,4},{1,5},{2,6},{3,7},{4,0},{5,1},{6,2},{7,3},{8,12},{9,13},{10,... | collective-permute-start | bytes 196616 | tf_op jit(solution)/shard_map/ppermute | solution.py:283
  5.7 1.0 %copy-done.1 = bf16[16,128,128]{2,1,0:T(8,128)(2,1)S(1)} copy-done((bf16[16,128,128]{2,1,0:T(8,128)(2,1)S(1)}, bf16[16,128,128]{2,1,0:T(8,128)(2,1)}, u32[]{:S(2)}) %copy-start.1) | copy-done | bytes 524312
  6.7 0.8 %copy-done.2 = bf16[16,2048]{1,0:T(8,128)(2,1)S(1)} copy-done((bf16[16,2048]{1,0:T(8,128)(2,1)S(1)}, bf16[16,2048]{1,0:T(8,128)(2,1)}, u32[]{:S(2)}) %copy-start.2) | copy-done | bytes 65560
  7.6 0.5 shard_map.86
  8.1 1.0 %collective-permute-done.z_ref = bf16[16,2048]{1,0:T(8,128)(2,1)S(1)} collective-permute-done((bf16[16,2048]{1,0:T(8,128)(2,1)}, bf16[16,2048]{1,0:T(8,128)(2,1)S(1)}, u32[]{:S(2)}, u32[]{:S(2)}) %collective-permute-start) | collective-permute-done | bytes 65568 | tf_op jit(solution)/shard_map/ppermute | solution.py:283
  9.2 2.8 %collective-permute-start.7 = (bf16[2,16,2048]{2,1,0:T(8,128)(2,1)S(1)}, bf16[2,16,2048]{2,1,0:T(8,128)(2,1)S(1)}, u32[]{:S(2)}, u32[]{:S(2)}) collective-permute-start(bf16[2,16,2048]{2,1,0:T(8,128)(2,1)S(1)} %get-tuple-element.27.refs_0_), channel_id=1, source_target_pairs={{0,96},{8,104},{16,112},{24,120},{32,0},{40,8},{48,16},{56,24},{64... | collective-permute-start | bytes 393224 | tf_op jit(solution)/shard_map/ppermute | solution.py:313
  12.0 0.8 %collective-permute-start.6 = (bf16[2,16,2048]{2,1,0:T(8,128)(2,1)S(1)}, bf16[2,16,2048]{2,1,0:T(8,128)(2,1)S(1)}, u32[]{:S(2)}, u32[]{:S(2)}) collective-permute-start(bf16[2,16,2048]{2,1,0:T(8,128)(2,1)S(1)} %get-tuple-element.27.refs_0_), channel_id=1, source_target_pairs={{0,64},{8,72},{16,80},{24,88},{32,96},{40,104},{48,112},{56,120},{... | collective-permute-start | bytes 393224 | tf_op jit(solution)/shard_map/ppermute | solution.py:313
  12.8 0.9 %collective-permute-start.5 = (bf16[2,16,2048]{2,1,0:T(8,128)(2,1)S(1)}, bf16[2,16,2048]{2,1,0:T(8,128)(2,1)S(1)}, u32[]{:S(2)}, u32[]{:S(2)}) collective-permute-start(bf16[2,16,2048]{2,1,0:T(8,128)(2,1)S(1)} %get-tuple-element.27.refs_0_), channel_id=1, source_target_pairs={{0,32},{8,40},{16,48},{24,56},{32,64},{40,72},{48,80},{56,88},{64,... | collective-permute-start | bytes 393224 | tf_op jit(solution)/shard_map/ppermute | solution.py:313
  13.7 3.0 %collective-permute-start.4 = (bf16[2,16,2048]{2,1,0:T(8,128)(2,1)S(1)}, bf16[2,16,2048]{2,1,0:T(8,128)(2,1)S(1)}, u32[]{:S(2)}, u32[]{:S(2)}) collective-permute-start(bf16[2,16,2048]{2,1,0:T(8,128)(2,1)S(1)} %get-tuple-element.26), channel_id=1, source_target_pairs={{0,3},{1,0},{2,1},{3,2},{4,7},{5,4},{6,5},{7,6},{8,11},{9,8},{10,9... | collective-permute-start | bytes 393224 | tf_op jit(solution)/shard_map/ppermute | solution.py:325
  16.7 0.6 %collective-permute-start.3 = (bf16[2,16,2048]{2,1,0:T(8,128)(2,1)S(1)}, bf16[2,16,2048]{2,1,0:T(8,128)(2,1)S(1)}, u32[]{:S(2)}, u32[]{:S(2)}) collective-permute-start(bf16[2,16,2048]{2,1,0:T(8,128)(2,1)S(1)} %get-tuple-element.26), channel_id=1, source_target_pairs={{0,2},{1,3},{2,0},{3,1},{4,6},{5,7},{6,4},{7,5},{8,10},{9,11},{10,... | collective-permute-start | bytes 393224 | tf_op jit(solution)/shard_map/ppermute | solution.py:325
  17.3 1.0 %collective-permute-start.2 = (bf16[2,16,2048]{2,1,0:T(8,128)(2,1)S(1)}, bf16[2,16,2048]{2,1,0:T(8,128)(2,1)S(1)}, u32[]{:S(2)}, u32[]{:S(2)}) collective-permute-start(bf16[2,16,2048]{2,1,0:T(8,128)(2,1)S(1)} %get-tuple-element.26), channel_id=1, source_target_pairs={{0,1},{1,2},{2,3},{3,0},{4,5},{5,6},{6,7},{7,4},{8,9},{9,10},{10,1... | collective-permute-start | bytes 393224 | tf_op jit(solution)/shard_map/ppermute | solution.py:325
  18.3 0.6 collective-permute-done.6.refs_2_
  18.9 1.3 %collective-permute-done.5.refs_1_ = bf16[2,16,2048]{2,1,0:T(8,128)(2,1)S(1)} collective-permute-done((bf16[2,16,2048]{2,1,0:T(8,128)(2,1)S(1)}, bf16[2,16,2048]{2,1,0:T(8,128)(2,1)S(1)}, u32[]{:S(2)}, u32[]{:S(2)}) %collective-permute-start.5) | collective-permute-done | bytes 131104 | tf_op jit(solution)/shard_map/ppermute | solution.py:313
  21.0 2.3 %collective-permute-done.3.refs_1_ = bf16[2,16,2048]{2,1,0:T(8,128)(2,1)S(1)} collective-permute-done((bf16[2,16,2048]{2,1,0:T(8,128)(2,1)S(1)}, bf16[2,16,2048]{2,1,0:T(8,128)(2,1)S(1)}, u32[]{:S(2)}, u32[]{:S(2)}) %collective-permute-start.3) | collective-permute-done | bytes 131104 | tf_op jit(solution)/shard_map/ppermute | solution.py:325
  23.3 1.3 %collective-permute-done.2.refs_0_ = bf16[2,16,2048]{2,1,0:T(8,128)(2,1)S(1)} collective-permute-done((bf16[2,16,2048]{2,1,0:T(8,128)(2,1)S(1)}, bf16[2,16,2048]{2,1,0:T(8,128)(2,1)S(1)}, u32[]{:S(2)}, u32[]{:S(2)}) %collective-permute-start.2) | collective-permute-done | bytes 131104 | tf_op jit(solution)/shard_map/ppermute | solution.py:325
  24.7 5.1 %shard_map.90 = (bf16[2,16,2048]{2,1,0:T(8,128)(2,1)S(1)}, bf16[2,16,2048]{2,1,0:T(8,128)(2,1)S(1)}, bf16[2,16,2048]{2,1,0:T(8,128)(2,1)S(1)}, f32[2,16,2048]{2,...) custom-call(s32[1,1]{1,0:T(1,128)S(6)} %copy.9.count_ref, s32[192]{0:T(256)} %bitcast.4, ...), custom_call_target="tpu_custom_call" | custom-call | tf_op jit(solution)/shard_map/pallas_call | solution.py:354
  29.9 2.0 %collective-permute-done.9.got_ref = bf16[9,16,2048]{2,1,0:T(8,128)(2,1)S(1)} collective-permute-done((bf16[9,16,2048]{2,1,0:T(8,128)(2,1)S(1)}, bf16[9,16,2048]{2,1,0:T(8,128)(2,1)S(1)}, u32[]{:S(2)}, u32[]{:S(2)}) %collective-permute-start.9) | collective-permute-done | bytes 589856 | tf_op jit(solution)/shard_map/ppermute | solution.py:371
  32.1 3.8 %collective-permute-start.11 = (bf16[2,16,2176]{2,1,0:T(8,128)(2,1)S(1)}, bf16[2,16,2176]{2,1,0:T(8,128)(2,1)S(1)}, u32[]{:S(2)}, u32[]{:S(2)}) collective-permute-start(bf16[2,16,2176]{2,1,0:T(8,128)(2,1)S(1)} %get-tuple-element.34), channel_id=1, source_target_pairs={{0,64},{8,72},{16,80},{24,88},{32,96},{40,104},{48,112},{56,120},{... | collective-permute-start | bytes 417800 | tf_op jit(solution)/shard_map/ppermute | solution.py:343
  35.9 2.8 %collective-permute-start.14 = (bf16[2,16,2048]{2,1,0:T(8,128)(2,1)S(1)}, bf16[2,16,2048]{2,1,0:T(8,128)(2,1)S(1)}, u32[]{:S(2)}, u32[]{:S(2)}) collective-permute-start(bf16[2,16,2048]{2,1,0:T(8,128)(2,1)S(1)} %get-tuple-element.37), channel_id=1, source_target_pairs={{0,2},{1,3},{2,0},{3,1},{4,6},{5,7},{6,4},{7,5},{8,10},{9,11},{10,... | collective-permute-start | bytes 393224 | tf_op jit(solution)/shard_map/ppermute | solution.py:340
  39.2 0.8 %collective-permute-start.15 = (bf16[2,16,2048]{2,1,0:T(8,128)(2,1)S(1)}, bf16[2,16,2048]{2,1,0:T(8,128)(2,1)S(1)}, u32[]{:S(2)}, u32[]{:S(2)}) collective-permute-start(bf16[2,16,2048]{2,1,0:T(8,128)(2,1)S(1)} %get-tuple-element.38), channel_id=1, source_target_pairs={{0,3},{1,0},{2,1},{3,2},{4,7},{5,4},{6,5},{7,6},{8,11},{9,8},{10,9... | collective-permute-start | bytes 393224 | tf_op jit(solution)/shard_map/ppermute | solution.py:340
  40.1 2.5 %collective-permute-done.11.refs_1_ = bf16[2,16,2176]{2,1,0:T(8,128)(2,1)S(1)} collective-permute-done((bf16[2,16,2176]{2,1,0:T(8,128)(2,1)S(1)}, bf16[2,16,2176]{2,1,0:T(8,128)(2,1)S(1)}, u32[]{:S(2)}, u32[]{:S(2)}) %collective-permute-start.11) | collective-permute-done | bytes 139296 | tf_op jit(solution)/shard_map/ppermute | solution.py:343
  42.7 1.6 %collective-permute-start.17 = (bf16[16,128]{1,0:T(8,128)(2,1)S(1)}, bf16[16,128]{1,0:T(8,128)(2,1)S(1)}, u32[]{:S(2)}, u32[]{:S(2)}) collective-permute-start(bf16[16,128]{1,0:T(8,128)(2,1)S(1)} %shard_map.93.refs_0_), channel_id=1, source_target_pairs={{0,2},{1,3},{2,0},{3,1},{4,6},{5,7},{6,4},{7,5},{8,10},{9,11},{10,... | collective-permute-start | bytes 12296 | tf_op jit(solution)/shard_map/ppermute | solution.py:340
  44.3 0.6 collective-permute-done.13.refs_3_
  44.9 0.7 %collective-permute-start.16 = (bf16[16,128]{1,0:T(8,128)(2,1)S(1)}, bf16[16,128]{1,0:T(8,128)(2,1)S(1)}, u32[]{:S(2)}, u32[]{:S(2)}) collective-permute-start(bf16[16,128]{1,0:T(8,128)(2,1)S(1)} %shard_map.93.refs_0_), channel_id=1, source_target_pairs={{0,1},{1,2},{2,3},{3,0},{4,5},{5,6},{6,7},{7,4},{8,9},{9,10},{10,1... | collective-permute-start | bytes 12296 | tf_op jit(solution)/shard_map/ppermute | solution.py:340
  46.3 1.6 %collective-permute-done.17.refs_2_ = bf16[16,128]{1,0:T(8,128)(2,1)S(1)} collective-permute-done((bf16[16,128]{1,0:T(8,128)(2,1)S(1)}, bf16[16,128]{1,0:T(8,128)(2,1)S(1)}, u32[]{:S(2)}, u32[]{:S(2)}) %collective-permute-start.17) | collective-permute-done | bytes 4128 | tf_op jit(solution)/shard_map/ppermute | solution.py:340
  47.9 1.8 %collective-permute-done.16.refs_1_ = bf16[16,128]{1,0:T(8,128)(2,1)S(1)} collective-permute-done((bf16[16,128]{1,0:T(8,128)(2,1)S(1)}, bf16[16,128]{1,0:T(8,128)(2,1)S(1)}, u32[]{:S(2)}, u32[]{:S(2)}) %collective-permute-start.16) | collective-permute-done | bytes 4128 | tf_op jit(solution)/shard_map/ppermute | solution.py:340
  49.8 2.7 %collective-permute-start.19 = (bf16[16,2176]{1,0:T(8,128)(2,1)S(1)}, bf16[16,2176]{1,0:T(8,128)(2,1)S(1)}, u32[]{:S(2)}, u32[]{:S(2)}) collective-permute-start(bf16[16,2176]{1,0:T(8,128)(2,1)S(1)} %get-tuple-element.43), channel_id=1, source_target_pairs={{0,16},{8,24},{16,0},{24,8},{32,48},{40,56},{48,32},{56,40},{64,80... | collective-permute-start | bytes 208904 | tf_op jit(solution)/shard_map/ppermute | solution.py:391
  52.5 1.5 %collective-permute-start.20 = (bf16[16,2176]{1,0:T(8,128)(2,1)S(1)}, bf16[16,2176]{1,0:T(8,128)(2,1)S(1)}, u32[]{:S(2)}, u32[]{:S(2)}) collective-permute-start(bf16[16,2176]{1,0:T(8,128)(2,1)S(1)} %get-tuple-element.44), channel_id=1, source_target_pairs={{0,4},{1,5},{2,6},{3,7},{4,0},{5,1},{6,2},{7,3},{8,12},{9,13},{10,... | collective-permute-start | bytes 208904 | tf_op jit(solution)/shard_map/ppermute | solution.py:392
  54.0 0.9 %collective-permute-start.21 = (bf16[16,128]{1,0:T(8,128)(2,1)S(1)}, bf16[16,128]{1,0:T(8,128)(2,1)S(1)}, u32[]{:S(2)}, u32[]{:S(2)}) collective-permute-start(bf16[16,128]{1,0:T(8,128)(2,1)S(1)} %get-tuple-element.45.tile_ref), channel_id=1, source_target_pairs={{0,20},{1,21},{2,22},{3,23},{4,16},{5,17},{6,18},{7,19},{8,28},{9,... | collective-permute-start | bytes 12296 | tf_op jit(solution)/shard_map/ppermute | solution.py:393
  54.9 3.9 %collective-permute-done.21.across_ref = bf16[16,128]{1,0:T(8,128)(2,1)S(1)} collective-permute-done((bf16[16,128]{1,0:T(8,128)(2,1)S(1)}, bf16[16,128]{1,0:T(8,128)(2,1)S(1)}, u32[]{:S(2)}, u32[]{:S(2)}) %collective-permute-start.21) | collective-permute-done | bytes 4128 | tf_op jit(solution)/shard_map/ppermute | solution.py:393
  58.8 1.1 %shard_map.95 = (f32[16,2048]{1,0:T(8,128)}, bf16[16,2048]{1,0:T(8,128)(2,1)}) custom-call(f32[16,2048]{1,0:T(8,128)S(1)} %get-tuple-element.39.own_ref, bf16[16,2176]{1,0:T(8,128)(2,1)S(1)} %collective-permute-done.19.col_ref, bf16[16,2176]{1,0:T(8,128)(2,1)S(1)} %collective-permute-done.20.row_ref, bf16[16,128]{1,0:T(8,128)(2,1)S(1)} %get-tuple-element.45.tile_ref, ...), custom_call_target="tpu_custom_call" | custom-call | tf_op jit(solution)/shard_map/pallas_call | solution.py:394
  (28 shorter events, 1.9 us)
Async XLA Ops:
  0.6 7.5 %collective-permute-start.1 = (bf16[16,2048]{1,0:T(8,128)(2,1)}, bf16[16,2048]{1,0:T(8,128)(2,1)S(1)}, u32[]{:S(2)}, u32[]{:S(2)}) collective-permute-start(bf16[16,2048]{1,0:T(8,128)(2,1)} %x_ref.1), channel_id=1, source_target_pairs={{0,16},{8,24},{16,0},{24,8},{32,48},{40,56},{48,32},{56,40},{64,80... | collective-permute-start | bytes 196616 | tf_op jit(solution)/shard_map/ppermute | solution.py:289
  4.7 4.5 %collective-permute-start = (bf16[16,2048]{1,0:T(8,128)(2,1)}, bf16[16,2048]{1,0:T(8,128)(2,1)S(1)}, u32[]{:S(2)}, u32[]{:S(2)}) collective-permute-start(bf16[16,2048]{1,0:T(8,128)(2,1)} %x_ref.1), channel_id=1, source_target_pairs={{0,4},{1,5},{2,6},{3,7},{4,0},{5,1},{6,2},{7,3},{8,12},{9,13},{10,... | collective-permute-start | bytes 196616 | tf_op jit(solution)/shard_map/ppermute | solution.py:283
  5.7 1.0 %copy-start.1 = (bf16[16,128,128]{2,1,0:T(8,128)(2,1)S(1)}, bf16[16,128,128]{2,1,0:T(8,128)(2,1)}, u32[]{:S(2)}) copy-start(bf16[16,128,128]{2,1,0:T(8,128)(2,1)} %diag_ref.1) | copy-start | bytes 1572868
  6.7 0.8 %copy-start.2 = (bf16[16,2048]{1,0:T(8,128)(2,1)S(1)}, bf16[16,2048]{1,0:T(8,128)(2,1)}, u32[]{:S(2)}) copy-start(bf16[16,2048]{1,0:T(8,128)(2,1)} %x_ref.1) | copy-start | bytes 196612
  9.2 8.2 %collective-permute-start.7 = (bf16[2,16,2048]{2,1,0:T(8,128)(2,1)S(1)}, bf16[2,16,2048]{2,1,0:T(8,128)(2,1)S(1)}, u32[]{:S(2)}, u32[]{:S(2)}) collective-permute-start(bf16[2,16,2048]{2,1,0:T(8,128)(2,1)S(1)} %get-tuple-element.27.refs_0_), channel_id=1, source_target_pairs={{0,96},{8,104},{16,112},{24,120},{32,0},{40,8},{48,16},{56,24},{64... | collective-permute-start | bytes 393224 | tf_op jit(solution)/shard_map/ppermute | solution.py:313
  12.0 6.9 %collective-permute-start.6 = (bf16[2,16,2048]{2,1,0:T(8,128)(2,1)S(1)}, bf16[2,16,2048]{2,1,0:T(8,128)(2,1)S(1)}, u32[]{:S(2)}, u32[]{:S(2)}) collective-permute-start(bf16[2,16,2048]{2,1,0:T(8,128)(2,1)S(1)} %get-tuple-element.27.refs_0_), channel_id=1, source_target_pairs={{0,64},{8,72},{16,80},{24,88},{32,96},{40,104},{48,112},{56,120},{... | collective-permute-start | bytes 393224 | tf_op jit(solution)/shard_map/ppermute | solution.py:313
  12.8 7.4 %collective-permute-start.5 = (bf16[2,16,2048]{2,1,0:T(8,128)(2,1)S(1)}, bf16[2,16,2048]{2,1,0:T(8,128)(2,1)S(1)}, u32[]{:S(2)}, u32[]{:S(2)}) collective-permute-start(bf16[2,16,2048]{2,1,0:T(8,128)(2,1)S(1)} %get-tuple-element.27.refs_0_), channel_id=1, source_target_pairs={{0,32},{8,40},{16,48},{24,56},{32,64},{40,72},{48,80},{56,88},{64,... | collective-permute-start | bytes 393224 | tf_op jit(solution)/shard_map/ppermute | solution.py:313
  13.7 7.3 %collective-permute-start.4 = (bf16[2,16,2048]{2,1,0:T(8,128)(2,1)S(1)}, bf16[2,16,2048]{2,1,0:T(8,128)(2,1)S(1)}, u32[]{:S(2)}, u32[]{:S(2)}) collective-permute-start(bf16[2,16,2048]{2,1,0:T(8,128)(2,1)S(1)} %get-tuple-element.26), channel_id=1, source_target_pairs={{0,3},{1,0},{2,1},{3,2},{4,7},{5,4},{6,5},{7,6},{8,11},{9,8},{10,9... | collective-permute-start | bytes 393224 | tf_op jit(solution)/shard_map/ppermute | solution.py:325
  16.7 6.6 %collective-permute-start.3 = (bf16[2,16,2048]{2,1,0:T(8,128)(2,1)S(1)}, bf16[2,16,2048]{2,1,0:T(8,128)(2,1)S(1)}, u32[]{:S(2)}, u32[]{:S(2)}) collective-permute-start(bf16[2,16,2048]{2,1,0:T(8,128)(2,1)S(1)} %get-tuple-element.26), channel_id=1, source_target_pairs={{0,2},{1,3},{2,0},{3,1},{4,6},{5,7},{6,4},{7,5},{8,10},{9,11},{10,... | collective-permute-start | bytes 393224 | tf_op jit(solution)/shard_map/ppermute | solution.py:325
  17.3 7.2 %collective-permute-start.2 = (bf16[2,16,2048]{2,1,0:T(8,128)(2,1)S(1)}, bf16[2,16,2048]{2,1,0:T(8,128)(2,1)S(1)}, u32[]{:S(2)}, u32[]{:S(2)}) collective-permute-start(bf16[2,16,2048]{2,1,0:T(8,128)(2,1)S(1)} %get-tuple-element.26), channel_id=1, source_target_pairs={{0,1},{1,2},{2,3},{3,0},{4,5},{5,6},{6,7},{7,4},{8,9},{9,10},{10,1... | collective-permute-start | bytes 393224 | tf_op jit(solution)/shard_map/ppermute | solution.py:325
  20.3 4.4 %collective-permute-start.8 = (bf16[4,2,16,2048]{3,2,1,0:T(8,128)(2,1)S(1)}, bf16[4,2,16,2048]{3,2,1,0:T(8,128)(2,1)S(1)}, u32[]{:S(2)}, u32[]{:S(2)}) collective-permute-start(bf16[4,2,16,2048]{3,2,1,0:T(8,128)(2,1)S(1)} %shard_map.88.refs_3_.xcol_ref), channel_id=1, source_target_pairs={{0,8},{8,0},{16,24},{24,16},{32,40},{40,32},{48,56},{56,48},{64,72... | collective-permute-start | bytes 1572872 | tf_op jit(solution)/shard_map/ppermute | solution.py:323
  24.7 34.1 %copy-start = (bf16[16,128,128]{2,1,0:T(8,128)(2,1)S(1)}, bf16[16,128,128]{2,1,0:T(8,128)(2,1)}, u32[]{:S(2)}) copy-start(bf16[16,128,128]{2,1,0:T(8,128)(2,1)} %pre_ref.1) | copy-start | bytes 1572868
  29.8 2.1 %collective-permute-start.9 = (bf16[9,16,2048]{2,1,0:T(8,128)(2,1)S(1)}, bf16[9,16,2048]{2,1,0:T(8,128)(2,1)S(1)}, u32[]{:S(2)}, u32[]{:S(2)}) collective-permute-start(bf16[9,16,2048]{2,1,0:T(8,128)(2,1)S(1)} %get-tuple-element.29.own_ref), channel_id=1, source_target_pairs={{0,8},{8,0},{16,24},{24,16},{32,40},{40,32},{48,56},{56,48},{64,72... | collective-permute-start | bytes 1769480 | tf_op jit(solution)/shard_map/ppermute | solution.py:371
  32.0 7.2 %collective-permute-start.10 = (bf16[2,16,2176]{2,1,0:T(8,128)(2,1)S(1)}, bf16[2,16,2176]{2,1,0:T(8,128)(2,1)S(1)}, u32[]{:S(2)}, u32[]{:S(2)}) collective-permute-start(bf16[2,16,2176]{2,1,0:T(8,128)(2,1)S(1)} %get-tuple-element.33), channel_id=1, source_target_pairs={{0,32},{8,40},{16,48},{24,56},{32,64},{40,72},{48,80},{56,88},{64,... | collective-permute-start | bytes 417800 | tf_op jit(solution)/shard_map/ppermute | solution.py:343
  32.1 10.5 %collective-permute-start.11 = (bf16[2,16,2176]{2,1,0:T(8,128)(2,1)S(1)}, bf16[2,16,2176]{2,1,0:T(8,128)(2,1)S(1)}, u32[]{:S(2)}, u32[]{:S(2)}) collective-permute-start(bf16[2,16,2176]{2,1,0:T(8,128)(2,1)S(1)} %get-tuple-element.34), channel_id=1, source_target_pairs={{0,64},{8,72},{16,80},{24,88},{32,96},{40,104},{48,112},{56,120},{... | collective-permute-start | bytes 417800 | tf_op jit(solution)/shard_map/ppermute | solution.py:343
  35.9 6.7 %collective-permute-start.12 = (bf16[2,16,2176]{2,1,0:T(8,128)(2,1)S(1)}, bf16[2,16,2176]{2,1,0:T(8,128)(2,1)S(1)}, u32[]{:S(2)}, u32[]{:S(2)}) collective-permute-start(bf16[2,16,2176]{2,1,0:T(8,128)(2,1)S(1)} %get-tuple-element.35), channel_id=1, source_target_pairs={{0,96},{8,104},{16,112},{24,120},{32,0},{40,8},{48,16},{56,24},{64... | collective-permute-start | bytes 417800 | tf_op jit(solution)/shard_map/ppermute | solution.py:343
  35.9 9.0 %collective-permute-start.13 = (bf16[2,16,2048]{2,1,0:T(8,128)(2,1)S(1)}, bf16[2,16,2048]{2,1,0:T(8,128)(2,1)S(1)}, u32[]{:S(2)}, u32[]{:S(2)}) collective-permute-start(bf16[2,16,2048]{2,1,0:T(8,128)(2,1)S(1)} %get-tuple-element.36), channel_id=1, source_target_pairs={{0,1},{1,2},{2,3},{3,0},{4,5},{5,6},{6,7},{7,4},{8,9},{9,10},{10,1... | collective-permute-start | bytes 393224 | tf_op jit(solution)/shard_map/ppermute | solution.py:340
  35.9 9.7 %collective-permute-start.14 = (bf16[2,16,2048]{2,1,0:T(8,128)(2,1)S(1)}, bf16[2,16,2048]{2,1,0:T(8,128)(2,1)S(1)}, u32[]{:S(2)}, u32[]{:S(2)}) collective-permute-start(bf16[2,16,2048]{2,1,0:T(8,128)(2,1)S(1)} %get-tuple-element.37), channel_id=1, source_target_pairs={{0,2},{1,3},{2,0},{3,1},{4,6},{5,7},{6,4},{7,5},{8,10},{9,11},{10,... | collective-permute-start | bytes 393224 | tf_op jit(solution)/shard_map/ppermute | solution.py:340
  39.2 6.4 %collective-permute-start.15 = (bf16[2,16,2048]{2,1,0:T(8,128)(2,1)S(1)}, bf16[2,16,2048]{2,1,0:T(8,128)(2,1)S(1)}, u32[]{:S(2)}, u32[]{:S(2)}) collective-permute-start(bf16[2,16,2048]{2,1,0:T(8,128)(2,1)S(1)} %get-tuple-element.38), channel_id=1, source_target_pairs={{0,3},{1,0},{2,1},{3,2},{4,7},{5,4},{6,5},{7,6},{8,11},{9,8},{10,9... | collective-permute-start | bytes 393224 | tf_op jit(solution)/shard_map/ppermute | solution.py:340
  42.7 3.6 %collective-permute-start.18 = (bf16[16,128]{1,0:T(8,128)(2,1)S(1)}, bf16[16,128]{1,0:T(8,128)(2,1)S(1)}, u32[]{:S(2)}, u32[]{:S(2)}) collective-permute-start(bf16[16,128]{1,0:T(8,128)(2,1)S(1)} %shard_map.93.refs_0_), channel_id=1, source_target_pairs={{0,3},{1,0},{2,1},{3,2},{4,7},{5,4},{6,5},{7,6},{8,11},{9,8},{10,9... | collective-permute-start | bytes 12296 | tf_op jit(solution)/shard_map/ppermute | solution.py:340
  42.7 5.2 %collective-permute-start.17 = (bf16[16,128]{1,0:T(8,128)(2,1)S(1)}, bf16[16,128]{1,0:T(8,128)(2,1)S(1)}, u32[]{:S(2)}, u32[]{:S(2)}) collective-permute-start(bf16[16,128]{1,0:T(8,128)(2,1)S(1)} %shard_map.93.refs_0_), channel_id=1, source_target_pairs={{0,2},{1,3},{2,0},{3,1},{4,6},{5,7},{6,4},{7,5},{8,10},{9,11},{10,... | collective-permute-start | bytes 12296 | tf_op jit(solution)/shard_map/ppermute | solution.py:340
  44.9 4.8 %collective-permute-start.16 = (bf16[16,128]{1,0:T(8,128)(2,1)S(1)}, bf16[16,128]{1,0:T(8,128)(2,1)S(1)}, u32[]{:S(2)}, u32[]{:S(2)}) collective-permute-start(bf16[16,128]{1,0:T(8,128)(2,1)S(1)} %shard_map.93.refs_0_), channel_id=1, source_target_pairs={{0,1},{1,2},{2,3},{3,0},{4,5},{5,6},{6,7},{7,4},{8,9},{9,10},{10,1... | collective-permute-start | bytes 12296 | tf_op jit(solution)/shard_map/ppermute | solution.py:340
  49.8 9.0 %collective-permute-start.19 = (bf16[16,2176]{1,0:T(8,128)(2,1)S(1)}, bf16[16,2176]{1,0:T(8,128)(2,1)S(1)}, u32[]{:S(2)}, u32[]{:S(2)}) collective-permute-start(bf16[16,2176]{1,0:T(8,128)(2,1)S(1)} %get-tuple-element.43), channel_id=1, source_target_pairs={{0,16},{8,24},{16,0},{24,8},{32,48},{40,56},{48,32},{56,40},{64,80... | collective-permute-start | bytes 208904 | tf_op jit(solution)/shard_map/ppermute | solution.py:391
  52.5 6.3 %collective-permute-start.20 = (bf16[16,2176]{1,0:T(8,128)(2,1)S(1)}, bf16[16,2176]{1,0:T(8,128)(2,1)S(1)}, u32[]{:S(2)}, u32[]{:S(2)}) collective-permute-start(bf16[16,2176]{1,0:T(8,128)(2,1)S(1)} %get-tuple-element.44), channel_id=1, source_target_pairs={{0,4},{1,5},{2,6},{3,7},{4,0},{5,1},{6,2},{7,3},{8,12},{9,13},{10,... | collective-permute-start | bytes 208904 | tf_op jit(solution)/shard_map/ppermute | solution.py:392
  54.0 4.8 %collective-permute-start.21 = (bf16[16,128]{1,0:T(8,128)(2,1)S(1)}, bf16[16,128]{1,0:T(8,128)(2,1)S(1)}, u32[]{:S(2)}, u32[]{:S(2)}) collective-permute-start(bf16[16,128]{1,0:T(8,128)(2,1)S(1)} %get-tuple-element.45.tile_ref), channel_id=1, source_target_pairs={{0,20},{1,21},{2,22},{3,23},{4,16},{5,17},{6,18},{7,19},{8,28},{9,... | collective-permute-start | bytes 12296 | tf_op jit(solution)/shard_map/ppermute | solution.py:393

commit v7 on v6

--- a/solution.py
+++ b/solution.py
@@ -9,6 +9,7 @@
 CHUNK = 32
 GROUP = 8
 LANES = 128
+PARTS = 2
 F32 = jnp.float32
 BF16 = jnp.bfloat16
 
@@ -95,9 +96,9 @@
         pltpu.make_async_copy(rows_hbm, rows_ref, index_sems.at[0]),
         pltpu.make_async_copy(cols_hbm, cols_ref, index_sems.at[1]),
     ]
+    copies = fetch(stiff_ref, buf, sems, count)
     for copy in index_copies:
         copy.start()
-    copies = fetch(stiff_ref, buf, sems, count)
     width, span = xcol_ref.shape[2:]
     owned = span // LANES
     acc_row[...] = jnp.zeros_like(acc_row)
@@ -216,18 +217,32 @@
         row_raw[:, here] = total[1][1].astype(BF16)
 
 
-def final_kernel(own_ref, col_ref, row_ref, tile_ref, across_ref, x_ref, pre_ref, image_ref, search_ref):
+def final_kernel(own_ref, col_ref, row_ref, tile_ref, across_ref, x_ref, pre_ref, image_hbm, search_hbm,
+                 image_ref, search_ref, sems):
     span = own_ref.shape[1]
+    quarter = span // PARTS
+    copies = []
+    for p in range(PARTS):
+        for k, (ref, out) in enumerate(((image_ref, image_hbm), (search_ref, search_hbm))):
+            here = pl.ds(p * quarter, quarter)
+            copies.append(pltpu.make_async_copy(ref.at[:, here], out.at[:, here], sems.at[2 * p + k]))
+    for p in range(PARTS):
+        for t in range(p * quarter // LANES, (p + 1) * quarter // LANES):
+            here = slice(t * LANES, (t + 1) * LANES)
+            image_ref[:, here] = own_ref[:, here] + col_ref[:, here].astype(F32) + row_ref[:, here].astype(F32)
+        copies[2 * p].start()
     tile = tile_ref[...].astype(F32) + across_ref[...].astype(F32)
     xy, xx = join_tile(tile + col_ref[:, span:].astype(F32) + row_ref[:, span:].astype(F32))
     theta = xy / xx
-    for t in range(span // LANES):
-        here = slice(t * LANES, (t + 1) * LANES)
-        total = own_ref[:, here] + col_ref[:, here].astype(F32) + row_ref[:, here].astype(F32)
-        image_ref[:, here] = total
-        resid = (total - theta * x_ref[:, here].astype(F32)).astype(BF16)
-        out = lax.dot_general(resid, pre_ref[t], (((1,), (1,)), ((), ())), preferred_element_type=F32)
-        search_ref[:, here] = out.astype(BF16)
+    for p in range(PARTS):
+        for t in range(p * quarter // LANES, (p + 1) * quarter // LANES):
+            here = slice(t * LANES, (t + 1) * LANES)
+            resid = (image_ref[:, here] - theta * x_ref[:, here].astype(F32)).astype(BF16)
+            out = lax.dot_general(resid, pre_ref[t], (((1,), (1,)), ((), ())), preferred_element_type=F32)
+            search_ref[:, here] = out.astype(BF16)
+        copies[2 * p + 1].start()
+    for copy in copies:
+        copy.wait()
 
 
 def pairs_kernel(x_ref, z_ref, h_ref, ring_ref, line_ref):
@@ -395,7 +410,12 @@
         final_kernel,
         out_shape=(shape(width, span, dtype=F32), shape(width, span)),
         in_specs=[VM] * 7,
-        out_specs=(VM, VM),
+        out_specs=(HBM, HBM),
+        scratch_shapes=[
+            pltpu.VMEM((width, span), F32),
+            pltpu.VMEM((width, span), BF16),
+            pltpu.SemaphoreType.DMA((2 * PARTS,)),
+        ],
         compiler_params=params(4),
     )(own, got_col, got_row, tile, across, own_x, precond)
 

time: 59.6 us -> 59.9 us (level); the launches traced: 59.9 us -> 59.4 us
  starting transfers between devices: 29.3 us -> 33.6 us
  waiting for transfers between devices: 20 us -> 17.4 us
  Pallas kernels: 7.32 us -> 5.14 us
    ppermute x6, starting transfers between devices: 5.98 us -> 9.68 us  [along_y(): lax.ppermute(x, 'col', [(i, i // runs * runs + (i + s) % runs) for i in r...]
    ppermute x3, waiting for transfers between devices: 3.05 us -> 0.85 us  [along_x(): lax.ppermute(x, 'row', [(i, (i + 4 * s) % row_devs) for i in range(row_de...]
    pallas_call x1, Pallas kernels: 5.09 us -> 2.9 us  [per_device(): pl.pallas_call(block_kernel, out_shape=(*[shape(2, width, span)] * (runs...]
    ppermute x3, starting transfers between devices: 3.88 us -> 5.18 us  [along_x(): lax.ppermute(x, 'row', [(i, (i + 4 * s) % row_devs) for i in range(row_de...]
    ppermute x6, waiting for transfers between devices: 4.53 us -> 3.38 us  [along_y(): lax.ppermute(x, 'col', [(i, i // runs * runs + (i + s) % runs) for i in r...]
    ppermute x1, starting transfers between devices: 2.67 us -> 3.72 us  [per_device(): lax.ppermute(col_out, 'row', [(i, i ^ 2) for i in range(row_devs)])]
    ppermute x1, starting transfers between devices: 1.51 us -> 0.45 us  [per_device(): lax.ppermute(row_out, 'col', [(i, (i + runs) % col_devs) for i in range(c...]
    ppermute x1, waiting for transfers between devices: 3.94 us -> 4.61 us  [per_device(): across = near(lax.ppermute(tile, ('row', 'col'), across_z))]
  transfers between devices with their start and end apart: 22 -> 22, of which waited for: 13 -> 9; matrix products, arithmetic and copies ran while one was open for 0% -> 0% of each run, Pallas kernels for 2% -> 2%
where the time goes in v7:
time: 59.9 us; the launch traced here: 59.4 us
  starting transfers between devices  33.6 us (56%)
  waiting for transfers between devices  17.4 us (29%)
  Pallas kernels  5.14 us (9%)
  local copies, waits for them, and re-layouts  1.89 us (3%)
  between operations  1.38 us (2%)
    ppermute x6, starting transfers between devices, along_y(): lax.ppermute(x, 'col', [(i, i // runs * runs + (i + s) % runs) for i in r...  9.68 us
    ppermute x3, starting transfers between devices, along_x(): lax.ppermute(x, 'row', [(i, (i + 4 * s) % row_devs) for i in range(row_de...  5.18 us
    ppermute x3, starting transfers between devices, per_device(): lax.ppermute(pair, 'col', [(i, i // runs * runs + (i + s) % runs) for i i...  4.62 us
    ppermute x1, waiting for transfers between devices, per_device(): across = near(lax.ppermute(tile, ('row', 'col'), across_z))  4.61 us
    ppermute x3, starting transfers between devices, per_device(): lax.ppermute(line, 'row', [(i, (i + 4 * s) % row_devs) for i in range(row...  4.51 us
    ppermute x1, starting transfers between devices, per_device(): lax.ppermute(vectors, 'row', [(i, i ^ 2) for i in range(row_devs)])  4.04 us
    ppermute x1, starting transfers between devices, per_device(): lax.ppermute(col_out, 'row', [(i, i ^ 2) for i in range(row_devs)])  3.72 us
    ppermute x3, waiting for transfers between devices, per_device(): lax.ppermute(pair, 'col', [(i, i // runs * runs + (i + s) % runs) for i i...  3.57 us
  transfers between devices with their start and end apart: 22, of which 9 were waited for; matrix products, arithmetic and copies ran while one was open for 0% of the time, Pallas kernels for 2%

profile of v7, /device:TPU:0, one launch (start us, length us, event | category | flops | bytes accessed | tf_op | source)
XLA Modules:
  0.0 59.4 jit_solution(10126748996776750289)
XLA Ops:
  0.6 4.0 %collective-permute-start.1 = (bf16[16,2048]{1,0:T(8,128)(2,1)}, bf16[16,2048]{1,0:T(8,128)(2,1)S(1)}, u32[]{:S(2)}, u32[]{:S(2)}) collective-permute-start(bf16[16,2048]{1,0:T(8,128)(2,1)} %x_ref.1), channel_id=1, source_target_pairs={{0,16},{8,24},{16,0},{24,8},{32,48},{40,56},{48,32},{56,40},{64,80... | collective-permute-start | bytes 196616 | tf_op jit(solution)/shard_map/ppermute | solution.py:304
  4.7 1.0 %collective-permute-start = (bf16[16,2048]{1,0:T(8,128)(2,1)}, bf16[16,2048]{1,0:T(8,128)(2,1)S(1)}, u32[]{:S(2)}, u32[]{:S(2)}) collective-permute-start(bf16[16,2048]{1,0:T(8,128)(2,1)} %x_ref.1), channel_id=1, source_target_pairs={{0,4},{1,5},{2,6},{3,7},{4,0},{5,1},{6,2},{7,3},{8,12},{9,13},{10,... | collective-permute-start | bytes 196616 | tf_op jit(solution)/shard_map/ppermute | solution.py:298
  5.7 1.0 %copy-done.1 = bf16[16,128,128]{2,1,0:T(8,128)(2,1)S(1)} copy-done((bf16[16,128,128]{2,1,0:T(8,128)(2,1)S(1)}, bf16[16,128,128]{2,1,0:T(8,128)(2,1)}, u32[]{:S(2)}) %copy-start.1) | copy-done | bytes 524312
  6.7 0.8 %copy-done.2 = bf16[16,2048]{1,0:T(8,128)(2,1)S(1)} copy-done((bf16[16,2048]{1,0:T(8,128)(2,1)S(1)}, bf16[16,2048]{1,0:T(8,128)(2,1)}, u32[]{:S(2)}) %copy-start.2) | copy-done | bytes 65560
  7.6 0.5 shard_map.86
  8.1 1.0 %collective-permute-done.z_ref = bf16[16,2048]{1,0:T(8,128)(2,1)S(1)} collective-permute-done((bf16[16,2048]{1,0:T(8,128)(2,1)}, bf16[16,2048]{1,0:T(8,128)(2,1)S(1)}, u32[]{:S(2)}, u32[]{:S(2)}) %collective-permute-start) | collective-permute-done | bytes 65568 | tf_op jit(solution)/shard_map/ppermute | solution.py:298
  9.2 2.8 %collective-permute-start.7 = (bf16[2,16,2048]{2,1,0:T(8,128)(2,1)S(1)}, bf16[2,16,2048]{2,1,0:T(8,128)(2,1)S(1)}, u32[]{:S(2)}, u32[]{:S(2)}) collective-permute-start(bf16[2,16,2048]{2,1,0:T(8,128)(2,1)S(1)} %get-tuple-element.27.refs_0_), channel_id=1, source_target_pairs={{0,96},{8,104},{16,112},{24,120},{32,0},{40,8},{48,16},{56,24},{64... | collective-permute-start | bytes 393224 | tf_op jit(solution)/shard_map/ppermute | solution.py:328
  12.0 0.8 %collective-permute-start.6 = (bf16[2,16,2048]{2,1,0:T(8,128)(2,1)S(1)}, bf16[2,16,2048]{2,1,0:T(8,128)(2,1)S(1)}, u32[]{:S(2)}, u32[]{:S(2)}) collective-permute-start(bf16[2,16,2048]{2,1,0:T(8,128)(2,1)S(1)} %get-tuple-element.27.refs_0_), channel_id=1, source_target_pairs={{0,64},{8,72},{16,80},{24,88},{32,96},{40,104},{48,112},{56,120},{... | collective-permute-start | bytes 393224 | tf_op jit(solution)/shard_map/ppermute | solution.py:328
  12.8 0.9 %collective-permute-start.5 = (bf16[2,16,2048]{2,1,0:T(8,128)(2,1)S(1)}, bf16[2,16,2048]{2,1,0:T(8,128)(2,1)S(1)}, u32[]{:S(2)}, u32[]{:S(2)}) collective-permute-start(bf16[2,16,2048]{2,1,0:T(8,128)(2,1)S(1)} %get-tuple-element.27.refs_0_), channel_id=1, source_target_pairs={{0,32},{8,40},{16,48},{24,56},{32,64},{40,72},{48,80},{56,88},{64,... | collective-permute-start | bytes 393224 | tf_op jit(solution)/shard_map/ppermute | solution.py:328
  13.7 3.0 %collective-permute-start.4 = (bf16[2,16,2048]{2,1,0:T(8,128)(2,1)S(1)}, bf16[2,16,2048]{2,1,0:T(8,128)(2,1)S(1)}, u32[]{:S(2)}, u32[]{:S(2)}) collective-permute-start(bf16[2,16,2048]{2,1,0:T(8,128)(2,1)S(1)} %get-tuple-element.26), channel_id=1, source_target_pairs={{0,3},{1,0},{2,1},{3,2},{4,7},{5,4},{6,5},{7,6},{8,11},{9,8},{10,9... | collective-permute-start | bytes 393224 | tf_op jit(solution)/shard_map/ppermute | solution.py:340
  16.7 0.6 %collective-permute-start.3 = (bf16[2,16,2048]{2,1,0:T(8,128)(2,1)S(1)}, bf16[2,16,2048]{2,1,0:T(8,128)(2,1)S(1)}, u32[]{:S(2)}, u32[]{:S(2)}) collective-permute-start(bf16[2,16,2048]{2,1,0:T(8,128)(2,1)S(1)} %get-tuple-element.26), channel_id=1, source_target_pairs={{0,2},{1,3},{2,0},{3,1},{4,6},{5,7},{6,4},{7,5},{8,10},{9,11},{10,... | collective-permute-start | bytes 393224 | tf_op jit(solution)/shard_map/ppermute | solution.py:340
  17.3 1.0 %collective-permute-start.2 = (bf16[2,16,2048]{2,1,0:T(8,128)(2,1)S(1)}, bf16[2,16,2048]{2,1,0:T(8,128)(2,1)S(1)}, u32[]{:S(2)}, u32[]{:S(2)}) collective-permute-start(bf16[2,16,2048]{2,1,0:T(8,128)(2,1)S(1)} %get-tuple-element.26), channel_id=1, source_target_pairs={{0,1},{1,2},{2,3},{3,0},{4,5},{5,6},{6,7},{7,4},{8,9},{9,10},{10,1... | collective-permute-start | bytes 393224 | tf_op jit(solution)/shard_map/ppermute | solution.py:340
  18.3 0.6 collective-permute-done.6.refs_2_
  18.9 1.3 %collective-permute-done.5.refs_1_ = bf16[2,16,2048]{2,1,0:T(8,128)(2,1)S(1)} collective-permute-done((bf16[2,16,2048]{2,1,0:T(8,128)(2,1)S(1)}, bf16[2,16,2048]{2,1,0:T(8,128)(2,1)S(1)}, u32[]{:S(2)}, u32[]{:S(2)}) %collective-permute-start.5) | collective-permute-done | bytes 131104 | tf_op jit(solution)/shard_map/ppermute | solution.py:328
  21.0 2.3 %collective-permute-done.3.refs_1_ = bf16[2,16,2048]{2,1,0:T(8,128)(2,1)S(1)} collective-permute-done((bf16[2,16,2048]{2,1,0:T(8,128)(2,1)S(1)}, bf16[2,16,2048]{2,1,0:T(8,128)(2,1)S(1)}, u32[]{:S(2)}, u32[]{:S(2)}) %collective-permute-start.3) | collective-permute-done | bytes 131104 | tf_op jit(solution)/shard_map/ppermute | solution.py:340
  23.3 1.3 %collective-permute-done.2.refs_0_ = bf16[2,16,2048]{2,1,0:T(8,128)(2,1)S(1)} collective-permute-done((bf16[2,16,2048]{2,1,0:T(8,128)(2,1)S(1)}, bf16[2,16,2048]{2,1,0:T(8,128)(2,1)S(1)}, u32[]{:S(2)}, u32[]{:S(2)}) %collective-permute-start.2) | collective-permute-done | bytes 131104 | tf_op jit(solution)/shard_map/ppermute | solution.py:340
  24.7 2.9 %shard_map.90 = (bf16[2,16,2048]{2,1,0:T(8,128)(2,1)S(1)}, bf16[2,16,2048]{2,1,0:T(8,128)(2,1)S(1)}, bf16[2,16,2048]{2,1,0:T(8,128)(2,1)S(1)}, f32[2,16,2048]{2,...) custom-call(s32[1,1]{1,0:T(1,128)S(6)} %copy.9.count_ref, s32[192]{0:T(256)} %bitcast.4, ...), custom_call_target="tpu_custom_call" | custom-call | tf_op jit(solution)/shard_map/pallas_call | solution.py:369
  27.7 2.0 %collective-permute-done.9.got_ref = bf16[9,16,2048]{2,1,0:T(8,128)(2,1)S(1)} collective-permute-done((bf16[9,16,2048]{2,1,0:T(8,128)(2,1)S(1)}, bf16[9,16,2048]{2,1,0:T(8,128)(2,1)S(1)}, u32[]{:S(2)}, u32[]{:S(2)}) %collective-permute-start.9) | collective-permute-done | bytes 589856 | tf_op jit(solution)/shard_map/ppermute | solution.py:386
  29.8 2.4 %collective-permute-start.10 = (bf16[2,16,2176]{2,1,0:T(8,128)(2,1)S(1)}, bf16[2,16,2176]{2,1,0:T(8,128)(2,1)S(1)}, u32[]{:S(2)}, u32[]{:S(2)}) collective-permute-start(bf16[2,16,2176]{2,1,0:T(8,128)(2,1)S(1)} %get-tuple-element.33), channel_id=1, source_target_pairs={{0,32},{8,40},{16,48},{24,56},{32,64},{40,72},{48,80},{56,88},{64,... | collective-permute-start | bytes 417800 | tf_op jit(solution)/shard_map/ppermute | solution.py:358
  32.2 2.0 %collective-permute-start.11 = (bf16[2,16,2176]{2,1,0:T(8,128)(2,1)S(1)}, bf16[2,16,2176]{2,1,0:T(8,128)(2,1)S(1)}, u32[]{:S(2)}, u32[]{:S(2)}) collective-permute-start(bf16[2,16,2176]{2,1,0:T(8,128)(2,1)S(1)} %get-tuple-element.34), channel_id=1, source_target_pairs={{0,64},{8,72},{16,80},{24,88},{32,96},{40,104},{48,112},{56,120},{... | collective-permute-start | bytes 417800 | tf_op jit(solution)/shard_map/ppermute | solution.py:358
  34.2 0.8 %collective-permute-start.12 = (bf16[2,16,2176]{2,1,0:T(8,128)(2,1)S(1)}, bf16[2,16,2176]{2,1,0:T(8,128)(2,1)S(1)}, u32[]{:S(2)}, u32[]{:S(2)}) collective-permute-start(bf16[2,16,2176]{2,1,0:T(8,128)(2,1)S(1)} %get-tuple-element.35), channel_id=1, source_target_pairs={{0,96},{8,104},{16,112},{24,120},{32,0},{40,8},{48,16},{56,24},{64... | collective-permute-start | bytes 417800 | tf_op jit(solution)/shard_map/ppermute | solution.py:358
  35.0 0.8 %collective-permute-start.13 = (bf16[2,16,2048]{2,1,0:T(8,128)(2,1)S(1)}, bf16[2,16,2048]{2,1,0:T(8,128)(2,1)S(1)}, u32[]{:S(2)}, u32[]{:S(2)}) collective-permute-start(bf16[2,16,2048]{2,1,0:T(8,128)(2,1)S(1)} %get-tuple-element.36), channel_id=1, source_target_pairs={{0,1},{1,2},{2,3},{3,0},{4,5},{5,6},{6,7},{7,4},{8,9},{9,10},{10,1... | collective-permute-start | bytes 393224 | tf_op jit(solution)/shard_map/ppermute | solution.py:355
  35.8 2.9 %collective-permute-start.14 = (bf16[2,16,2048]{2,1,0:T(8,128)(2,1)S(1)}, bf16[2,16,2048]{2,1,0:T(8,128)(2,1)S(1)}, u32[]{:S(2)}, u32[]{:S(2)}) collective-permute-start(bf16[2,16,2048]{2,1,0:T(8,128)(2,1)S(1)} %get-tuple-element.37), channel_id=1, source_target_pairs={{0,2},{1,3},{2,0},{3,1},{4,6},{5,7},{6,4},{7,5},{8,10},{9,11},{10,... | collective-permute-start | bytes 393224 | tf_op jit(solution)/shard_map/ppermute | solution.py:355
  38.7 1.4 %collective-permute-start.15 = (bf16[2,16,2048]{2,1,0:T(8,128)(2,1)S(1)}, bf16[2,16,2048]{2,1,0:T(8,128)(2,1)S(1)}, u32[]{:S(2)}, u32[]{:S(2)}) collective-permute-start(bf16[2,16,2048]{2,1,0:T(8,128)(2,1)S(1)} %get-tuple-element.38), channel_id=1, source_target_pairs={{0,3},{1,0},{2,1},{3,2},{4,7},{5,4},{6,5},{7,6},{8,11},{9,8},{10,9... | collective-permute-start | bytes 393224 | tf_op jit(solution)/shard_map/ppermute | solution.py:355
  40.1 0.8 %collective-permute-done.11.refs_1_ = bf16[2,16,2176]{2,1,0:T(8,128)(2,1)S(1)} collective-permute-done((bf16[2,16,2176]{2,1,0:T(8,128)(2,1)S(1)}, bf16[2,16,2176]{2,1,0:T(8,128)(2,1)S(1)}, u32[]{:S(2)}, u32[]{:S(2)}) %collective-permute-start.11) | collective-permute-done | bytes 139296 | tf_op jit(solution)/shard_map/ppermute | solution.py:358
  41.0 3.0 %collective-permute-start.18 = (bf16[16,128]{1,0:T(8,128)(2,1)S(1)}, bf16[16,128]{1,0:T(8,128)(2,1)S(1)}, u32[]{:S(2)}, u32[]{:S(2)}) collective-permute-start(bf16[16,128]{1,0:T(8,128)(2,1)S(1)} %shard_map.93.refs_0_), channel_id=1, source_target_pairs={{0,3},{1,0},{2,1},{3,2},{4,7},{5,4},{6,5},{7,6},{8,11},{9,8},{10,9... | collective-permute-start | bytes 12296 | tf_op jit(solution)/shard_map/ppermute | solution.py:355
  44.3 1.3 %collective-permute-start.16 = (bf16[16,128]{1,0:T(8,128)(2,1)S(1)}, bf16[16,128]{1,0:T(8,128)(2,1)S(1)}, u32[]{:S(2)}, u32[]{:S(2)}) collective-permute-start(bf16[16,128]{1,0:T(8,128)(2,1)S(1)} %shard_map.93.refs_0_), channel_id=1, source_target_pairs={{0,1},{1,2},{2,3},{3,0},{4,5},{5,6},{6,7},{7,4},{8,9},{9,10},{10,1... | collective-permute-start | bytes 12296 | tf_op jit(solution)/shard_map/ppermute | solution.py:355
  45.8 3.4 %collective-permute-done.17.refs_2_ = bf16[16,128]{1,0:T(8,128)(2,1)S(1)} collective-permute-done((bf16[16,128]{1,0:T(8,128)(2,1)S(1)}, bf16[16,128]{1,0:T(8,128)(2,1)S(1)}, u32[]{:S(2)}, u32[]{:S(2)}) %collective-permute-start.17) | collective-permute-done | bytes 4128 | tf_op jit(solution)/shard_map/ppermute | solution.py:355
  49.3 3.7 %collective-permute-start.19 = (bf16[16,2176]{1,0:T(8,128)(2,1)S(1)}, bf16[16,2176]{1,0:T(8,128)(2,1)S(1)}, u32[]{:S(2)}, u32[]{:S(2)}) collective-permute-start(bf16[16,2176]{1,0:T(8,128)(2,1)S(1)} %get-tuple-element.43), channel_id=1, source_target_pairs={{0,16},{8,24},{16,0},{24,8},{32,48},{40,56},{48,32},{56,40},{64,80... | collective-permute-start | bytes 208904 | tf_op jit(solution)/shard_map/ppermute | solution.py:406
  53.0 0.5 collective-permute-start.20
  53.6 4.6 %collective-permute-done.21.across_ref = bf16[16,128]{1,0:T(8,128)(2,1)S(1)} collective-permute-done((bf16[16,128]{1,0:T(8,128)(2,1)S(1)}, bf16[16,128]{1,0:T(8,128)(2,1)S(1)}, u32[]{:S(2)}, u32[]{:S(2)}) %collective-permute-start.21) | collective-permute-done | bytes 4128 | tf_op jit(solution)/shard_map/ppermute | solution.py:408
  58.3 1.1 %shard_map.95 = (f32[16,2048]{1,0:T(8,128)}, bf16[16,2048]{1,0:T(8,128)(2,1)}) custom-call(f32[16,2048]{1,0:T(8,128)S(1)} %get-tuple-element.39.own_ref, bf16[16,2176]{1,0:T(8,128)(2,1)S(1)} %collective-permute-done.19.col_ref, bf16[16,2176]{1,0:T(8,128)(2,1)S(1)} %collective-permute-done.20.row_ref, bf16[16,128]{1,0:T(8,128)(2,1)S(1)} %get-tuple-element.45.tile_ref, ...), custom_call_target="tpu_custom_call" | custom-call | tf_op jit(solution)/shard_map/pallas_call | solution.py:409
  (28 shorter events, 1.3 us)
Async XLA Ops:
  0.6 7.5 %collective-permute-start.1 = (bf16[16,2048]{1,0:T(8,128)(2,1)}, bf16[16,2048]{1,0:T(8,128)(2,1)S(1)}, u32[]{:S(2)}, u32[]{:S(2)}) collective-permute-start(bf16[16,2048]{1,0:T(8,128)(2,1)} %x_ref.1), channel_id=1, source_target_pairs={{0,16},{8,24},{16,0},{24,8},{32,48},{40,56},{48,32},{56,40},{64,80... | collective-permute-start | bytes 196616 | tf_op jit(solution)/shard_map/ppermute | solution.py:304
  4.7 4.5 %collective-permute-start = (bf16[16,2048]{1,0:T(8,128)(2,1)}, bf16[16,2048]{1,0:T(8,128)(2,1)S(1)}, u32[]{:S(2)}, u32[]{:S(2)}) collective-permute-start(bf16[16,2048]{1,0:T(8,128)(2,1)} %x_ref.1), channel_id=1, source_target_pairs={{0,4},{1,5},{2,6},{3,7},{4,0},{5,1},{6,2},{7,3},{8,12},{9,13},{10,... | collective-permute-start | bytes 196616 | tf_op jit(solution)/shard_map/ppermute | solution.py:298
  5.7 1.0 %copy-start.1 = (bf16[16,128,128]{2,1,0:T(8,128)(2,1)S(1)}, bf16[16,128,128]{2,1,0:T(8,128)(2,1)}, u32[]{:S(2)}) copy-start(bf16[16,128,128]{2,1,0:T(8,128)(2,1)} %diag_ref.1) | copy-start | bytes 1572868
  6.7 0.8 %copy-start.2 = (bf16[16,2048]{1,0:T(8,128)(2,1)S(1)}, bf16[16,2048]{1,0:T(8,128)(2,1)}, u32[]{:S(2)}) copy-start(bf16[16,2048]{1,0:T(8,128)(2,1)} %x_ref.1) | copy-start | bytes 196612
  9.2 8.2 %collective-permute-start.7 = (bf16[2,16,2048]{2,1,0:T(8,128)(2,1)S(1)}, bf16[2,16,2048]{2,1,0:T(8,128)(2,1)S(1)}, u32[]{:S(2)}, u32[]{:S(2)}) collective-permute-start(bf16[2,16,2048]{2,1,0:T(8,128)(2,1)S(1)} %get-tuple-element.27.refs_0_), channel_id=1, source_target_pairs={{0,96},{8,104},{16,112},{24,120},{32,0},{40,8},{48,16},{56,24},{64... | collective-permute-start | bytes 393224 | tf_op jit(solution)/shard_map/ppermute | solution.py:328
  12.0 6.9 %collective-permute-start.6 = (bf16[2,16,2048]{2,1,0:T(8,128)(2,1)S(1)}, bf16[2,16,2048]{2,1,0:T(8,128)(2,1)S(1)}, u32[]{:S(2)}, u32[]{:S(2)}) collective-permute-start(bf16[2,16,2048]{2,1,0:T(8,128)(2,1)S(1)} %get-tuple-element.27.refs_0_), channel_id=1, source_target_pairs={{0,64},{8,72},{16,80},{24,88},{32,96},{40,104},{48,112},{56,120},{... | collective-permute-start | bytes 393224 | tf_op jit(solution)/shard_map/ppermute | solution.py:328
  12.8 7.4 %collective-permute-start.5 = (bf16[2,16,2048]{2,1,0:T(8,128)(2,1)S(1)}, bf16[2,16,2048]{2,1,0:T(8,128)(2,1)S(1)}, u32[]{:S(2)}, u32[]{:S(2)}) collective-permute-start(bf16[2,16,2048]{2,1,0:T(8,128)(2,1)S(1)} %get-tuple-element.27.refs_0_), channel_id=1, source_target_pairs={{0,32},{8,40},{16,48},{24,56},{32,64},{40,72},{48,80},{56,88},{64,... | collective-permute-start | bytes 393224 | tf_op jit(solution)/shard_map/ppermute | solution.py:328
  13.7 7.3 %collective-permute-start.4 = (bf16[2,16,2048]{2,1,0:T(8,128)(2,1)S(1)}, bf16[2,16,2048]{2,1,0:T(8,128)(2,1)S(1)}, u32[]{:S(2)}, u32[]{:S(2)}) collective-permute-start(bf16[2,16,2048]{2,1,0:T(8,128)(2,1)S(1)} %get-tuple-element.26), channel_id=1, source_target_pairs={{0,3},{1,0},{2,1},{3,2},{4,7},{5,4},{6,5},{7,6},{8,11},{9,8},{10,9... | collective-permute-start | bytes 393224 | tf_op jit(solution)/shard_map/ppermute | solution.py:340
  16.7 6.6 %collective-permute-start.3 = (bf16[2,16,2048]{2,1,0:T(8,128)(2,1)S(1)}, bf16[2,16,2048]{2,1,0:T(8,128)(2,1)S(1)}, u32[]{:S(2)}, u32[]{:S(2)}) collective-permute-start(bf16[2,16,2048]{2,1,0:T(8,128)(2,1)S(1)} %get-tuple-element.26), channel_id=1, source_target_pairs={{0,2},{1,3},{2,0},{3,1},{4,6},{5,7},{6,4},{7,5},{8,10},{9,11},{10,... | collective-permute-start | bytes 393224 | tf_op jit(solution)/shard_map/ppermute | solution.py:340
  17.3 7.2 %collective-permute-start.2 = (bf16[2,16,2048]{2,1,0:T(8,128)(2,1)S(1)}, bf16[2,16,2048]{2,1,0:T(8,128)(2,1)S(1)}, u32[]{:S(2)}, u32[]{:S(2)}) collective-permute-start(bf16[2,16,2048]{2,1,0:T(8,128)(2,1)S(1)} %get-tuple-element.26), channel_id=1, source_target_pairs={{0,1},{1,2},{2,3},{3,0},{4,5},{5,6},{6,7},{7,4},{8,9},{9,10},{10,1... | collective-permute-start | bytes 393224 | tf_op jit(solution)/shard_map/ppermute | solution.py:340
  20.3 4.4 %collective-permute-start.8 = (bf16[4,2,16,2048]{3,2,1,0:T(8,128)(2,1)S(1)}, bf16[4,2,16,2048]{3,2,1,0:T(8,128)(2,1)S(1)}, u32[]{:S(2)}, u32[]{:S(2)}) collective-permute-start(bf16[4,2,16,2048]{3,2,1,0:T(8,128)(2,1)S(1)} %shard_map.88.refs_3_.xcol_ref), channel_id=1, source_target_pairs={{0,8},{8,0},{16,24},{24,16},{32,40},{40,32},{48,56},{56,48},{64,72... | collective-permute-start | bytes 1572872 | tf_op jit(solution)/shard_map/ppermute | solution.py:338
  24.7 33.6 %copy-start = (bf16[16,128,128]{2,1,0:T(8,128)(2,1)S(1)}, bf16[16,128,128]{2,1,0:T(8,128)(2,1)}, u32[]{:S(2)}) copy-start(bf16[16,128,128]{2,1,0:T(8,128)(2,1)} %pre_ref.1) | copy-start | bytes 1572868
  27.6 2.1 %collective-permute-start.9 = (bf16[9,16,2048]{2,1,0:T(8,128)(2,1)S(1)}, bf16[9,16,2048]{2,1,0:T(8,128)(2,1)S(1)}, u32[]{:S(2)}, u32[]{:S(2)}) collective-permute-start(bf16[9,16,2048]{2,1,0:T(8,128)(2,1)S(1)} %get-tuple-element.29.own_ref), channel_id=1, source_target_pairs={{0,8},{8,0},{16,24},{24,16},{32,40},{40,32},{48,56},{56,48},{64,72... | collective-permute-start | bytes 1769480 | tf_op jit(solution)/shard_map/ppermute | solution.py:386
  29.8 8.9 %collective-permute-start.10 = (bf16[2,16,2176]{2,1,0:T(8,128)(2,1)S(1)}, bf16[2,16,2176]{2,1,0:T(8,128)(2,1)S(1)}, u32[]{:S(2)}, u32[]{:S(2)}) collective-permute-start(bf16[2,16,2176]{2,1,0:T(8,128)(2,1)S(1)} %get-tuple-element.33), channel_id=1, source_target_pairs={{0,32},{8,40},{16,48},{24,56},{32,64},{40,72},{48,80},{56,88},{64,... | collective-permute-start | bytes 417800 | tf_op jit(solution)/shard_map/ppermute | solution.py:358
  32.2 8.7 %collective-permute-start.11 = (bf16[2,16,2176]{2,1,0:T(8,128)(2,1)S(1)}, bf16[2,16,2176]{2,1,0:T(8,128)(2,1)S(1)}, u32[]{:S(2)}, u32[]{:S(2)}) collective-permute-start(bf16[2,16,2176]{2,1,0:T(8,128)(2,1)S(1)} %get-tuple-element.34), channel_id=1, source_target_pairs={{0,64},{8,72},{16,80},{24,88},{32,96},{40,104},{48,112},{56,120},{... | collective-permute-start | bytes 417800 | tf_op jit(solution)/shard_map/ppermute | solution.py:358
  34.2 6.7 %collective-permute-start.12 = (bf16[2,16,2176]{2,1,0:T(8,128)(2,1)S(1)}, bf16[2,16,2176]{2,1,0:T(8,128)(2,1)S(1)}, u32[]{:S(2)}, u32[]{:S(2)}) collective-permute-start(bf16[2,16,2176]{2,1,0:T(8,128)(2,1)S(1)} %get-tuple-element.35), channel_id=1, source_target_pairs={{0,96},{8,104},{16,112},{24,120},{32,0},{40,8},{48,16},{56,24},{64... | collective-permute-start | bytes 417800 | tf_op jit(solution)/shard_map/ppermute | solution.py:358
  35.0 9.3 %collective-permute-start.13 = (bf16[2,16,2048]{2,1,0:T(8,128)(2,1)S(1)}, bf16[2,16,2048]{2,1,0:T(8,128)(2,1)S(1)}, u32[]{:S(2)}, u32[]{:S(2)}) collective-permute-start(bf16[2,16,2048]{2,1,0:T(8,128)(2,1)S(1)} %get-tuple-element.36), channel_id=1, source_target_pairs={{0,1},{1,2},{2,3},{3,0},{4,5},{5,6},{6,7},{7,4},{8,9},{9,10},{10,1... | collective-permute-start | bytes 393224 | tf_op jit(solution)/shard_map/ppermute | solution.py:355
  35.8 9.9 %collective-permute-start.14 = (bf16[2,16,2048]{2,1,0:T(8,128)(2,1)S(1)}, bf16[2,16,2048]{2,1,0:T(8,128)(2,1)S(1)}, u32[]{:S(2)}, u32[]{:S(2)}) collective-permute-start(bf16[2,16,2048]{2,1,0:T(8,128)(2,1)S(1)} %get-tuple-element.37), channel_id=1, source_target_pairs={{0,2},{1,3},{2,0},{3,1},{4,6},{5,7},{6,4},{7,5},{8,10},{9,11},{10,... | collective-permute-start | bytes 393224 | tf_op jit(solution)/shard_map/ppermute | solution.py:355
  38.7 6.9 %collective-permute-start.15 = (bf16[2,16,2048]{2,1,0:T(8,128)(2,1)S(1)}, bf16[2,16,2048]{2,1,0:T(8,128)(2,1)S(1)}, u32[]{:S(2)}, u32[]{:S(2)}) collective-permute-start(bf16[2,16,2048]{2,1,0:T(8,128)(2,1)S(1)} %get-tuple-element.38), channel_id=1, source_target_pairs={{0,3},{1,0},{2,1},{3,2},{4,7},{5,4},{6,5},{7,6},{8,11},{9,8},{10,9... | collective-permute-start | bytes 393224 | tf_op jit(solution)/shard_map/ppermute | solution.py:355
  41.0 4.8 %collective-permute-start.18 = (bf16[16,128]{1,0:T(8,128)(2,1)S(1)}, bf16[16,128]{1,0:T(8,128)(2,1)S(1)}, u32[]{:S(2)}, u32[]{:S(2)}) collective-permute-start(bf16[16,128]{1,0:T(8,128)(2,1)S(1)} %shard_map.93.refs_0_), channel_id=1, source_target_pairs={{0,3},{1,0},{2,1},{3,2},{4,7},{5,4},{6,5},{7,6},{8,11},{9,8},{10,9... | collective-permute-start | bytes 12296 | tf_op jit(solution)/shard_map/ppermute | solution.py:355
  44.0 5.1 %collective-permute-start.17 = (bf16[16,128]{1,0:T(8,128)(2,1)S(1)}, bf16[16,128]{1,0:T(8,128)(2,1)S(1)}, u32[]{:S(2)}, u32[]{:S(2)}) collective-permute-start(bf16[16,128]{1,0:T(8,128)(2,1)S(1)} %shard_map.93.refs_0_), channel_id=1, source_target_pairs={{0,2},{1,3},{2,0},{3,1},{4,6},{5,7},{6,4},{7,5},{8,10},{9,11},{10,... | collective-permute-start | bytes 12296 | tf_op jit(solution)/shard_map/ppermute | solution.py:355
  44.3 4.9 %collective-permute-start.16 = (bf16[16,128]{1,0:T(8,128)(2,1)S(1)}, bf16[16,128]{1,0:T(8,128)(2,1)S(1)}, u32[]{:S(2)}, u32[]{:S(2)}) collective-permute-start(bf16[16,128]{1,0:T(8,128)(2,1)S(1)} %shard_map.93.refs_0_), channel_id=1, source_target_pairs={{0,1},{1,2},{2,3},{3,0},{4,5},{5,6},{6,7},{7,4},{8,9},{9,10},{10,1... | collective-permute-start | bytes 12296 | tf_op jit(solution)/shard_map/ppermute | solution.py:355
  49.3 9.0 %collective-permute-start.19 = (bf16[16,2176]{1,0:T(8,128)(2,1)S(1)}, bf16[16,2176]{1,0:T(8,128)(2,1)S(1)}, u32[]{:S(2)}, u32[]{:S(2)}) collective-permute-start(bf16[16,2176]{1,0:T(8,128)(2,1)S(1)} %get-tuple-element.43), channel_id=1, source_target_pairs={{0,16},{8,24},{16,0},{24,8},{32,48},{40,56},{48,32},{56,40},{64,80... | collective-permute-start | bytes 208904 | tf_op jit(solution)/shard_map/ppermute | solution.py:406
  53.0 5.3 %collective-permute-start.20 = (bf16[16,2176]{1,0:T(8,128)(2,1)S(1)}, bf16[16,2176]{1,0:T(8,128)(2,1)S(1)}, u32[]{:S(2)}, u32[]{:S(2)}) collective-permute-start(bf16[16,2176]{1,0:T(8,128)(2,1)S(1)} %get-tuple-element.44), channel_id=1, source_target_pairs={{0,4},{1,5},{2,6},{3,7},{4,0},{5,1},{6,2},{7,3},{8,12},{9,13},{10,... | collective-permute-start | bytes 208904 | tf_op jit(solution)/shard_map/ppermute | solution.py:407
  53.4 4.8 %collective-permute-start.21 = (bf16[16,128]{1,0:T(8,128)(2,1)S(1)}, bf16[16,128]{1,0:T(8,128)(2,1)S(1)}, u32[]{:S(2)}, u32[]{:S(2)}) collective-permute-start(bf16[16,128]{1,0:T(8,128)(2,1)S(1)} %get-tuple-element.45.tile_ref), channel_id=1, source_target_pairs={{0,20},{1,21},{2,22},{3,23},{4,16},{5,17},{6,18},{7,19},{8,28},{9,... | collective-permute-start | bytes 12296 | tf_op jit(solution)/shard_map/ppermute | solution.py:408
